TPU v7x, 256 devices: a whole 4x4x8 slice. The times are simulated.
256 devices in a mesh: lat: 4 (over y_lo, core), lon: 16 (over y_hi, z), ch: 4 (over x).
Axes of the slice: x: 4, y: 4 (y_hi: 2, y_lo: 2; y = y_hi * 2 + y_lo), z: 8, core: 2. Of those that a mesh axis runs over, the one named last changes fastest.
Arguments:
- grid_field: bfloat16 [1440, 4, 49152], P('lon', 'ch', 'lat'), may hold values from -6 to 6
- first_weight: bfloat16 [4, 2, 96, 96], P('ch'), may hold values from -0.4375 to 0.4375
- first_bias: float32 [4, 2, 96], P('ch'), may hold values from -3 to 3
- second_weight: bfloat16 [4, 2, 96, 96], P('ch'), may hold values from -0.4375 to 0.4375
- second_bias: float32 [4, 2, 96], P('ch'), may hold values from -3 to 3
Outputs:
- mixed: bfloat16 [1440, 4, 49152], P('lon', 'ch', 'lat')
All inputs are finite; a program needn't handle non-finite values.
Results may differ from a plain program's by a relative error of at most 0.0073.
Values may be sent and summed in bfloat16 or wider, within the bound.
No kernel may reach another device: no remote copies, remote signals or barrier semaphores. Data moves between devices by JAX's collectives and lax.ppermute only.
A program may use at most 128 MiB of HBM per device.

v0:
```python
import math

import jax
import jax.numpy as jnp
from jax import lax
from jax.sharding import PartitionSpec as P

shrink_level = 0.01


def phase_tables(length):
    indices = jnp.arange(length, dtype=jnp.int32)
    product = indices[:, None] * indices[None, :] % length
    angles = product.astype(jnp.float32) * (2.0 * math.pi / length)
    return (jnp.cos(angles), jnp.sin(angles))


def lon_tables(length):
    cosine_tab, sine_tab = phase_tables(length)
    kept_modes = length // 2
    factor = 1.0 / math.sqrt(length)
    forward = jnp.concatenate([cosine_tab[:kept_modes], -sine_tab[:kept_modes]], axis=0) * factor
    weights = jnp.where(jnp.arange(kept_modes) == 0, 1.0, 2.0).astype(jnp.float32)
    inverse = (
        jnp.concatenate(
            [cosine_tab[:, :kept_modes] * weights, -sine_tab[:, :kept_modes] * weights], axis=1
        )
        * factor
    )
    return (forward.astype(jnp.bfloat16), inverse.astype(jnp.bfloat16))


def lat_tables(length):
    cosine_tab, sine_tab = phase_tables(length)
    factor = 1.0 / math.sqrt(length)
    forward = (
        jnp.stack(
            [jnp.stack([cosine_tab, sine_tab], axis=1), jnp.stack([-sine_tab, cosine_tab], axis=1)],
            axis=0,
        )
        * factor
    )
    inverse = (
        jnp.stack(
            [jnp.stack([cosine_tab, -sine_tab], axis=1), jnp.stack([sine_tab, cosine_tab], axis=1)],
            axis=0,
        )
        * factor
    )
    return (forward.astype(jnp.bfloat16), inverse.astype(jnp.bfloat16))


def complex_blocks(weight):
    real_part, imag_part = (weight[:, 0], weight[:, 1])
    return jnp.stack(
        [jnp.stack([real_part, imag_part], axis=2), jnp.stack([-imag_part, real_part], axis=2)],
        axis=1,
    )


def block_mixing(mode_data, first_weight, first_bias, second_weight, second_bias):
    shape = mode_data.shape
    blocks_here = first_weight.shape[0]
    block_width = first_weight.shape[2]
    split_data = mode_data.reshape(shape[0], shape[1], shape[2], blocks_here, block_width)
    hidden = jnp.einsum(
        "rkqbc,brcsd->skqbd",
        split_data,
        complex_blocks(first_weight),
        preferred_element_type=jnp.float32,
    )
    hidden = jax.nn.relu(hidden + jnp.moveaxis(first_bias, 1, 0)[:, None, None, :, :]).astype(
        jnp.bfloat16
    )
    output = jnp.einsum(
        "rkqbc,brcsd->skqbd",
        hidden,
        complex_blocks(second_weight),
        preferred_element_type=jnp.float32,
    )
    output = output + jnp.moveaxis(second_bias, 1, 0)[:, None, None, :, :]
    shrunk = jnp.sign(output) * jnp.maximum(jnp.abs(output) - shrink_level, 0.0)
    return shrunk.astype(jnp.bfloat16).reshape(shape)


def lat_apply(data, table):
    columns = lax.all_to_all(data, "lat", split_axis=3, concat_axis=2, tiled=True)
    result = jnp.einsum(
        "sqrh,rkhc->skqc", table, columns, preferred_element_type=jnp.float32
    ).astype(jnp.bfloat16)
    return lax.all_to_all(result, "lat", split_axis=2, concat_axis=3, tiled=True)


def per_device(grid_field, first_weight, first_bias, second_weight, second_bias):
    lon_devices = lax.axis_size("lon")
    lat_devices = lax.axis_size("lat")
    block_width = first_weight.shape[2]
    local_lon, blocks_here, merged = grid_field.shape
    local_lat = merged // block_width
    local_chan = blocks_here * block_width
    lon_size = local_lon * lon_devices
    lat_size = local_lat * lat_devices
    kept_modes = lon_size // 2
    lon_forward, lon_inverse = lon_tables(lon_size)
    lat_forward, lat_inverse = lat_tables(lat_size)
    reordered = grid_field.reshape(local_lon, blocks_here, local_lat, block_width).transpose(
        0, 2, 1, 3
    )
    flattened = reordered.reshape(local_lon, local_lat * local_chan)
    gathered = lax.all_to_all(flattened, "lon", split_axis=1, concat_axis=0, tiled=True)
    spectra = jnp.dot(lon_forward, gathered, preferred_element_type=jnp.float32).astype(
        jnp.bfloat16
    )
    spectra = spectra.reshape(2, kept_modes, gathered.shape[1])
    spectra = lax.all_to_all(spectra, "lon", split_axis=1, concat_axis=2, tiled=True)
    spectra = spectra.reshape(2, spectra.shape[1], local_lat, local_chan)
    mode_data = lat_apply(spectra, lat_forward)
    shrunk = block_mixing(mode_data, first_weight, first_bias, second_weight, second_bias)
    returned = lat_apply(shrunk, lat_inverse)
    returned = returned.reshape(2, returned.shape[1], local_lat * local_chan)
    returned = lax.all_to_all(returned, "lon", split_axis=2, concat_axis=1, tiled=True)
    columns = returned.reshape(2 * kept_modes, returned.shape[2])
    grid_out = jnp.dot(lon_inverse, columns, preferred_element_type=jnp.float32) + gathered.astype(
        jnp.float32
    )
    grid_out = lax.all_to_all(
        grid_out.astype(jnp.bfloat16), "lon", split_axis=0, concat_axis=1, tiled=True
    )
    grid_out = grid_out.reshape(local_lon, local_lat, blocks_here, block_width).transpose(
        0, 2, 1, 3
    )
    return grid_out.reshape(grid_field.shape)


def solution(mesh):
    in_specs = (
        P("lon", "ch", "lat"),
        P("ch", None, None, None),
        P("ch", None, None),
        P("ch", None, None, None),
        P("ch", None, None),
    )
    out_specs = P("lon", "ch", "lat")
    return jax.shard_map(
        per_device, mesh=mesh, in_specs=in_specs, out_specs=out_specs, check_vma=False
    )
```

profile of v0, /device:TPU:38, one launch (start us, length us, event | category | flops | bytes accessed | tf_op | source)
XLA Modules:
  0.0 631.3 jit_solution(6902518026747214721)
XLA Ops:
  4.5 11.2 %all-to-all-start = ((bf16[90,16,768]{2,0,1:T(8,128)(2,1)}), bf16[90,16,768]{2,0,1:T(8,128)(2,1)S(1)}, u32[]{:S(2)}, u32[]{:S(2)}) async-start(bf16[90,16,768]{2,0,1:T(8,128)(2,1)} %copy.81), calls=%async_computation | async-start | bytes 4718592 | tf_op jit(solution)/shard_map/all_to_all | solution.py:110
  15.7 36.9 %fusion.6 = (f32[1440,1440]{1,0:T(8,128)S(1)}, f32[1440,1440]{1,0:T(8,128)S(1)}) fusion(), kind=kLoop, calls=%fused_computation.10 | loop fusion | flops 18662400 | bytes 16588800 | tf_op jit(solution)/shard_map/sin | solution.py:15
  62.4 8.7 %all-to-all-done = bf16[90,16,768]{2,0,1:T(8,128)(2,1)S(1)} async-done(((bf16[90,16,768]{2,0,1:T(8,128)(2,1)}), bf16[90,16,768]{2,0,1:T(8,128)(2,1)S(1)}, u32[]{:S(2)}, u32[]{:S(2)}) %all-to-all-start) | async-done | bytes 2211872 | tf_op jit(solution)/shard_map/all_to_all | solution.py:110
  73.2 7.8 %fusion.20 = bf16[1440,768]{1,0:T(8,128)(2,1)S(1)} fusion(bf16[1440,768]{1,0:T(8,128)(2,1)} %all_to_all.99, f32[720,1440]{1,0:T(8,128)} %slice_negate_fusion, f32[720,1440]{1,0:T(8,128)} %slice.34), kind=kOutput, calls=%fused_computation.33 | convolution fusion | flops 3192376320 | bytes 12718080 | tf_op jit(solution)/shard_map/dot_general | solution.py:111
  82.8 61.5 %all_to_all.131 = bf16[2,720,768]{2,0,1:T(2,128)(2,1)S(1)} all-to-all(bf16[2,720,768]{2,0,1:T(2,128)(2,1)S(1)} %copy.82), channel_id=1, replica_groups=mesh['lat'=4,'lon'=16,'ch'=4] {'lon'}, dimensions={1} | all-to-all | bytes 4423680 | tf_op jit(solution)/shard_map/all_to_all | solution.py:115
  146.0 5.0 reshape.158
  151.0 4.4 copy.84
  163.0 4.1 fusion.62
  167.1 4.0 fusion.38
  171.1 14.9 %all-to-all-done.2 = bf16[2,45,128,96]{2,0,1,3:T(2,128)(2,1)S(1)} async-done(((bf16[2,45,128,96]{2,0,1,3:T(2,128)(2,1)}), bf16[2,45,128,96]{2,0,1,3:T(2,128)(2,1)S(1)}, u32[]{:S(2)}, u32[]{:S(2)}) %all-to-all-start.2) | async-done | bytes 2211872 | tf_op jit(solution)/shard_map/all_to_all | solution.py:87
  190.1 5.4 fusion.26
  195.5 8.2 %copy.87 = bf16[2,45,512,24]{1,3,0,2:T(8,128)(2,1)} copy(bf16[2,45,512,24]{2,3,0,1:T(8,128)(2,1)S(1)} %fusion.26) | data formatting | bytes 4423680 | tf_op jit(solution)/shard_map/convert_element_type | solution.py:90
  203.7 13.5 %reshape.178 = bf16[4,2,138240]{2,1,0:T(2,128)(2,1)} reshape(bf16[512,2,24,45]{3,2,1,0:T(8,128)(2,1)} %bitcast.156) | data formatting | bytes 4423680
  217.2 4.0 all-to-all-start.3
  221.8 26.3 %all-to-all-done.3 = bf16[4,2,138240]{2,1,0:T(2,128)(2,1)S(1)} async-done(((bf16[4,2,138240]{2,1,0:T(2,128)(2,1)}), bf16[4,2,138240]{2,1,0:T(2,128)(2,1)S(1)}, u32[]{:S(2)}, u32[]{:S(2)}) %all-to-all-start.3) | async-done | bytes 2211872 | tf_op jit(solution)/shard_map/all_to_all | solution.py:91
  248.1 19.2 %reshape.179 = bf16[512,2,24,45]{3,2,1,0:T(8,128)(2,1)} reshape(bf16[4,2,138240]{2,1,0:T(2,128)(2,1)S(1)} %all-to-all-done.3) | data formatting | bytes 4423680
  267.3 7.8 %copy.88 = bf16[2,45,4,128,24]{3,4,2,0,1:T(8,128)(2,1)S(1)} copy(bf16[2,45,4,128,24]{1,4,0,3,2:T(8,128)(2,1)} %bitcast.157) | data formatting | bytes 4423680 | tf_op jit(solution)/shard_map/all_to_all | solution.py:91
  279.9 29.8 %all_to_all.132 = bf16[2,45,128,96]{2,0,1,3:T(2,128)(2,1)S(1)} all-to-all(bf16[2,45,128,96]{2,0,1,3:T(2,128)(2,1)S(1)} %copy.90), channel_id=1, replica_groups=mesh['lat'=4,'lon'=16,'ch'=4] {'lat'}, dimensions={3} | all-to-all | bytes 4423680 | tf_op jit(solution)/shard_map/all_to_all | solution.py:87
  313.2 5.4 fusion.28
  318.6 8.2 %copy.92 = bf16[2,45,512,24]{1,3,0,2:T(8,128)(2,1)} copy(bf16[2,45,512,24]{2,3,0,1:T(8,128)(2,1)S(1)} %fusion.28) | data formatting | bytes 4423680 | tf_op jit(solution)/shard_map/convert_element_type | solution.py:90
  326.8 12.6 %reshape.180 = bf16[4,2,138240]{2,1,0:T(2,128)(2,1)S(1)} reshape(bf16[512,2,24,45]{3,2,1,0:T(8,128)(2,1)} %bitcast.158) | data formatting | bytes 4423680
  339.5 30.3 %all_to_all.133 = bf16[4,2,138240]{2,1,0:T(2,128)(2,1)} all-to-all(bf16[4,2,138240]{2,1,0:T(2,128)(2,1)S(1)} %reshape.180), channel_id=1, replica_groups=mesh['lat'=4,'lon'=16,'ch'=4] {'lat'}, dimensions={0} | all-to-all | bytes 4423680 | tf_op jit(solution)/shard_map/all_to_all | solution.py:91
  369.8 20.1 %reshape.181 = bf16[512,2,24,45]{3,2,1,0:T(8,128)(2,1)} reshape(bf16[4,2,138240]{2,1,0:T(2,128)(2,1)} %all_to_all.133) | data formatting | bytes 4423680
  393.8 52.8 %copy.122 = bf16[2,45,12288]{1,0,2:T(2,128)(2,1)} copy(bf16[2,45,12288]{1,2,0:T(8,128)(2,1)S(1)} %bitcast.154) | data formatting | bytes 4423680 | tf_op jit(solution)/shard_map/reshape | solution.py:120
  446.5 12.6 %reshape.182 = bf16[16,2,34560]{2,1,0:T(2,128)(2,1)} reshape(bf16[12288,2,45]{2,1,0:T(2,128)(2,1)} %bitcast.155) | data formatting | bytes 4423680
  459.1 4.6 all-to-all-start.6
  463.8 7.7 %slice_multiply_fusion = (f32[1440,720]{1,0:T(8,128)}, f32[1440,720]{1,0:T(8,128)}) fusion(f32[1440,1440]{1,0:T(8,128)} %copy-done.1, f32[720]{0:T(1024)S(1)} %fusion.69, f32[1440,1440]{1,0:T(8,128)} %copy-done), kind=kLoop, calls=%fused_computation.18 | loop fusion | flops 3110400 | bytes 16591680 | tf_op jit(solution)/shard_map/mul | solution.py:26
  471.5 45.1 %all-to-all-done.6 = bf16[16,2,34560]{2,1,0:T(2,128)(2,1)S(1)} async-done(((bf16[16,2,34560]{2,1,0:T(2,128)(2,1)}), bf16[16,2,34560]{2,1,0:T(2,128)(2,1)S(1)}, u32[]{:S(2)}, u32[]{:S(2)}) %all-to-all-start.6) | async-done | bytes 2211872 | tf_op jit(solution)/shard_map/all_to_all | solution.py:121
  516.6 18.6 %reshape.183 = bf16[12288,2,45]{2,1,0:T(2,128)(2,1)} reshape(bf16[16,2,34560]{2,1,0:T(2,128)(2,1)S(1)} %all-to-all-done.6) | data formatting | bytes 4423680
  535.2 14.6 %copy.107 = bf16[2,45,16,768]{3,1,2,0:T(8,128)(2,1)S(1)} copy(bf16[2,45,16,768]{1,0,3,2:T(2,128)(2,1)} %bitcast.159) | data formatting | bytes 4423680 | tf_op jit(solution)/shard_map/all_to_all | solution.py:121
  552.0 10.0 %add_convert_fusion = bf16[1440,768]{1,0:T(8,128)(2,1)} fusion(bf16[1440,768]{1,0:T(8,128)(2,1)} %all_to_all.99, bf16[1440,768]{1,0:T(8,128)(2,1)} %reshape.163, f32[1440,720]{1,0:T(8,128)} %get-tuple-element.20, f32[1440,720]{1,0:T(8,128)} %get-tuple-element.19), kind=kOutput, calls=%fused_computation.26 | convolution fusion | flops 3194588160 | bytes 14929920 | tf_op jit(solution)/shard_map/dot_general | solution.py:123
  564.6 62.8 %all_to_all.134 = bf16[16,90,768]{2,1,0:T(8,128)(2,1)S(1)} all-to-all(bf16[16,90,768]{2,1,0:T(8,128)(2,1)S(1)} %all_to_all.120), channel_id=1, replica_groups=mesh['lat'=4,'lon'=16,'ch'=4] {'lon'}, dimensions={0} | all-to-all | bytes 4423680 | tf_op jit(solution)/shard_map/all_to_all | solution.py:126
  (46 shorter events, 52.6 us)
Async XLA Ops:
  4.5 66.6 %all-to-all-start = ((bf16[90,16,768]{2,0,1:T(8,128)(2,1)}), bf16[90,16,768]{2,0,1:T(8,128)(2,1)S(1)}, u32[]{:S(2)}, u32[]{:S(2)}) async-start(bf16[90,16,768]{2,0,1:T(8,128)(2,1)} %copy.81), calls=%async_computation | async-start | bytes 4718592 | tf_op jit(solution)/shard_map/all_to_all | solution.py:110
  52.6 3.4 copy-start.1
  52.6 7.3 %copy-start = (f32[1440,1440]{1,0:T(8,128)}, f32[1440,1440]{1,0:T(8,128)S(1)}, u32[]{:S(2)}) copy-start(f32[1440,1440]{1,0:T(8,128)S(1)} %get-tuple-element.23) | copy-start | bytes 24883204
  155.4 30.6 %all-to-all-start.2 = ((bf16[2,45,128,96]{2,0,1,3:T(2,128)(2,1)}), bf16[2,45,128,96]{2,0,1,3:T(2,128)(2,1)S(1)}, u32[]{:S(2)}, u32[]{:S(2)}) async-start(bf16[2,45,128,96]{2,0,1,3:T(2,128)(2,1)} %copy.84), calls=%async_computation.2 | async-start | bytes 4423680 | tf_op jit(solution)/shard_map/all_to_all | solution.py:87
  217.2 4.0 copy-start.2
  217.2 4.3 copy-start.3
  217.2 30.9 %all-to-all-start.3 = ((bf16[4,2,138240]{2,1,0:T(2,128)(2,1)}), bf16[4,2,138240]{2,1,0:T(2,128)(2,1)S(1)}, u32[]{:S(2)}, u32[]{:S(2)}) async-start(bf16[4,2,138240]{2,1,0:T(2,128)(2,1)} %reshape.178), calls=%async_computation.3 | async-start | bytes 4423680 | tf_op jit(solution)/shard_map/all_to_all | solution.py:91
  267.3 7.8 %copy-start.4 = (f32[1,2,96]{2,1,0:T(2,128)S(1)}, f32[1,2,96]{2,1,0:T(2,128)}, u32[]{:S(2)}) copy-start(f32[1,2,96]{2,1,0:T(2,128)} %param.7) | copy-start | bytes 2308
  275.1 0.8 copy-start.5
  459.1 57.5 %all-to-all-start.6 = ((bf16[16,2,34560]{2,1,0:T(2,128)(2,1)}), bf16[16,2,34560]{2,1,0:T(2,128)(2,1)S(1)}, u32[]{:S(2)}, u32[]{:S(2)}) async-start(bf16[16,2,34560]{2,1,0:T(2,128)(2,1)} %reshape.182), calls=%async_computation.6 | async-start | bytes 4423680 | tf_op jit(solution)/shard_map/all_to_all | solution.py:121
where the time goes:
time: 643 us; the launch traced here: 631 us
  local copies, waits for them, and re-layouts  237 us (37%)
  blocking collectives  184 us (29%)
  waiting for transfers between devices  94.9 us (15%)
  other arithmetic  59.1 us (9%)
  matrix products  31.7 us (5%)
  starting transfers between devices  23.6 us (4%)
    unnamed x23, local copies, waits for them, and re-layouts  104 us
    all_to_all x1, blocking collectives, per_device(): lax.all_to_all(grid_out.astype(jnp.bfloat16), 'lon', split_axis=0, concat...  62.8 us
    all_to_all x1, blocking collectives, per_device(): lax.all_to_all(spectra, 'lon', split_axis=1, concat_axis=2, tiled=True)  61.5 us
    reshape x1, local copies, waits for them, and re-layouts, per_device(): returned = returned.reshape(2, returned.shape[1], local_lat * local_chan)  52.8 us
    all_to_all x1, waiting for transfers between devices, per_device(): lax.all_to_all(returned, 'lon', split_axis=2, concat_axis=1, tiled=True)  45.1 us
    sin x2, other arithmetic, phase_tables(): return (jnp.cos(angles), jnp.sin(angles))  40.9 us
    all_to_all x1, blocking collectives, lat_apply(): lax.all_to_all(result, 'lat', split_axis=2, concat_axis=3, tiled=True)  30.3 us
    all_to_all x1, blocking collectives, lat_apply(): lax.all_to_all(data, 'lat', split_axis=3, concat_axis=2, tiled=True)  29.8 us
  transfers between devices with their start and end apart: 4, of which 4 were waited for; matrix products, arithmetic and copies ran while one was open for 10% of the time, Pallas kernels for 0%

commit v1 on v0

v1 whole, which is shorter than its diff:
```python
import functools
import math

import jax
import jax.numpy as jnp
import numpy as np
from jax import lax
from jax.experimental import pallas as pl
from jax.experimental.pallas import tpu as pltpu
from jax.sharding import PartitionSpec as P

shrink_level = 0.01
group = ("lat", "lon")


def phases(left, right, length):
    product = (left[:, None].astype(np.int64) * right[None, :]) % length
    angles = product.astype(np.float32) * np.float32(2.0 * math.pi / length)
    angles = angles.astype(np.float64)
    return np.cos(angles).astype(np.float32), np.sin(angles).astype(np.float32)


def lon_tables(lat_devices, lon_devices, local_lon, rows):
    length = local_lon * lon_devices
    kept = length // 2
    i, j, r = np.meshgrid(
        np.arange(lat_devices), np.arange(lon_devices), np.arange(rows), indexing="ij"
    )
    offset = (i * rows + r).reshape(-1)
    place = (j.reshape(-1) * local_lon + offset).astype(np.int64)
    real = (offset < local_lon).astype(np.float32)
    place = np.where(offset < local_lon, place, 0)
    cosine, sine = phases(np.arange(kept), place, length)
    factor = np.float32(1.0 / math.sqrt(length))
    forward = np.concatenate([cosine, -sine], axis=0) * factor * real
    weights = np.where(np.arange(kept) == 0, 1.0, 2.0).astype(np.float32)[:, None]
    inverse = np.concatenate([cosine * weights, -sine * weights], axis=0).T * factor
    inverse = inverse * real[:, None]
    return forward.astype(jnp.bfloat16), inverse.astype(jnp.bfloat16)


def lat_table(length):
    half = length // 2
    cosine, sine = phases(np.arange(half + 1), np.arange(length), length)
    sine[0] = cosine[half]
    table = np.stack([cosine[:half], sine[:half]], axis=1).reshape(length, length)
    return (table * np.float32(1.0 / math.sqrt(length))).astype(jnp.bfloat16)


def first_layer(weight, special):
    u, v = weight[0], weight[1]
    z = jnp.zeros_like(u)
    rows = lambda *blocks: jnp.concatenate([jnp.concatenate(b, axis=1) for b in blocks], axis=0)
    pair = rows((u, v, u, v), (v, -u, -v, u), (-v, u, -v, u), (u, v, -u, -v))
    single = rows((u, v, z, z), (z, z, u, v), (-v, u, z, z), (z, z, -v, u))
    return jnp.stack([jnp.where(special, single, pair), pair])


def second_layer(weight, bias, lanes):
    u, v = weight[0], weight[1]
    width = u.shape[0]
    z = jnp.zeros((width, lanes), u.dtype)
    wide = lambda m: jnp.pad(m, ((0, 0), (0, lanes - width)))
    u, v, m = wide(u), wide(v), wide(-v)
    rows = [(u, v, z, z), (m, u, z, z), (z, z, u, v), (z, z, m, u)]
    matrix = jnp.concatenate([jnp.concatenate(r, axis=1) for r in rows], axis=0)
    padded = jnp.pad(bias, ((0, 0), (0, lanes - width))).reshape(-1)
    return matrix, jnp.concatenate([padded, padded])[None]


def spectral_kernel(flag, x, fwd, inv, w1, b1, w2, b2, out, z, y):
    kept = fwd.shape[0] // 2
    width = w1.shape[1] // 4
    slots = x.shape[1] // (2 * width)
    lanes = w2.shape[1] // 4
    for part in range(2):
        rows = pl.ds(part * kept, kept)
        z[rows, :] = jnp.dot(fwd[rows, :], x[...], preferred_element_type=jnp.float32).astype(
            z.dtype
        )
    for s in range(slots):
        cols = pl.ds(s * 2 * width, 2 * width)
        layer = w1[min(s, 1)]
        hidden = jnp.dot(
            z[pl.ds(0, kept), cols], layer[: 2 * width], preferred_element_type=jnp.float32
        )
        hidden = hidden + jnp.dot(
            z[pl.ds(kept, kept), cols], layer[2 * width :], preferred_element_type=jnp.float32
        )
        hidden = jnp.maximum(hidden + b1[...], 0.0).astype(jnp.bfloat16)
        v = jnp.dot(hidden, w2[...], preferred_element_type=jnp.float32) + b2[...]
        v = v - jnp.minimum(jnp.maximum(v, -shrink_level), shrink_level)
        re, im, re2, im2 = [v[:, n * lanes : (n + 1) * lanes] for n in range(4)]
        top = (re + re2, im2 - im)
        bottom = (im + im2, re - re2)
        if s == 0:
            alone = flag[0] == 1
            top = (jnp.where(alone, re, top[0]), jnp.where(alone, re2, top[1]))
            bottom = (jnp.where(alone, im, bottom[0]), jnp.where(alone, im2, bottom[1]))
        for start, (a, b) in ((0, top), (kept, bottom)):
            y[pl.ds(start, kept), cols] = jnp.concatenate(
                [a[:, :width], b[:, :width]], axis=1
            ).astype(y.dtype)
    block = inv.shape[0] // 2
    for part in range(2):
        rows = pl.ds(part * block, block)
        out[rows, :] = jnp.dot(inv[rows, :], y[...], preferred_element_type=jnp.float32).astype(
            out.dtype
        )


def spectral(flag, x, fwd, inv, w1, b1, w2, b2):
    whole = pl.BlockSpec(memory_space=pltpu.VMEM)
    rows, cols = fwd.shape[0], x.shape[1]
    return pl.pallas_call(
        spectral_kernel,
        out_shape=jax.ShapeDtypeStruct(x.shape, jnp.bfloat16),
        in_specs=[pl.BlockSpec(memory_space=pltpu.SMEM)] + [whole] * 7,
        out_specs=whole,
        scratch_shapes=[pltpu.VMEM((rows, cols), jnp.bfloat16)] * 2,
        compiler_params=pltpu.CompilerParams(vmem_limit_bytes=60 * 2**20),
        name="spectral",
    )(flag, x, fwd, inv, w1, b1, w2, b2)


def per_device(grid_field, first_weight, first_bias, second_weight, second_bias):
    lon_n, lat_n = lax.axis_size("lon"), lax.axis_size("lat")
    width = first_weight.shape[2]
    local_lon, _, merged = grid_field.shape
    local_lat = merged // width
    rows = -(-local_lon // (8 * lat_n)) * 8
    lat_size = local_lat * lat_n
    everyone = lat_n * lon_n
    fwd, inv = lon_tables(lat_n, lon_n, local_lon, rows)
    lat = lat_table(lat_size)
    special = (lax.axis_index("lat") == 0) & (lax.axis_index("lon") == 0)
    w1 = first_layer(first_weight[0], special)
    b1 = jnp.concatenate([first_bias[0].reshape(-1)] * 2)[None]
    w2, b2 = second_layer(second_weight[0], second_bias[0], 128)
    flag = special.astype(jnp.int32).reshape(1)

    field = jnp.pad(grid_field[:, 0], ((0, rows * lat_n - local_lon), (0, 0)))
    field = field.reshape(lat_n, rows, merged)
    field = lax.all_to_all(field, "lat", split_axis=0, concat_axis=0, tiled=True)
    field = field.reshape(lat_n, rows, local_lat, width)
    table = jnp.asarray(lat).reshape(lat_size, lat_n, local_lat)
    comps = jnp.einsum(
        "qih,iwhc->wqc", table, field, preferred_element_type=jnp.float32
    ).astype(jnp.bfloat16)
    comps = comps.reshape(rows, everyone, -1).transpose(1, 0, 2)
    comps = lax.all_to_all(comps, group, split_axis=0, concat_axis=0, tiled=True)
    x = comps.reshape(everyone * rows, -1)
    x = spectral(flag, x, jnp.asarray(fwd), jnp.asarray(inv), w1, b1, w2, b2)
    back = x.reshape(everyone, rows, -1)
    back = lax.all_to_all(back, group, split_axis=0, concat_axis=0, tiled=True)
    back = back.transpose(1, 0, 2).reshape(rows, lat_size, width)
    mixed = jnp.einsum("qih,wqc->iwhc", table, back, preferred_element_type=jnp.float32)
    mixed = (mixed + field.astype(jnp.float32)).astype(jnp.bfloat16)
    mixed = mixed.reshape(lat_n, rows, merged)
    mixed = lax.all_to_all(mixed, "lat", split_axis=0, concat_axis=0, tiled=True)
    return mixed.reshape(lat_n * rows, merged)[:local_lon, None, :]


def solution(mesh):
    in_specs = (
        P("lon", "ch", "lat"),
        P("ch", None, None, None),
        P("ch", None, None),
        P("ch", None, None, None),
        P("ch", None, None),
    )
    return jax.shard_map(
        per_device, mesh=mesh, in_specs=in_specs, out_specs=P("lon", "ch", "lat"), check_vma=False
    )
```

time: 643 us -> 264 us (0.41); the launches traced: 631 us -> 261 us
  local copies, waits for them, and re-layouts: 237 us -> 43.5 us
  blocking collectives: 184 us -> 63.8 us
  other arithmetic: 59.1 us -> 2.95 us
  matrix products: 31.7 us -> 9.05 us
  Pallas kernels: 0 us -> 16.5 us
  waiting for transfers between devices: 94.9 us -> 105 us
    all_to_all x4 -> x2, blocking collectives: 184 us -> 63.8 us  [the longest x1 32.1 us: per_device(): lax.all_to_all(mixed, 'lat', split_axis=0, concat_axis=0, tiled=True)]
    unnamed x23 -> x8, local copies, waits for them, and re-layouts: 104 us -> 0.01 us
    reshape x6, local copies, waits for them, and re-layouts: 67.8 us -> 23.5 us  [the longest x2 7.13 us: per_device(): field = field.reshape(lat_n, rows, local_lat, width)]
    all_to_all x14 -> x0, local copies, waits for them, and re-layouts: 43.7 us -> none  [the longest x1 14.6 us: per_device(): lax.all_to_all(returned, 'lon', split_axis=2, concat_axis=1, tiled=True)]
    sin x2 -> x0, other arithmetic: 40.9 us -> none  [phase_tables(): return (jnp.cos(angles), jnp.sin(angles))]
    dot_general x6 -> x2, matrix products: 31.7 us -> 9.05 us  [the longest x1 4.68 us: per_device(): jnp.einsum('qih,wqc->iwhc', table, back, preferred_element_type=jnp.float32)]
    pallas_call x0 -> x1, Pallas kernels: none -> 16.5 us  [spectral(): pl.pallas_call(spectral_kernel, out_shape=jax.ShapeDtypeStruct(x.shape, j...]
    all_to_all x4 -> x2, waiting for transfers between devices: 94.9 us -> 105 us  [the longest x1 53.4 us: per_device(): back = lax.all_to_all(back, group, split_axis=0, concat_axis=0, tiled=True)]
  transfers between devices with their start and end apart: 4 -> 2, of which waited for: 4 -> 2; matrix products, arithmetic and copies ran while one was open for 10% -> 2% of each run, Pallas kernels for 0% -> 0%
where the time goes in v1:
time: 264 us; the launch traced here: 261 us
  waiting for transfers between devices  105 us (40%)
  blocking collectives  63.8 us (24%)
  local copies, waits for them, and re-layouts  43.5 us (16%)
  starting transfers between devices  19.2 us (7%)
  Pallas kernels  16.5 us (6%)
  matrix products  9.05 us (3%)
  other arithmetic  2.95 us (1%)
    all_to_all x1, waiting for transfers between devices, per_device(): back = lax.all_to_all(back, group, split_axis=0, concat_axis=0, tiled=True)  53.4 us
    all_to_all x1, waiting for transfers between devices, per_device(): lax.all_to_all(comps, group, split_axis=0, concat_axis=0, tiled=True)  52.1 us
    all_to_all x1, blocking collectives, per_device(): lax.all_to_all(mixed, 'lat', split_axis=0, concat_axis=0, tiled=True)  32.1 us
    all_to_all x1, blocking collectives, per_device(): lax.all_to_all(field, 'lat', split_axis=0, concat_axis=0, tiled=True)  31.7 us
    pallas_call x1, Pallas kernels, spectral(): pl.pallas_call(spectral_kernel, out_shape=jax.ShapeDtypeStruct(x.shape, j...  16.5 us
    all_to_all x1, starting transfers between devices, per_device(): lax.all_to_all(comps, group, split_axis=0, concat_axis=0, tiled=True)  12.1 us
    all_to_all x1, starting transfers between devices, per_device(): back = lax.all_to_all(back, group, split_axis=0, concat_axis=0, tiled=True)  7.17 us
    reshape x2, local copies, waits for them, and re-layouts, per_device(): field = field.reshape(lat_n, rows, local_lat, width)  7.13 us
  transfers between devices with their start and end apart: 2, of which 2 were waited for; matrix products, arithmetic and copies ran while one was open for 2% of the time, Pallas kernels for 0%

profile of v1, /device:TPU:38, one launch (start us, length us, event | category | flops | bytes accessed | tf_op | source)
XLA Modules:
  0.0 260.7 jit_solution(14010861927589768904)
XLA Ops:
  0.0 1.9 pad.18
  1.9 31.7 %all_to_all.20 = bf16[4,24,12288]{2,1,0:T(8,128)(2,1)} all-to-all(bf16[4,24,12288]{2,1,0:T(8,128)(2,1)S(1)} %bitcast.72), channel_id=1, replica_groups=mesh['lat'=4,'lon'=16,'ch'=4] {'lat'}, dimensions={0} | all-to-all | bytes 4718592 | tf_op jit(solution)/shard_map/all_to_all | solution.py:144
  33.6 4.5 %reshape.153 = bf16[4,24,128,96]{3,2,1,0:T(8,128)(2,1)S(1)} reshape(bf16[4,24,12288]{2,1,0:T(8,128)(2,1)} %all_to_all.20) | data formatting | bytes 4718592 | tf_op jit(solution)/shard_map/reshape | solution.py:145
  38.1 4.4 %fusion.3 = bf16[24,512,96]{1,2,0:T(8,128)(2,1)} fusion(bf16[4,24,128,96]{3,2,1,0:T(8,128)(2,1)S(1)} %reshape.153, bf16[512,4,128,1]{2,0,3,1:T(8,128)(2,1)} %constant.44), kind=kOutput, calls=%fused_computation.5 | convolution fusion | flops 1209139200 | bytes 5242880 | tf_op jit(solution)/shard_map/qih,iwhc->wqc/dot_general | solution.py:147
  42.5 4.5 %copy.17 = bf16[24,512,96]{2,1,0:T(8,128)(2,1)} copy(bf16[24,512,96]{1,2,0:T(8,128)(2,1)} %fusion.3) | data formatting | bytes 4718592 | tf_op jit(solution)/shard_map/convert_element_type | solution.py:149
  47.0 6.0 %reshape.155 = bf16[24,64,768]{2,1,0:T(8,128)(2,1)} reshape(bf16[24,512,96]{2,1,0:T(8,128)(2,1)} %copy.17) | data formatting | bytes 4718592 | tf_op jit(solution)/shard_map/reshape | solution.py:150
  53.0 4.4 %copy.18 = bf16[64,24,768]{2,1,0:T(8,128)(2,1)} copy(bf16[64,24,768]{2,0,1:T(8,128)(2,1)} %bitcast.74) | data formatting | bytes 4718592 | tf_op jit(solution)/shard_map/transpose | solution.py:150
  57.4 12.1 %all-to-all-start.1 = ((bf16[64,24,768]{2,1,0:T(8,128)(2,1)}), bf16[64,24,768]{2,1,0:T(8,128)(2,1)}, u32[]{:S(2)}, u32[]{:S(2)}) async-start(bf16[64,24,768]{2,1,0:T(8,128)(2,1)} %copy.18), calls=%async_computation.1 | async-start | bytes 4718592 | tf_op jit(solution)/shard_map/all_to_all | solution.py:151
  69.5 0.0 copy-done.2
  69.5 0.1 reshape_squeeze.3
  69.5 0.1 pad_maximum_fusion.15
  69.6 0.6 broadcast_in_dim.9.b1
  70.2 0.0 copy-done.1
  70.3 0.6 pad_maximum_fusion.16
  70.9 0.2 fusion.11
  71.1 0.2 maximum_bitcast_fusion
  71.3 0.2 fusion.8
  71.5 0.1 maximum_select_fusion
  71.6 0.8 maximum_maximum_fusion.w2
  72.4 0.9 pad_maximum_fusion.w1
  73.3 52.1 %all-to-all-done.1 = bf16[64,24,768]{2,1,0:T(8,128)(2,1)} async-done(((bf16[64,24,768]{2,1,0:T(8,128)(2,1)}), bf16[64,24,768]{2,1,0:T(8,128)(2,1)}, u32[]{:S(2)}, u32[]{:S(2)}) %all-to-all-start.1) | async-done | bytes 2359328 | tf_op jit(solution)/shard_map/all_to_all | solution.py:151
  125.3 16.5 %spectral.1 = bf16[1536,768]{1,0:T(8,128)(2,1)} custom-call(s32[1]{0:T(128)} %bitcast.flag, bf16[1536,768]{1,0:T(8,128)(2,1)} %bitcast.8.x, bf16[1440,1536]{1,0:T(8,128)(2,1)} %constant.26.clone.fwd, bf16[1536,1440]{1,0:T(8,128)(2,1)} %constant.27.clone.inv, bf16[2,384,384]{2,1,0:T(8,128)(2,1)} %pad_maximum_fusion.w1, f32[1,384]{1,0:T(1,128)} %broadcast_in_dim.9.b1, ...), custom_call_target="tpu_custom_call" | custom-call | tf_op jit(solution)/shard_map/spectral/pallas_call | solution.py:115
  141.9 7.2 %all-to-all-start.2 = ((bf16[64,24,768]{2,1,0:T(8,128)(2,1)}), bf16[64,24,768]{2,1,0:T(8,128)(2,1)}, u32[]{:S(2)}, u32[]{:S(2)}) async-start(bf16[64,24,768]{2,1,0:T(8,128)(2,1)} %bitcast.73), calls=%async_computation.2 | async-start | bytes 4718592 | tf_op jit(solution)/shard_map/all_to_all | solution.py:155
  149.0 2.6 %copy.21 = bf16[4,24,128,96]{2,3,0,1:T(8,128)(2,1)} copy(bf16[4,24,128,96]{3,2,1,0:T(8,128)(2,1)S(1)} %reshape.153) | data formatting | bytes 4718592 | tf_op jit(solution)/shard_map/reshape | solution.py:145
  151.7 53.4 %all-to-all-done.2 = bf16[64,24,768]{2,1,0:T(8,128)(2,1)} async-done(((bf16[64,24,768]{2,1,0:T(8,128)(2,1)}), bf16[64,24,768]{2,1,0:T(8,128)(2,1)}, u32[]{:S(2)}, u32[]{:S(2)}) %all-to-all-start.2) | async-done | bytes 2359328 | tf_op jit(solution)/shard_map/all_to_all | solution.py:155
  205.1 3.6 %copy.19 = bf16[24,64,768]{2,1,0:T(8,128)(2,1)} copy(bf16[24,64,768]{2,0,1:T(8,128)(2,1)} %bitcast.26) | data formatting | bytes 4718592 | tf_op jit(solution)/shard_map/transpose | solution.py:156
  208.6 5.3 %reshape.159 = bf16[24,512,96]{2,1,0:T(8,128)(2,1)S(1)} reshape(bf16[24,64,768]{2,1,0:T(8,128)(2,1)} %copy.19) | data formatting | bytes 4718592 | tf_op jit(solution)/shard_map/reshape | solution.py:156
  213.9 4.7 %fusion = bf16[4,24,128,96]{2,3,0,1:T(8,128)(2,1)} fusion(bf16[4,24,128,96]{2,3,0,1:T(8,128)(2,1)} %copy.21, bf16[512,4,128,1]{2,0,1,3:T(8,128)(2,1)} %constant.45, bf16[24,512,96]{2,1,0:T(8,128)(2,1)S(1)} %reshape.159), kind=kOutput, calls=%fused_computation.1 | convolution fusion | flops 1211498496 | bytes 7602176 | tf_op jit(solution)/shard_map/qih,wqc->iwhc/dot_general | solution.py:157
  218.6 3.4 %copy.22 = bf16[4,24,128,96]{3,2,1,0:T(8,128)(2,1)S(1)} copy(bf16[4,24,128,96]{2,3,0,1:T(8,128)(2,1)} %fusion) | data formatting | bytes 4718592 | tf_op jit(solution)/shard_map/convert_element_type | solution.py:158
  222.0 5.1 %reshape.160 = bf16[4,24,12288]{2,1,0:T(8,128)(2,1)} reshape(bf16[4,24,128,96]{3,2,1,0:T(8,128)(2,1)S(1)} %copy.22) | data formatting | bytes 4718592 | tf_op jit(solution)/shard_map/reshape | solution.py:159
  227.1 32.1 %all_to_all.21 = bf16[4,24,12288]{2,1,0:T(8,128)(2,1)S(1)} all-to-all(bf16[4,24,12288]{2,1,0:T(8,128)(2,1)} %reshape.160), channel_id=1, replica_groups=mesh['lat'=4,'lon'=16,'ch'=4] {'lat'}, dimensions={0} | all-to-all | bytes 4718592 | tf_op jit(solution)/shard_map/all_to_all | solution.py:160
  259.2 1.6 slice_bitcast_fusion
  (16 shorter events, 0.1 us)
Async XLA Ops:
  57.3 12.1 %copy-start.2 = (f32[1,2,96]{2,1,0:T(2,128)S(1)}, f32[1,2,96]{2,1,0:T(2,128)}, u32[]{:S(2)}) copy-start(f32[1,2,96]{2,1,0:T(2,128)} %param.10) | copy-start | bytes 2308
  57.3 12.9 %copy-start.1 = (bf16[1,2,96,96]{3,2,1,0:T(8,128)(2,1)S(1)}, bf16[1,2,96,96]{3,2,1,0:T(8,128)(2,1)}, u32[]{:S(2)}) copy-start(bf16[1,2,96,96]{3,2,1,0:T(8,128)(2,1)} %param.11) | copy-start | bytes 110596
  57.3 12.9 %copy-start.3 = (f32[1,2,96]{2,1,0:T(2,128)S(1)}, f32[1,2,96]{2,1,0:T(2,128)}, u32[]{:S(2)}) copy-start(f32[1,2,96]{2,1,0:T(2,128)} %param.12) | copy-start | bytes 2308
  57.3 13.5 %copy-start = (bf16[1,2,96,96]{3,2,1,0:T(8,128)(2,1)S(1)}, bf16[1,2,96,96]{3,2,1,0:T(8,128)(2,1)}, u32[]{:S(2)}) copy-start(bf16[1,2,96,96]{3,2,1,0:T(8,128)(2,1)} %param.9) | copy-start | bytes 110596
  57.4 68.0 %all-to-all-start.1 = ((bf16[64,24,768]{2,1,0:T(8,128)(2,1)}), bf16[64,24,768]{2,1,0:T(8,128)(2,1)}, u32[]{:S(2)}, u32[]{:S(2)}) async-start(bf16[64,24,768]{2,1,0:T(8,128)(2,1)} %copy.18), calls=%async_computation.1 | async-start | bytes 4718592 | tf_op jit(solution)/shard_map/all_to_all | solution.py:151
  141.9 63.2 %all-to-all-start.2 = ((bf16[64,24,768]{2,1,0:T(8,128)(2,1)}), bf16[64,24,768]{2,1,0:T(8,128)(2,1)}, u32[]{:S(2)}, u32[]{:S(2)}) async-start(bf16[64,24,768]{2,1,0:T(8,128)(2,1)} %bitcast.73), calls=%async_computation.2 | async-start | bytes 4718592 | tf_op jit(solution)/shard_map/all_to_all | solution.py:155

commit v2 on v1

v2 whole, which is shorter than its diff:
```python
import functools
import math

import jax
import jax.numpy as jnp
import numpy as np
from jax import lax
from jax.experimental import pallas as pl
from jax.experimental.pallas import tpu as pltpu
from jax.sharding import PartitionSpec as P


shrink_level = 0.01
group = ("lat", "lon")


def phases(left, right, length):
    product = (left[:, None].astype(np.int64) * right[None, :]) % length
    angles = product.astype(np.float32) * np.float32(2.0 * math.pi / length)
    angles = angles.astype(np.float64)
    return np.cos(angles).astype(np.float32), np.sin(angles).astype(np.float32)


def lon_tables(lat_devices, lon_devices, local_lon, rows, chunk):
    length = local_lon * lon_devices
    kept = length // 2
    i, j, r = np.meshgrid(
        np.arange(lat_devices), np.arange(lon_devices), np.arange(*chunk), indexing="ij"
    )
    offset = (i * rows + r).reshape(-1)
    place = (j.reshape(-1) * local_lon + offset).astype(np.int64)
    real = (offset < local_lon).astype(np.float32)
    place = np.where(offset < local_lon, place, 0)
    cosine, sine = phases(np.arange(kept), place, length)
    factor = np.float32(1.0 / math.sqrt(length))
    forward = np.concatenate([cosine, -sine], axis=0) * factor * real
    weights = np.where(np.arange(kept) == 0, 1.0, 2.0).astype(np.float32)[:, None]
    inverse = np.concatenate([cosine * weights, -sine * weights], axis=0).T * factor
    inverse = inverse * real[:, None]
    return forward.astype(jnp.bfloat16), inverse.astype(jnp.bfloat16)


def lat_table(length):
    half = length // 2
    cosine, sine = phases(np.arange(half + 1), np.arange(length), length)
    sine[0] = cosine[half]
    table = np.stack([cosine[:half], sine[:half]], axis=1).reshape(length, length)
    return (table * np.float32(1.0 / math.sqrt(length))).astype(jnp.bfloat16)


def first_layer(weight, special):
    u, v = weight[0], weight[1]
    z = jnp.zeros_like(u)
    rows = lambda *blocks: jnp.concatenate([jnp.concatenate(b, axis=1) for b in blocks], axis=0)
    pair = rows((u, v, u, v), (v, -u, -v, u), (-v, u, -v, u), (u, v, -u, -v))
    single = rows((u, v, z, z), (z, z, u, v), (-v, u, z, z), (z, z, -v, u))
    return jnp.stack([jnp.where(special, single, pair), pair])


def second_layer(weight, bias, lanes):
    u, v = weight[0], weight[1]
    width = u.shape[0]
    z = jnp.zeros((width, lanes), u.dtype)
    wide = lambda m: jnp.pad(m, ((0, 0), (0, lanes - width)))
    u, v, m = wide(u), wide(v), wide(-v)
    rows = [(u, v, z, z), (m, u, z, z), (z, z, u, v), (z, z, m, u)]
    matrix = jnp.concatenate([jnp.concatenate(r, axis=1) for r in rows], axis=0)
    padded = jnp.pad(bias, ((0, 0), (0, lanes - width))).reshape(-1)
    return matrix, jnp.concatenate([padded, padded])[None]


def soft_threshold(v):
    return v - jnp.minimum(jnp.maximum(v, -shrink_level), shrink_level)


def spectral_kernel(flag, *refs, chunks):
    xs, fwds = refs[:chunks], refs[chunks : 2 * chunks]
    inv, w1, b1, w2, b2, out, y, z = refs[2 * chunks :]
    kept = fwds[0].shape[0] // 2
    width = w1.shape[1] // 4
    slots = y.shape[1] // (2 * width)
    lanes = w2.shape[1] // 4
    for part in range(2):
        rows = pl.ds(part * kept, kept)
        total = None
        for x, fwd in zip(xs, fwds):
            term = jnp.dot(fwd[rows, :], x[...], preferred_element_type=jnp.float32)
            total = term if total is None else total + term
        z[rows, :] = total.astype(z.dtype)
    for s in range(slots):
        cols = pl.ds(s * 2 * width, 2 * width)
        layer = w1[min(s, 1)]
        hidden = jnp.dot(
            z[pl.ds(0, kept), cols], layer[: 2 * width], preferred_element_type=jnp.float32
        )
        hidden = hidden + jnp.dot(
            z[pl.ds(kept, kept), cols], layer[2 * width :], preferred_element_type=jnp.float32
        )
        hidden = jnp.maximum(hidden + b1[...], 0.0).astype(jnp.bfloat16)
        v = jnp.dot(hidden, w2[...], preferred_element_type=jnp.float32) + b2[...]
        v = soft_threshold(v)
        re, im, re2, im2 = [v[:, n * lanes : (n + 1) * lanes] for n in range(4)]
        top = (re + re2, im2 - im)
        bottom = (im + im2, re - re2)
        if s == 0:
            alone = flag[0] == 1
            top = (jnp.where(alone, re, top[0]), jnp.where(alone, re2, top[1]))
            bottom = (jnp.where(alone, im, bottom[0]), jnp.where(alone, im2, bottom[1]))
        for start, (a, b) in ((0, top), (kept, bottom)):
            y[pl.ds(start, kept), cols] = jnp.concatenate(
                [a[:, :width], b[:, :width]], axis=1
            ).astype(y.dtype)
    out[...] = jnp.dot(inv[...], y[...], preferred_element_type=jnp.float32).astype(out.dtype)


def spectral(flag, xs, fwds, inv, w1, b1, w2, b2):
    whole = pl.BlockSpec(memory_space=pltpu.VMEM)
    rows, cols = fwds[0].shape[0], xs[0].shape[1]
    return pl.pallas_call(
        functools.partial(spectral_kernel, chunks=len(xs)),
        out_shape=[
            jax.ShapeDtypeStruct((inv.shape[0], cols), jnp.bfloat16),
            jax.ShapeDtypeStruct((rows, cols), jnp.bfloat16),
        ],
        in_specs=[pl.BlockSpec(memory_space=pltpu.SMEM)] + [whole] * (2 * len(xs) + 5),
        out_specs=[whole, whole],
        scratch_shapes=[pltpu.VMEM((rows, cols), jnp.bfloat16)],
        compiler_params=pltpu.CompilerParams(vmem_limit_bytes=60 * 2**20),
        cost_estimate=pl.CostEstimate(
            flops=9 * 10**9, bytes_accessed=14 * 10**6, transcendentals=0
        ),
        name="spectral",
    )(flag, *xs, *fwds, inv, w1, b1, w2, b2)


def spread(scratch, start, group, width):
    for n in range(group.shape[1] // width):
        scratch[pl.ds(start + 8 * n, 8), pl.ds(0, width)] = group[:, n * width : (n + 1) * width]


def gather(scratch, start, count, width):
    return jnp.concatenate(
        [scratch[pl.ds(start + 8 * n, 8), :][:, :width] for n in range(count)], axis=1
    )


def transform(table, source, target, size):
    for r in range(0, 8, 2):
        pair = [source[pl.ds(r + k, size, stride=8), :].astype(jnp.bfloat16) for k in range(2)]
        sums = jnp.dot(
            table[...], jnp.concatenate(pair, axis=1), preferred_element_type=jnp.float32
        )
        for k in range(2):
            target[pl.ds(r + k, size, stride=8), :] = sums[:, k * 128 : (k + 1) * 128]


def lat_forward_kernel(place, *refs, width):
    fields, (table, out, source, target) = refs[:-4], refs[-4:]
    size = table.shape[0]
    span = 4 * width
    local = size // len(fields)
    for m, field in enumerate(fields):
        base = (place[0] ^ m) * (8 * local)

        def step(g, carry, field=field, base=base):
            group = field[:, pl.ds(pl.multiple_of(g * span, 128), span)].astype(jnp.float32)
            spread(source, pl.multiple_of(base + g * 32, 8), group, width)
            return carry

        lax.fori_loop(0, local // 4, step, 0, unroll=8)
    transform(table, source, target, size)
    per = out.shape[2] // span

    def finish(d, carry):
        for p in range(per):
            start = pl.multiple_of((d * per + p) * 32, 8)
            out[d, :, pl.ds(p * span, span)] = gather(target, start, 4, width).astype(out.dtype)
        return carry

    lax.fori_loop(0, out.shape[0], finish, 0, unroll=4)


def lat_inverse_kernel(place, back, table, *refs, width, count):
    fields, outs, (source, target) = refs[:count], refs[count : 2 * count], refs[2 * count :]
    size = table.shape[0]
    span = 4 * width
    local = size // count
    per = back.shape[2] // span

    def begin(d, carry):
        for p in range(per):
            start = pl.multiple_of((d * per + p) * 32, 8)
            spread(source, start, back[d, :, pl.ds(p * span, span)].astype(jnp.float32), width)
        return carry

    lax.fori_loop(0, back.shape[0], begin, 0, unroll=4)
    transform(table, source, target, size)
    for m, (field, out) in enumerate(zip(fields, outs)):
        base = (place[0] ^ m) * (8 * local)

        def step(g, carry, field=field, out=out, base=base):
            lanes = pl.ds(pl.multiple_of(g * span, 128), span)
            sums = gather(target, pl.multiple_of(base + g * 32, 8), 4, width)
            out[:, lanes] = (sums + field[:, lanes].astype(jnp.float32)).astype(out.dtype)
            return carry

        lax.fori_loop(0, local // 4, step, 0, unroll=8)


def lat_call(kernel, args, in_specs, out_shape, out_specs, rows, size, moved):
    return pl.pallas_call(
        kernel,
        grid=(rows // 8,),
        out_shape=out_shape,
        in_specs=[pl.BlockSpec(memory_space=pltpu.SMEM)] + in_specs,
        out_specs=out_specs,
        scratch_shapes=[pltpu.VMEM((8 * size, 128), jnp.float32)] * 2,
        compiler_params=pltpu.CompilerParams(vmem_limit_bytes=40 * 2**20),
        cost_estimate=pl.CostEstimate(
            flops=2 * rows * size * size * 128, bytes_accessed=2 * moved, transcendentals=0
        ),
    )(*args)


def lat_forward(place, fields, table, everyone, width):
    rows, merged = fields[0].shape
    size = table.shape[0]
    lanes = size * width // everyone
    strip = pl.BlockSpec((8, merged), lambda n: (n, 0))
    return lat_call(
        functools.partial(lat_forward_kernel, width=width),
        (place, *fields, table),
        [strip] * len(fields) + [pl.BlockSpec((size, size), lambda n: (0, 0))],
        jax.ShapeDtypeStruct((everyone, rows, lanes), jnp.bfloat16),
        pl.BlockSpec((everyone, 8, lanes), lambda n: (0, n, 0)),
        rows,
        size,
        rows * size * width * 2,
    )


def lat_inverse(place, back, table, fields, width):
    everyone, rows, lanes = back.shape
    size = table.shape[0]
    merged = fields[0].shape[1]
    strip = pl.BlockSpec((8, merged), lambda n: (n, 0))
    return lat_call(
        functools.partial(lat_inverse_kernel, width=width, count=len(fields)),
        (place, back, table, *fields),
        [
            pl.BlockSpec((everyone, 8, lanes), lambda n: (0, n, 0)),
            pl.BlockSpec((size, size), lambda n: (0, 0)),
        ]
        + [strip] * len(fields),
        [jax.ShapeDtypeStruct((rows, merged), jnp.bfloat16)] * len(fields),
        [strip] * len(fields),
        rows,
        size,
        rows * size * width * 2,
    )


def assemble_kernel(place, *refs, chunks, count):
    pieces, out = refs[:-1], refs[-1]
    rows, length = chunks[-1][1], out.shape[0]
    for n, (start, stop) in enumerate(chunks):
        for m in range(count):
            piece = pieces[n * count + m]
            block = place[0] ^ m
            rest = length - (count - 1) * rows - start

            def fill(piece=piece, block=block, start=start, stop=stop):
                row = pl.multiple_of(block * rows + start, 8)
                out[pl.ds(row, stop - start), :] = piece[...]

            if rest >= stop - start:
                fill()
            else:
                pl.when(block < count - 1)(fill)

                @pl.when(block == count - 1)
                def _(piece=piece, rest=rest):
                    out[pl.ds(length - rest, rest), :] = piece[pl.ds(0, rest), :]


def assemble(place, mixed, chunks, length):
    whole = pl.BlockSpec(memory_space=pltpu.VMEM)
    pieces = [piece for chunk in mixed for piece in chunk]
    return pl.pallas_call(
        functools.partial(assemble_kernel, chunks=chunks, count=len(mixed[0])),
        out_shape=jax.ShapeDtypeStruct((length, pieces[0].shape[1]), jnp.bfloat16),
        in_specs=[pl.BlockSpec(memory_space=pltpu.SMEM)] + [whole] * len(pieces),
        out_specs=whole,
        compiler_params=pltpu.CompilerParams(vmem_limit_bytes=16 * 2**20),
        cost_estimate=pl.CostEstimate(flops=0, bytes_accessed=5 * 10**6, transcendentals=0),
        name="assemble",
    )(place, *pieces)


def swap(pieces, count):
    return [pieces[0]] + [
        lax.ppermute(pieces[m], "lat", [(i, i ^ m) for i in range(count)]) for m in range(1, count)
    ]


def layer(grid_field, first_weight, first_bias, second_weight, second_bias):
    lon_n, lat_n = lax.axis_size("lon"), lax.axis_size("lat")
    width = first_weight.shape[2]
    local_lon, _, merged = grid_field.shape
    local_lat = merged // width
    rows = -(-local_lon // (8 * lat_n)) * 8
    lat_size = local_lat * lat_n
    everyone = lat_n * lon_n
    chunks = ((0, 8), (8, rows))
    tables = [lon_tables(lat_n, lon_n, local_lon, rows, c) for c in chunks]
    fwds = [jnp.asarray(t[0]) for t in tables]
    invs = [jnp.asarray(t[1]) for t in tables]
    lat = lat_table(lat_size)
    lat, lat_back = jnp.asarray(lat), jnp.asarray(np.ascontiguousarray(lat.T))
    special = (lax.axis_index("lat") == 0) & (lax.axis_index("lon") == 0)
    w1 = first_layer(first_weight[0], special)
    b1 = jnp.concatenate([first_bias[0].reshape(-1)] * 2)[None]
    w2, b2 = second_layer(second_weight[0], second_bias[0], 128)
    flag = special.astype(jnp.int32).reshape(1)
    me = lax.axis_index("lat")
    place = me.astype(jnp.int32).reshape(1)

    field = grid_field[:, 0]
    padded = jnp.pad(field, ((0, rows * lat_n - local_lon), (0, 0)))
    exchange = lambda x: lax.all_to_all(x, group, split_axis=0, concat_axis=0, tiled=True)
    flat = lambda x: x.reshape(-1, x.shape[-1])

    fields, xs = [], []
    for start, stop in chunks:
        whole = padded if (lat_n - 1) * rows + stop > local_lon else field
        pieces = [
            lax.dynamic_slice(whole, (rows * (me ^ m) + start, 0), (stop - start, merged))
            for m in range(lat_n)
        ]
        fields.append(swap(pieces, lat_n))
        xs.append(lat_forward(place, fields[-1], lat, everyone, width))
    for n in range(2):
        xs[n] = exchange(xs[n])
    last, y = spectral(flag, [flat(x) for x in xs], fwds, invs[1], w1, b1, w2, b2)
    outs = [None, last]
    outs[0] = jnp.dot(invs[0], y, preferred_element_type=jnp.float32).astype(jnp.bfloat16)
    mixed, backs = [None, None], [None, None]
    for n in (1, 0):
        if n == 0:
            outs[0], backs[1] = lax.optimization_barrier((outs[0], backs[1]))
        backs[n] = exchange(outs[n].reshape(everyone, chunks[n][1] - chunks[n][0], -1))
    for n in (1, 0):
        start, stop = chunks[n]
        pieces = lat_inverse(place, backs[n], lat_back, fields[n], width)
        mixed[n] = swap(pieces, lat_n)
    return assemble(place, mixed, chunks, local_lon)[:, None, :]


def solution(mesh):
    in_specs = (
        P("lon", "ch", "lat"),
        P("ch", None, None, None),
        P("ch", None, None),
        P("ch", None, None, None),
        P("ch", None, None),
    )
    return jax.shard_map(
        layer, mesh=mesh, in_specs=in_specs, out_specs=P("lon", "ch", "lat"), check_vma=False
    )
```

time: 264 us -> 238 us (0.902)
  blocking collectives: 63.8 us -> 0 us
  local copies, waits for them, and re-layouts: 43.5 us -> 14.1 us
  Pallas kernels: 16.5 us -> 42.8 us
  waiting for transfers between devices: 105 us -> 129 us
  starting transfers between devices: 19.2 us -> 43 us
  matrix products: 9.05 us -> 3.52 us
    all_to_all x2 -> x0, blocking collectives: 63.8 us -> none  [the longest x1 32.1 us: per_device(): lax.all_to_all(mixed, 'lat', split_axis=0, concat_axis=0, tiled=True)]
    ppermute x0 -> x12, waiting for transfers between devices: none -> 49.4 us  [swap(): lax.ppermute(pieces[m], 'lat', [(i, i ^ m) for i in range(count)])]
    pallas_call x1 -> x6, Pallas kernels: 16.5 us -> 42.8 us  [the longest x4 25.6 us: lat_call(): pl.pallas_call(kernel, grid=(rows // 8,), out_shape=out_shape, in_specs=[...]
    all_to_all x2 -> x4, waiting for transfers between devices: 105 us -> 79.3 us  [layer(): lax.all_to_all(x, group, split_axis=0, concat_axis=0, tiled=True)]
    reshape x5 -> x0, local copies, waits for them, and re-layouts: 23.5 us -> none  [the longest x2 7.13 us: per_device(): field = field.reshape(lat_n, rows, local_lat, width)]
    all_to_all x2 -> x4, starting transfers between devices: 19.2 us -> 34.9 us  [layer(): lax.all_to_all(x, group, split_axis=0, concat_axis=0, tiled=True)]
    unnamed x8 -> x36, local copies, waits for them, and re-layouts: 0.01 us -> 10.3 us
    ppermute x0 -> x12, starting transfers between devices: none -> 8.08 us  [swap(): lax.ppermute(pieces[m], 'lat', [(i, i ^ m) for i in range(count)])]
  transfers between devices with their start and end apart: 2 -> 16, of which waited for: 2 -> 10; matrix products, arithmetic and copies ran while one was open for 2% -> 3% of each run, Pallas kernels for 0% -> 9%
where the time goes in v2:
time: 238 us; the launch traced here: 235 us
  waiting for transfers between devices  129 us (54%)
  starting transfers between devices  43 us (18%)
  Pallas kernels  42.8 us (18%)
  local copies, waits for them, and re-layouts  14.1 us (6%)
  matrix products  3.52 us (1%)
  other arithmetic  2.97 us (1%)
    all_to_all x4, waiting for transfers between devices, layer(): lax.all_to_all(x, group, split_axis=0, concat_axis=0, tiled=True)  79.3 us
    ppermute x12, waiting for transfers between devices, swap(): lax.ppermute(pieces[m], 'lat', [(i, i ^ m) for i in range(count)])  49.4 us
    all_to_all x4, starting transfers between devices, layer(): lax.all_to_all(x, group, split_axis=0, concat_axis=0, tiled=True)  34.9 us
    pallas_call x4, Pallas kernels, lat_call(): pl.pallas_call(kernel, grid=(rows // 8,), out_shape=out_shape, in_specs=[...  25.6 us
    pallas_call x1, Pallas kernels, spectral(): pl.pallas_call(functools.partial(spectral_kernel, chunks=len(xs)), out_sh...  14.7 us
    unnamed x36, local copies, waits for them, and re-layouts  10.3 us
    ppermute x12, starting transfers between devices, swap(): lax.ppermute(pieces[m], 'lat', [(i, i ^ m) for i in range(count)])  8.08 us
  transfers between devices with their start and end apart: 16, of which 10 were waited for; matrix products, arithmetic and copies ran while one was open for 3% of the time, Pallas kernels for 9%

profile of v2, /device:TPU:38, one launch (start us, length us, event | category | flops | bytes accessed | tf_op | source)
XLA Modules:
  0.0 235.3 jit_solution(1692445059263840705)
XLA Ops:
  0.0 1.6 dynamic-slice_bitcast_fusion
  1.6 1.1 collective-permute-start.2
  3.5 5.2 %collective-permute-done.2.refs_3_ = bf16[8,12288]{1,0:T(8,128)(2,1)S(1)} collective-permute-done((bf16[8,12288]{1,0:T(8,128)(2,1)S(1)}, bf16[8,12288]{1,0:T(8,128)(2,1)S(1)}, u32[]{:S(2)}, u32[]{:S(2)}) %collective-permute-start.2) | collective-permute-done | bytes 196640 | tf_op jit(solution)/shard_map/ppermute | solution.py:302
  8.7 4.3 %collective-permute-done.1.refs_2_ = bf16[8,12288]{1,0:T(8,128)(2,1)S(1)} collective-permute-done((bf16[8,12288]{1,0:T(8,128)(2,1)S(1)}, bf16[8,12288]{1,0:T(8,128)(2,1)S(1)}, u32[]{:S(2)}, u32[]{:S(2)}) %collective-permute-start.1) | collective-permute-done | bytes 196640 | tf_op jit(solution)/shard_map/ppermute | solution.py:302
  13.1 1.0 copy-done.2
  14.1 4.6 %shard_map.109 = bf16[64,8,768]{2,1,0:T(8,128)(2,1)} custom-call(s32[1]{0:T(128)} %bitcast.place, bf16[8,12288]{1,0:T(8,128)(2,1)S(1)} %get-tuple-element.36.refs_0_, bf16[8,12288]{1,0:T(8,128)(2,1)S(1)} %collective-permute-done.refs_1_, bf16[8,12288]{1,0:T(8,128)(2,1)S(1)} %collective-permute-done.1.refs_2_, ...), custom_call_target="tpu_custom_call" | custom-call | flops 536870912 | bytes 1572864 | tf_op jit(solution)/shard_map/pallas_call | solution.py:211
  18.8 11.9 %all-to-all-start = ((bf16[64,8,768]{2,1,0:T(8,128)(2,1)}), bf16[64,8,768]{2,1,0:T(8,128)(2,1)}, u32[]{:S(2)}, u32[]{:S(2)}) async-start(bf16[64,8,768]{2,1,0:T(8,128)(2,1)} %shard_map.109), calls=%async_computation | async-start | bytes 1572864 | tf_op jit(solution)/shard_map/all_to_all | solution.py:330
  31.1 1.5 collective-permute-start.5
  33.3 13.8 %collective-permute-done.5.refs_3_ = bf16[16,12288]{1,0:T(8,128)(2,1)S(1)} collective-permute-done((bf16[16,12288]{1,0:T(8,128)(2,1)S(1)}, bf16[16,12288]{1,0:T(8,128)(2,1)S(1)}, u32[]{:S(2)}, u32[]{:S(2)}) %collective-permute-start.5) | collective-permute-done | bytes 393248 | tf_op jit(solution)/shard_map/ppermute | solution.py:302
  47.1 11.3 %collective-permute-done.4.refs_2_ = bf16[16,12288]{1,0:T(8,128)(2,1)S(1)} collective-permute-done((bf16[16,12288]{1,0:T(8,128)(2,1)S(1)}, bf16[16,12288]{1,0:T(8,128)(2,1)S(1)}, u32[]{:S(2)}, u32[]{:S(2)}) %collective-permute-start.4) | collective-permute-done | bytes 393248 | tf_op jit(solution)/shard_map/ppermute | solution.py:302
  58.4 8.3 %shard_map.110 = bf16[64,16,768]{2,1,0:T(8,128)(2,1)} custom-call(s32[1]{0:T(128)} %bitcast.place, bf16[16,12288]{1,0:T(8,128)(2,1)S(1)} %get-tuple-element.32.refs_0_, bf16[16,12288]{1,0:T(8,128)(2,1)S(1)} %collective-permute-done.3.refs_1_, bf16[16,12288]{1,0:T(8,128)(2,1)S(1)} %collective-permute-done.4.refs_2_, ...), custom_call_target="tpu_custom_call" | custom-call | flops 1073741824 | bytes 3145728 | tf_op jit(solution)/shard_map/pallas_call | solution.py:211
  69.0 10.1 %all-to-all-start.1 = ((bf16[64,16,768]{2,1,0:T(8,128)(2,1)}), bf16[64,16,768]{2,1,0:T(8,128)(2,1)S(1)}, u32[]{:S(2)}, u32[]{:S(2)}) async-start(bf16[64,16,768]{2,1,0:T(8,128)(2,1)} %shard_map.110), calls=%async_computation.1 | async-start | bytes 3145728 | tf_op jit(solution)/shard_map/all_to_all | solution.py:330
  82.9 35.8 %all-to-all-done.1 = bf16[64,16,768]{2,1,0:T(8,128)(2,1)S(1)} async-done(((bf16[64,16,768]{2,1,0:T(8,128)(2,1)}), bf16[64,16,768]{2,1,0:T(8,128)(2,1)S(1)}, u32[]{:S(2)}, u32[]{:S(2)}) %all-to-all-start.1) | async-done | bytes 1572896 | tf_op jit(solution)/shard_map/all_to_all | solution.py:330
  118.7 1.2 copy-done.13
  119.9 14.7 %spectral.1 = (bf16[1024,768]{1,0:T(8,128)(2,1)}, bf16[1440,768]{1,0:T(8,128)(2,1)}) custom-call(s32[1]{0:T(128)} %bitcast.1.flag, bf16[512,768]{1,0:T(8,128)(2,1)} %bitcast.6.refs_0_, bf16[1024,768]{1,0:T(8,128)(2,1)} %bitcast.58, bf16[1440,512]{1,0:T(8,128)(2,1)} %constant.53.clone.refs_2_, bf16[1440,1024]{1,0:T(8,128)(2,1)} %constant.54.clone.refs_3_, ...), custom_call_target="tpu_custom_call" | custom-call | flops 8999999488 | bytes 14000000 | tf_op jit(solution)/shard_map/spectral/pallas_call | solution.py:119
  134.5 6.4 %all-to-all-start.2 = ((bf16[64,16,768]{2,1,0:T(8,128)(2,1)}), bf16[64,16,768]{2,1,0:T(8,128)(2,1)S(1)}, u32[]{:S(2)}, u32[]{:S(2)}) async-start(bf16[64,16,768]{2,1,0:T(8,128)(2,1)} %bitcast.59), calls=%async_computation.2 | async-start | bytes 3145728 | tf_op jit(solution)/shard_map/all_to_all | solution.py:330
  141.0 3.5 %fusion = bf16[512,768]{0,1:T(8,128)(2,1)S(1)} fusion(bf16[1440,768]{1,0:T(8,128)(2,1)} %get-tuple-element.17, bf16[512,1440]{1,0:T(8,128)(2,1)} %constant.55.clone), kind=kOutput, calls=%fused_computation.5 | convolution fusion | flops 1132855296 | bytes 4472832 | tf_op jit(solution)/shard_map/dot_general | solution.py:346
  144.5 36.1 %all-to-all-done.2.back = bf16[64,16,768]{2,1,0:T(8,128)(2,1)S(1)} async-done(((bf16[64,16,768]{2,1,0:T(8,128)(2,1)}), bf16[64,16,768]{2,1,0:T(8,128)(2,1)S(1)}, u32[]{:S(2)}, u32[]{:S(2)}) %all-to-all-start.2) | async-done | bytes 1572896 | tf_op jit(solution)/shard_map/all_to_all | solution.py:330
  180.6 1.2 copy.12
  181.7 6.4 %all-to-all-start.3 = ((bf16[64,8,768]{2,1,0:T(8,128)(2,1)}), bf16[64,8,768]{2,1,0:T(8,128)(2,1)S(1)}, u32[]{:S(2)}, u32[]{:S(2)}) async-start(bf16[64,8,768]{2,1,0:T(8,128)(2,1)} %bitcast.57), calls=%async_computation.3 | async-start | bytes 1572864 | tf_op jit(solution)/shard_map/all_to_all | solution.py:330
  188.2 1.0 copy-done
  189.2 1.0 copy-done.7
  190.2 1.0 copy-done.9
  192.2 8.8 %shard_map.112 = (bf16[16,12288]{1,0:T(8,128)(2,1)S(1)}, bf16[16,12288]{1,0:T(8,128)(2,1)}, bf16[16,12288]{1,0:T(8,128)(2,1)}, bf16[16,12288]{1,0:T(8,128)(2,1)}) custom-call(s32[1]{0:T(128)} %bitcast.place, bf16[64,16,768]{2,1,0:T(8,128)(2,1)S(1)} %all-to-all-done.2.back, bf16[512,512]{1,0:T(8,128)(2,1)S(1)} %copy-done, ...), custom_call_target="tpu_custom_call" | custom-call | flops 1073741824 | bytes 3145728 | tf_op jit(solution)/shard_map/pallas_call | solution.py:211
  201.8 1.7 collective-permute-start.10
  203.6 7.5 %all-to-all-done.3.back = bf16[64,8,768]{2,1,0:T(8,128)(2,1)S(1)} async-done(((bf16[64,8,768]{2,1,0:T(8,128)(2,1)}), bf16[64,8,768]{2,1,0:T(8,128)(2,1)S(1)}, u32[]{:S(2)}, u32[]{:S(2)}) %all-to-all-start.3) | async-done | bytes 786464 | tf_op jit(solution)/shard_map/all_to_all | solution.py:330
  211.0 1.0 copy-done.1
  212.1 3.9 %shard_map.111 = (bf16[8,12288]{1,0:T(8,128)(2,1)S(1)}, bf16[8,12288]{1,0:T(8,128)(2,1)S(1)}, bf16[8,12288]{1,0:T(8,128)(2,1)S(1)}, bf16[8,12288]{1,0:T(8,128)(2,1)S(1)}) custom-call(s32[1]{0:T(128)} %bitcast.place, bf16[64,8,768]{2,1,0:T(8,128)(2,1)S(1)} %all-to-all-done.3.back, bf16[512,512]{1,0:T(8,128)(2,1)S(1)} %copy-done.1, ...), custom_call_target="tpu_custom_call" | custom-call | flops 536870912 | bytes 1572864 | tf_op jit(solution)/shard_map/pallas_call | solution.py:211
  218.0 6.4 %collective-permute-done.11.refs_7_ = bf16[16,12288]{1,0:T(8,128)(2,1)} collective-permute-done((bf16[16,12288]{1,0:T(8,128)(2,1)}, bf16[16,12288]{1,0:T(8,128)(2,1)}, u32[]{:S(2)}, u32[]{:S(2)}) %collective-permute-start.11) | collective-permute-done | bytes 393248 | tf_op jit(solution)/shard_map/ppermute | solution.py:302
  224.4 4.5 %collective-permute-done.7.refs_2_ = bf16[8,12288]{1,0:T(8,128)(2,1)S(1)} collective-permute-done((bf16[8,12288]{1,0:T(8,128)(2,1)S(1)}, bf16[8,12288]{1,0:T(8,128)(2,1)S(1)}, u32[]{:S(2)}, u32[]{:S(2)}) %collective-permute-start.7) | collective-permute-done | bytes 196640 | tf_op jit(solution)/shard_map/ppermute | solution.py:302
  228.9 3.8 %collective-permute-done.8.refs_3_ = bf16[8,12288]{1,0:T(8,128)(2,1)S(1)} collective-permute-done((bf16[8,12288]{1,0:T(8,128)(2,1)S(1)}, bf16[8,12288]{1,0:T(8,128)(2,1)S(1)}, u32[]{:S(2)}, u32[]{:S(2)}) %collective-permute-start.8) | collective-permute-done | bytes 196640 | tf_op jit(solution)/shard_map/ppermute | solution.py:302
  232.7 2.6 %assemble.1 = bf16[90,12288]{1,0:T(8,128)(2,1)} custom-call(s32[1]{0:T(128)} %bitcast.place, bf16[8,12288]{1,0:T(8,128)(2,1)S(1)} %get-tuple-element.20.refs_0_, bf16[8,12288]{1,0:T(8,128)(2,1)S(1)} %collective-permute-done.6.refs_1_, bf16[8,12288]{1,0:T(8,128)(2,1)S(1)} %collective-permute-done.7.refs_2_, ...), custom_call_target="tpu_custom_call" | custom-call | bytes 5000000 | tf_op jit(solution)/shard_map/assemble/pallas_call | solution.py:289
  (66 shorter events, 11.9 us)
Async XLA Ops:
  1.6 7.2 %collective-permute-start.2 = (bf16[8,12288]{1,0:T(8,128)(2,1)S(1)}, bf16[8,12288]{1,0:T(8,128)(2,1)S(1)}, u32[]{:S(2)}, u32[]{:S(2)}) collective-permute-start(bf16[8,12288]{1,0:T(8,128)(2,1)S(1)} %get-tuple-element.33), channel_id=1, source_target_pairs={{0,192},{64,128},{128,64},{192,0},{1,193},{65,129},{129,65},{193,1... | collective-permute-start | bytes 589832 | tf_op jit(solution)/shard_map/ppermute | solution.py:302
  2.7 10.4 %collective-permute-start.1 = (bf16[8,12288]{1,0:T(8,128)(2,1)S(1)}, bf16[8,12288]{1,0:T(8,128)(2,1)S(1)}, u32[]{:S(2)}, u32[]{:S(2)}) collective-permute-start(bf16[8,12288]{1,0:T(8,128)(2,1)S(1)} %get-tuple-element.34), channel_id=1, source_target_pairs={{0,128},{64,192},{128,0},{192,64},{1,129},{65,193},{129,1},{193,65... | collective-permute-start | bytes 589832 | tf_op jit(solution)/shard_map/ppermute | solution.py:302
  3.4 9.7 %collective-permute-start = (bf16[8,12288]{1,0:T(8,128)(2,1)S(1)}, bf16[8,12288]{1,0:T(8,128)(2,1)S(1)}, u32[]{:S(2)}, u32[]{:S(2)}) collective-permute-start(bf16[8,12288]{1,0:T(8,128)(2,1)S(1)} %get-tuple-element.35), channel_id=1, source_target_pairs={{0,64},{64,0},{128,192},{192,128},{1,65},{65,1},{129,193},{193,129... | collective-permute-start | bytes 589832 | tf_op jit(solution)/shard_map/ppermute | solution.py:302
  13.1 1.0 copy-start.2
  14.1 16.6 %copy-start.12 = (bf16[90,1,12288]{2,0,1:T(8,128)(2,1)S(1)}, bf16[90,1,12288]{2,0,1:T(8,128)(2,1)}, u32[]{:S(2)}) copy-start(bf16[90,1,12288]{2,0,1:T(8,128)(2,1)} %param.11) | copy-start | bytes 6635524
  18.8 50.3 %all-to-all-start = ((bf16[64,8,768]{2,1,0:T(8,128)(2,1)}), bf16[64,8,768]{2,1,0:T(8,128)(2,1)}, u32[]{:S(2)}, u32[]{:S(2)}) async-start(bf16[64,8,768]{2,1,0:T(8,128)(2,1)} %shard_map.109), calls=%async_computation | async-start | bytes 1572864 | tf_op jit(solution)/shard_map/all_to_all | solution.py:330
  30.7 27.7 %copy-start.3 = (bf16[512,512]{1,0:T(8,128)(2,1)S(1)}, bf16[512,512]{1,0:T(8,128)(2,1)}, u32[]{:S(2)}) copy-start(bf16[512,512]{1,0:T(8,128)(2,1)} %constant.57.clone.refs_4_) | copy-start | bytes 1572868
  31.1 16.0 %collective-permute-start.5 = (bf16[16,12288]{1,0:T(8,128)(2,1)S(1)}, bf16[16,12288]{1,0:T(8,128)(2,1)S(1)}, u32[]{:S(2)}, u32[]{:S(2)}) collective-permute-start(bf16[16,12288]{1,0:T(8,128)(2,1)S(1)} %get-tuple-element.29), channel_id=1, source_target_pairs={{0,192},{64,128},{128,64},{192,0},{1,193},{65,129},{129,65},{193,1... | collective-permute-start | bytes 1179656 | tf_op jit(solution)/shard_map/ppermute | solution.py:302
  32.6 14.5 %collective-permute-start.3 = (bf16[16,12288]{1,0:T(8,128)(2,1)S(1)}, bf16[16,12288]{1,0:T(8,128)(2,1)S(1)}, u32[]{:S(2)}, u32[]{:S(2)}) collective-permute-start(bf16[16,12288]{1,0:T(8,128)(2,1)S(1)} %get-tuple-element.30), channel_id=1, source_target_pairs={{0,64},{64,0},{128,192},{192,128},{1,65},{65,1},{129,193},{193,129... | collective-permute-start | bytes 1179656 | tf_op jit(solution)/shard_map/ppermute | solution.py:302
  32.8 25.6 %collective-permute-start.4 = (bf16[16,12288]{1,0:T(8,128)(2,1)S(1)}, bf16[16,12288]{1,0:T(8,128)(2,1)S(1)}, u32[]{:S(2)}, u32[]{:S(2)}) collective-permute-start(bf16[16,12288]{1,0:T(8,128)(2,1)S(1)} %get-tuple-element.31), channel_id=1, source_target_pairs={{0,128},{64,192},{128,0},{192,64},{1,129},{65,193},{129,1},{193,65... | collective-permute-start | bytes 1179656 | tf_op jit(solution)/shard_map/ppermute | solution.py:302
  67.5 0.8 copy-start.8
  68.2 0.8 copy-start.10
  69.0 10.1 %copy-start.16 = (f32[1,2,96]{2,1,0:T(2,128)S(1)}, f32[1,2,96]{2,1,0:T(2,128)}, u32[]{:S(2)}) copy-start(f32[1,2,96]{2,1,0:T(2,128)} %param.13) | copy-start | bytes 2308
  69.0 10.8 %copy-start.15 = (bf16[1,2,96,96]{3,2,1,0:T(8,128)(2,1)S(1)}, bf16[1,2,96,96]{3,2,1,0:T(8,128)(2,1)}, u32[]{:S(2)}) copy-start(bf16[1,2,96,96]{3,2,1,0:T(8,128)(2,1)} %param.14) | copy-start | bytes 110596
  69.0 10.9 %copy-start.17 = (f32[1,2,96]{2,1,0:T(2,128)S(1)}, f32[1,2,96]{2,1,0:T(2,128)}, u32[]{:S(2)}) copy-start(f32[1,2,96]{2,1,0:T(2,128)} %param.15) | copy-start | bytes 2308
  69.0 11.5 %copy-start.14 = (bf16[1,2,96,96]{3,2,1,0:T(8,128)(2,1)S(1)}, bf16[1,2,96,96]{3,2,1,0:T(8,128)(2,1)}, u32[]{:S(2)}) copy-start(bf16[1,2,96,96]{3,2,1,0:T(8,128)(2,1)} %param.12) | copy-start | bytes 110596
  69.0 49.7 %all-to-all-start.1 = ((bf16[64,16,768]{2,1,0:T(8,128)(2,1)}), bf16[64,16,768]{2,1,0:T(8,128)(2,1)S(1)}, u32[]{:S(2)}, u32[]{:S(2)}) async-start(bf16[64,16,768]{2,1,0:T(8,128)(2,1)} %shard_map.110), calls=%async_computation.1 | async-start | bytes 3145728 | tf_op jit(solution)/shard_map/all_to_all | solution.py:330
  118.7 1.2 copy-start.13
  134.5 46.0 %all-to-all-start.2 = ((bf16[64,16,768]{2,1,0:T(8,128)(2,1)}), bf16[64,16,768]{2,1,0:T(8,128)(2,1)S(1)}, u32[]{:S(2)}, u32[]{:S(2)}) async-start(bf16[64,16,768]{2,1,0:T(8,128)(2,1)} %bitcast.59), calls=%async_computation.2 | async-start | bytes 3145728 | tf_op jit(solution)/shard_map/all_to_all | solution.py:330
  181.7 29.3 %all-to-all-start.3 = ((bf16[64,8,768]{2,1,0:T(8,128)(2,1)}), bf16[64,8,768]{2,1,0:T(8,128)(2,1)S(1)}, u32[]{:S(2)}, u32[]{:S(2)}) async-start(bf16[64,8,768]{2,1,0:T(8,128)(2,1)} %bitcast.57), calls=%async_computation.3 | async-start | bytes 1572864 | tf_op jit(solution)/shard_map/all_to_all | solution.py:330
  188.2 1.0 copy-start
  189.2 1.0 copy-start.7
  190.2 1.0 copy-start.9
  191.2 1.0 copy-start.11
  201.7 15.6 %collective-permute-start.9 = (bf16[16,12288]{1,0:T(8,128)(2,1)}, bf16[16,12288]{1,0:T(8,128)(2,1)S(1)}, u32[]{:S(2)}, u32[]{:S(2)}) collective-permute-start(bf16[16,12288]{1,0:T(8,128)(2,1)} %get-tuple-element.26), channel_id=1, source_target_pairs={{0,64},{64,0},{128,192},{192,128},{1,65},{65,1},{129,193},{193,129... | collective-permute-start | bytes 1179656 | tf_op jit(solution)/shard_map/ppermute | solution.py:302
  201.8 16.2 %collective-permute-start.10 = (bf16[16,12288]{1,0:T(8,128)(2,1)}, bf16[16,12288]{1,0:T(8,128)(2,1)S(1)}, u32[]{:S(2)}, u32[]{:S(2)}) collective-permute-start(bf16[16,12288]{1,0:T(8,128)(2,1)} %get-tuple-element.27), channel_id=1, source_target_pairs={{0,128},{64,192},{128,0},{192,64},{1,129},{65,193},{129,1},{193,65... | collective-permute-start | bytes 1179656 | tf_op jit(solution)/shard_map/ppermute | solution.py:302
  203.5 20.9 %collective-permute-start.11 = (bf16[16,12288]{1,0:T(8,128)(2,1)}, bf16[16,12288]{1,0:T(8,128)(2,1)}, u32[]{:S(2)}, u32[]{:S(2)}) collective-permute-start(bf16[16,12288]{1,0:T(8,128)(2,1)} %get-tuple-element.28), channel_id=1, source_target_pairs={{0,192},{64,128},{128,64},{192,0},{1,193},{65,129},{129,65},{193,1... | collective-permute-start | bytes 1179656 | tf_op jit(solution)/shard_map/ppermute | solution.py:302
  211.0 1.0 copy-start.1
  212.1 20.6 %copy-start.5 = (bf16[16,12288]{1,0:T(8,128)(2,1)S(1)}, bf16[16,12288]{1,0:T(8,128)(2,1)}, u32[]{:S(2)}) copy-start(bf16[16,12288]{1,0:T(8,128)(2,1)} %copy-done.4) | copy-start | bytes 1179652
  215.9 8.5 %collective-permute-start.6 = (bf16[8,12288]{1,0:T(8,128)(2,1)S(1)}, bf16[8,12288]{1,0:T(8,128)(2,1)S(1)}, u32[]{:S(2)}, u32[]{:S(2)}) collective-permute-start(bf16[8,12288]{1,0:T(8,128)(2,1)S(1)} %get-tuple-element.21), channel_id=1, source_target_pairs={{0,64},{64,0},{128,192},{192,128},{1,65},{65,1},{129,193},{193,129... | collective-permute-start | bytes 589832 | tf_op jit(solution)/shard_map/ppermute | solution.py:302
  216.5 12.4 %collective-permute-start.7 = (bf16[8,12288]{1,0:T(8,128)(2,1)S(1)}, bf16[8,12288]{1,0:T(8,128)(2,1)S(1)}, u32[]{:S(2)}, u32[]{:S(2)}) collective-permute-start(bf16[8,12288]{1,0:T(8,128)(2,1)S(1)} %get-tuple-element.22), channel_id=1, source_target_pairs={{0,128},{64,192},{128,0},{192,64},{1,129},{65,193},{129,1},{193,65... | collective-permute-start | bytes 589832 | tf_op jit(solution)/shard_map/ppermute | solution.py:302
  217.3 15.4 %collective-permute-start.8 = (bf16[8,12288]{1,0:T(8,128)(2,1)S(1)}, bf16[8,12288]{1,0:T(8,128)(2,1)S(1)}, u32[]{:S(2)}, u32[]{:S(2)}) collective-permute-start(bf16[8,12288]{1,0:T(8,128)(2,1)S(1)} %get-tuple-element.23), channel_id=1, source_target_pairs={{0,192},{64,128},{128,64},{192,0},{1,193},{65,129},{129,65},{193,1... | collective-permute-start | bytes 589832 | tf_op jit(solution)/shard_map/ppermute | solution.py:302
  (2 other events, 1.5 us)

commit v3 on v2

--- a/solution.py
+++ b/solution.py
@@ -12,6 +12,7 @@
 
 shrink_level = 0.01
 group = ("lat", "lon")
+LIMITS = (40, 62)
 
 
 def phases(left, right, length):
@@ -113,6 +114,25 @@
     out[...] = jnp.dot(inv[...], y[...], preferred_element_type=jnp.float32).astype(out.dtype)
 
 
+def unwind_kernel(inv, y, out):
+    out[...] = jnp.dot(inv[...], y[...], preferred_element_type=jnp.float32).astype(out.dtype)
+
+
+def unwind(inv, y):
+    whole = pl.BlockSpec(memory_space=pltpu.VMEM)
+    return pl.pallas_call(
+        unwind_kernel,
+        out_shape=jax.ShapeDtypeStruct((inv.shape[0], y.shape[1]), jnp.bfloat16),
+        in_specs=[whole] * 2,
+        out_specs=whole,
+        compiler_params=pltpu.CompilerParams(vmem_limit_bytes=62 * 2**20),
+        cost_estimate=pl.CostEstimate(
+            flops=10**9, bytes_accessed=4 * 10**6, transcendentals=0
+        ),
+        name="unwind",
+    )(inv, y)
+
+
 def spectral(flag, xs, fwds, inv, w1, b1, w2, b2):
     whole = pl.BlockSpec(memory_space=pltpu.VMEM)
     rows, cols = fwds[0].shape[0], xs[0].shape[1]
@@ -159,15 +179,16 @@
     size = table.shape[0]
     span = 4 * width
     local = size // len(fields)
-    for m, field in enumerate(fields):
-        base = (place[0] ^ m) * (8 * local)
-
-        def step(g, carry, field=field, base=base):
-            group = field[:, pl.ds(pl.multiple_of(g * span, 128), span)].astype(jnp.float32)
-            spread(source, pl.multiple_of(base + g * 32, 8), group, width)
-            return carry
-
-        lax.fori_loop(0, local // 4, step, 0, unroll=8)
+    bases = [(place[0] ^ m) * (8 * local) for m in range(len(fields))]
+
+    def step(g, carry):
+        lanes = pl.ds(pl.multiple_of(g * span, 128), span)
+        for field, base in zip(fields, bases):
+            start = pl.multiple_of(base + g * 32, 8)
+            spread(source, start, field[:, lanes].astype(jnp.float32), width)
+        return carry
+
+    lax.fori_loop(0, local // 4, step, 0, unroll=8)
     transform(table, source, target, size)
     per = out.shape[2] // span
 
@@ -177,7 +198,7 @@
             out[d, :, pl.ds(p * span, span)] = gather(target, start, 4, width).astype(out.dtype)
         return carry
 
-    lax.fori_loop(0, out.shape[0], finish, 0, unroll=4)
+    lax.fori_loop(0, out.shape[0], finish, 0, unroll=16)
 
 
 def lat_inverse_kernel(place, back, table, *refs, width, count):
@@ -193,21 +214,21 @@
             spread(source, start, back[d, :, pl.ds(p * span, span)].astype(jnp.float32), width)
         return carry
 
-    lax.fori_loop(0, back.shape[0], begin, 0, unroll=4)
+    lax.fori_loop(0, back.shape[0], begin, 0, unroll=16)
     transform(table, source, target, size)
-    for m, (field, out) in enumerate(zip(fields, outs)):
-        base = (place[0] ^ m) * (8 * local)
-
-        def step(g, carry, field=field, out=out, base=base):
-            lanes = pl.ds(pl.multiple_of(g * span, 128), span)
+    bases = [(place[0] ^ m) * (8 * local) for m in range(count)]
+
+    def step(g, carry):
+        lanes = pl.ds(pl.multiple_of(g * span, 128), span)
+        for field, out, base in zip(fields, outs, bases):
             sums = gather(target, pl.multiple_of(base + g * 32, 8), 4, width)
             out[:, lanes] = (sums + field[:, lanes].astype(jnp.float32)).astype(out.dtype)
-            return carry
-
-        lax.fori_loop(0, local // 4, step, 0, unroll=8)
-
-
-def lat_call(kernel, args, in_specs, out_shape, out_specs, rows, size, moved):
+        return carry
+
+    lax.fori_loop(0, local // 4, step, 0, unroll=8)
+
+
+def lat_call(kernel, args, in_specs, out_shape, out_specs, rows, size, moved, limit=40):
     return pl.pallas_call(
         kernel,
         grid=(rows // 8,),
@@ -215,7 +236,7 @@
         in_specs=[pl.BlockSpec(memory_space=pltpu.SMEM)] + in_specs,
         out_specs=out_specs,
         scratch_shapes=[pltpu.VMEM((8 * size, 128), jnp.float32)] * 2,
-        compiler_params=pltpu.CompilerParams(vmem_limit_bytes=40 * 2**20),
+        compiler_params=pltpu.CompilerParams(vmem_limit_bytes=limit * 2**20),
         cost_estimate=pl.CostEstimate(
             flops=2 * rows * size * size * 128, bytes_accessed=2 * moved, transcendentals=0
         ),
@@ -239,8 +260,8 @@
     )
 
 
-def lat_inverse(place, back, table, fields, width):
-    everyone, rows, lanes = back.shape
+def lat_inverse(place, back, table, fields, width, tile, limit):
+    everyone, _, lanes = back.shape
     size = table.shape[0]
     merged = fields[0].shape[1]
     strip = pl.BlockSpec((8, merged), lambda n: (n, 0))
@@ -248,21 +269,22 @@
         functools.partial(lat_inverse_kernel, width=width, count=len(fields)),
         (place, back, table, *fields),
         [
-            pl.BlockSpec((everyone, 8, lanes), lambda n: (0, n, 0)),
+            pl.BlockSpec((everyone, 8, lanes), lambda n: (0, n + tile, 0)),
             pl.BlockSpec((size, size), lambda n: (0, 0)),
         ]
-        + [strip] * len(fields),
-        [jax.ShapeDtypeStruct((rows, merged), jnp.bfloat16)] * len(fields),
+        + [pl.BlockSpec((8, merged), lambda n: (n + tile, 0))] * len(fields),
+        [jax.ShapeDtypeStruct((8, merged), jnp.bfloat16)] * len(fields),
         [strip] * len(fields),
-        rows,
+        8,
         size,
-        rows * size * width * 2,
-    )
-
-
-def assemble_kernel(place, *refs, chunks, count):
+        8 * size * width * 2,
+        limit,
+    )
+
+
+def assemble_kernel(place, *refs, chunks, rows, count):
     pieces, out = refs[:-1], refs[-1]
-    rows, length = chunks[-1][1], out.shape[0]
+    length = out.shape[0]
     for n, (start, stop) in enumerate(chunks):
         for m in range(count):
             piece = pieces[n * count + m]
@@ -283,18 +305,45 @@
                     out[pl.ds(length - rest, rest), :] = piece[pl.ds(0, rest), :]
 
 
-def assemble(place, mixed, chunks, length):
-    whole = pl.BlockSpec(memory_space=pltpu.VMEM)
-    pieces = [piece for chunk in mixed for piece in chunk]
-    return pl.pallas_call(
-        functools.partial(assemble_kernel, chunks=chunks, count=len(mixed[0])),
-        out_shape=jax.ShapeDtypeStruct((length, pieces[0].shape[1]), jnp.bfloat16),
-        in_specs=[pl.BlockSpec(memory_space=pltpu.SMEM)] + [whole] * len(pieces),
+def insert_kernel(place, *refs, start, rows, count):
+    pieces, out, sems = refs[:count], refs[-2], refs[-1]
+    copies = []
+    for m in range(count):
+        row = pl.multiple_of((place[0] ^ m) * rows + start, 8)
+        copies.append(
+            pltpu.make_async_copy(pieces[m], out.at[pl.ds(row, pieces[m].shape[0])], sems.at[m])
+        )
+        copies[-1].start()
+    for copy in copies:
+        copy.wait()
+
+
+def assemble(place, mixed, chunks, rows, length):
+    whole, away = pl.BlockSpec(memory_space=pltpu.VMEM), pl.BlockSpec(memory_space=pl.ANY)
+    scalar = pl.BlockSpec(memory_space=pltpu.SMEM)
+    pieces = [piece for chunk in mixed[:-1] for piece in chunk]
+    count = len(mixed[0])
+    shape = jax.ShapeDtypeStruct((length, pieces[0].shape[1]), jnp.bfloat16)
+    most = pl.pallas_call(
+        functools.partial(assemble_kernel, chunks=chunks[:-1], rows=rows, count=count),
+        out_shape=shape,
+        in_specs=[scalar] + [whole] * len(pieces),
         out_specs=whole,
         compiler_params=pltpu.CompilerParams(vmem_limit_bytes=16 * 2**20),
         cost_estimate=pl.CostEstimate(flops=0, bytes_accessed=5 * 10**6, transcendentals=0),
         name="assemble",
     )(place, *pieces)
+    return pl.pallas_call(
+        functools.partial(insert_kernel, start=chunks[-1][0], rows=rows, count=count),
+        out_shape=shape,
+        in_specs=[scalar] + [whole] * count + [away],
+        out_specs=away,
+        input_output_aliases={1 + count: 0},
+        scratch_shapes=[pltpu.SemaphoreType.DMA((count,))],
+        compiler_params=pltpu.CompilerParams(vmem_limit_bytes=16 * 2**20),
+        cost_estimate=pl.CostEstimate(flops=0, bytes_accessed=2 * 10**6, transcendentals=0),
+        name="insert",
+    )(place, *mixed[-1], most)
 
 
 def swap(pieces, count):
@@ -343,17 +392,22 @@
         xs[n] = exchange(xs[n])
     last, y = spectral(flag, [flat(x) for x in xs], fwds, invs[1], w1, b1, w2, b2)
     outs = [None, last]
-    outs[0] = jnp.dot(invs[0], y, preferred_element_type=jnp.float32).astype(jnp.bfloat16)
-    mixed, backs = [None, None], [None, None]
+    outs[0] = unwind(invs[0], y)
+    backs = [None, None]
     for n in (1, 0):
         if n == 0:
             outs[0], backs[1] = lax.optimization_barrier((outs[0], backs[1]))
         backs[n] = exchange(outs[n].reshape(everyone, chunks[n][1] - chunks[n][0], -1))
+    strips, mixed = [], []
     for n in (1, 0):
         start, stop = chunks[n]
-        pieces = lat_inverse(place, backs[n], lat_back, fields[n], width)
-        mixed[n] = swap(pieces, lat_n)
-    return assemble(place, mixed, chunks, local_lon)[:, None, :]
+        for first in range(start, stop, 8):
+            pieces = lat_inverse(
+                place, backs[n], lat_back, fields[n], width, (first - start) // 8, LIMITS[n]
+            )
+            mixed.append(swap(pieces, lat_n))
+            strips.append((first, first + 8))
+    return assemble(place, mixed, strips, rows, local_lon)[:, None, :]
 
 
 def solution(mesh):

time: 238 us -> 226 us (0.950)
  waiting for transfers between devices: 129 us -> 123 us
  local copies, waits for them, and re-layouts: 14.1 us -> 8.59 us
  matrix products: 3.52 us -> 0 us
  starting transfers between devices: 43 us -> 46.3 us
    ppermute x12 -> x15, waiting for transfers between devices: 49.4 us -> 42.5 us  [swap(): lax.ppermute(pieces[m], 'lat', [(i, i ^ m) for i in range(count)])]
    pallas_call x4 -> x5, Pallas kernels: 25.6 us -> 19.2 us  [lat_call(): pl.pallas_call(kernel, grid=(rows // 8,), out_shape=out_shape, in_specs=[...]
    pallas_call x1 -> x3, Pallas kernels: 2.6 us -> 7.95 us  [the longest x1 4.38 us: unwind(): pl.pallas_call(unwind_kernel, out_shape=jax.ShapeDtypeStruct((inv.shape[0...]
    unnamed x36 -> x42, local copies, waits for them, and re-layouts: 10.3 us -> 5.94 us
    dot_general x1 -> x0, matrix products: 3.52 us -> none  [layer(): jnp.dot(invs[0], y, preferred_element_type=jnp.float32).astype(jnp.bfloat16)]
    ppermute x12 -> x15, starting transfers between devices: 8.08 us -> 11.3 us  [swap(): lax.ppermute(pieces[m], 'lat', [(i, i ^ m) for i in range(count)])]
  transfers between devices with their start and end apart: 16 -> 19, of which waited for: 10 -> 10; matrix products, arithmetic and copies ran while one was open for 3% -> 2% of each run, Pallas kernels for 9% -> 10%
where the time goes in v3:
time: 226 us; the launch traced here: 223 us
  waiting for transfers between devices  123 us (54%)
  starting transfers between devices  46.3 us (20%)
  Pallas kernels  41.8 us (18%)
  local copies, waits for them, and re-layouts  8.59 us (4%)
  other arithmetic  2.97 us (1%)
    all_to_all x4, waiting for transfers between devices, layer(): lax.all_to_all(x, group, split_axis=0, concat_axis=0, tiled=True)  80.3 us
    ppermute x15, waiting for transfers between devices, swap(): lax.ppermute(pieces[m], 'lat', [(i, i ^ m) for i in range(count)])  42.5 us
    all_to_all x4, starting transfers between devices, layer(): lax.all_to_all(x, group, split_axis=0, concat_axis=0, tiled=True)  35.1 us
    pallas_call x5, Pallas kernels, lat_call(): pl.pallas_call(kernel, grid=(rows // 8,), out_shape=out_shape, in_specs=[...  19.2 us
    pallas_call x1, Pallas kernels, spectral(): pl.pallas_call(functools.partial(spectral_kernel, chunks=len(xs)), out_sh...  14.6 us
    ppermute x15, starting transfers between devices, swap(): lax.ppermute(pieces[m], 'lat', [(i, i ^ m) for i in range(count)])  11.3 us
    unnamed x42, local copies, waits for them, and re-layouts  5.94 us
  transfers between devices with their start and end apart: 19, of which 10 were waited for; matrix products, arithmetic and copies ran while one was open for 2% of the time, Pallas kernels for 10%

profile of v3, /device:TPU:38, one launch (start us, length us, event | category | flops | bytes accessed | tf_op | source)
XLA Modules:
  0.0 223.0 jit_solution(15102978007495647100)
XLA Ops:
  0.0 1.6 dynamic-slice_bitcast_fusion
  1.6 1.1 collective-permute-start.2
  3.5 5.2 %collective-permute-done.2.refs_3_ = bf16[8,12288]{1,0:T(8,128)(2,1)S(1)} collective-permute-done((bf16[8,12288]{1,0:T(8,128)(2,1)S(1)}, bf16[8,12288]{1,0:T(8,128)(2,1)S(1)}, u32[]{:S(2)}, u32[]{:S(2)}) %collective-permute-start.2) | collective-permute-done | bytes 196640 | tf_op jit(solution)/shard_map/ppermute | solution.py:351
  8.7 4.3 %collective-permute-done.1.refs_2_ = bf16[8,12288]{1,0:T(8,128)(2,1)S(1)} collective-permute-done((bf16[8,12288]{1,0:T(8,128)(2,1)S(1)}, bf16[8,12288]{1,0:T(8,128)(2,1)S(1)}, u32[]{:S(2)}, u32[]{:S(2)}) %collective-permute-start.1) | collective-permute-done | bytes 196640 | tf_op jit(solution)/shard_map/ppermute | solution.py:351
  13.1 1.2 copy-done.11
  14.3 2.9 %shard_map.109 = bf16[64,8,768]{2,1,0:T(8,128)(2,1)} custom-call(s32[1]{0:T(128)} %bitcast.place, bf16[8,12288]{1,0:T(8,128)(2,1)S(1)} %get-tuple-element.44.refs_0_, bf16[8,12288]{1,0:T(8,128)(2,1)S(1)} %collective-permute-done.refs_1_, bf16[8,12288]{1,0:T(8,128)(2,1)S(1)} %collective-permute-done.1.refs_2_, ...), custom_call_target="tpu_custom_call" | custom-call | flops 536870912 | bytes 1572864 | tf_op jit(solution)/shard_map/pallas_call | solution.py:232
  17.2 11.9 %all-to-all-start = ((bf16[64,8,768]{2,1,0:T(8,128)(2,1)}), bf16[64,8,768]{2,1,0:T(8,128)(2,1)}, u32[]{:S(2)}, u32[]{:S(2)}) async-start(bf16[64,8,768]{2,1,0:T(8,128)(2,1)} %shard_map.109), calls=%async_computation | async-start | bytes 1572864 | tf_op jit(solution)/shard_map/all_to_all | solution.py:379
  29.5 1.5 collective-permute-start.5
  31.8 13.7 %collective-permute-done.5.refs_3_ = bf16[16,12288]{1,0:T(8,128)(2,1)S(1)} collective-permute-done((bf16[16,12288]{1,0:T(8,128)(2,1)S(1)}, bf16[16,12288]{1,0:T(8,128)(2,1)S(1)}, u32[]{:S(2)}, u32[]{:S(2)}) %collective-permute-start.5) | collective-permute-done | bytes 393248 | tf_op jit(solution)/shard_map/ppermute | solution.py:351
  45.5 11.3 %collective-permute-done.4.refs_2_ = bf16[16,12288]{1,0:T(8,128)(2,1)S(1)} collective-permute-done((bf16[16,12288]{1,0:T(8,128)(2,1)S(1)}, bf16[16,12288]{1,0:T(8,128)(2,1)S(1)}, u32[]{:S(2)}, u32[]{:S(2)}) %collective-permute-start.4) | collective-permute-done | bytes 393248 | tf_op jit(solution)/shard_map/ppermute | solution.py:351
  56.8 4.9 %shard_map.110 = bf16[64,16,768]{2,1,0:T(8,128)(2,1)} custom-call(s32[1]{0:T(128)} %bitcast.place, bf16[16,12288]{1,0:T(8,128)(2,1)S(1)} %get-tuple-element.40.refs_0_, bf16[16,12288]{1,0:T(8,128)(2,1)S(1)} %collective-permute-done.3.refs_1_, bf16[16,12288]{1,0:T(8,128)(2,1)S(1)} %collective-permute-done.4.refs_2_, ...), custom_call_target="tpu_custom_call" | custom-call | flops 1073741824 | bytes 3145728 | tf_op jit(solution)/shard_map/pallas_call | solution.py:232
  62.6 10.1 %all-to-all-start.1 = ((bf16[64,16,768]{2,1,0:T(8,128)(2,1)}), bf16[64,16,768]{2,1,0:T(8,128)(2,1)S(1)}, u32[]{:S(2)}, u32[]{:S(2)}) async-start(bf16[64,16,768]{2,1,0:T(8,128)(2,1)} %shard_map.110), calls=%async_computation.1 | async-start | bytes 3145728 | tf_op jit(solution)/shard_map/all_to_all | solution.py:379
  76.5 35.7 %all-to-all-done.1 = bf16[64,16,768]{2,1,0:T(8,128)(2,1)S(1)} async-done(((bf16[64,16,768]{2,1,0:T(8,128)(2,1)}), bf16[64,16,768]{2,1,0:T(8,128)(2,1)S(1)}, u32[]{:S(2)}, u32[]{:S(2)}) %all-to-all-start.1) | async-done | bytes 1572896 | tf_op jit(solution)/shard_map/all_to_all | solution.py:379
  112.2 1.2 copy-done.16
  113.4 14.6 %spectral.1 = (bf16[1024,768]{1,0:T(8,128)(2,1)}, bf16[1440,768]{1,0:T(8,128)(2,1)}) custom-call(s32[1]{0:T(128)} %bitcast.1.flag, bf16[512,768]{1,0:T(8,128)(2,1)} %bitcast.6.refs_0_, bf16[1024,768]{1,0:T(8,128)(2,1)} %bitcast.54, bf16[1440,512]{1,0:T(8,128)(2,1)} %constant.53.clone.refs_2_, bf16[1440,1024]{1,0:T(8,128)(2,1)} %constant.54.clone.refs_3_, ...), custom_call_target="tpu_custom_call" | custom-call | flops 8999999488 | bytes 14000000 | tf_op jit(solution)/shard_map/spectral/pallas_call | solution.py:139
  128.0 6.6 %all-to-all-start.2 = ((bf16[64,16,768]{2,1,0:T(8,128)(2,1)}), bf16[64,16,768]{2,1,0:T(8,128)(2,1)}, u32[]{:S(2)}, u32[]{:S(2)}) async-start(bf16[64,16,768]{2,1,0:T(8,128)(2,1)} %bitcast.55), calls=%async_computation.2 | async-start | bytes 3145728 | tf_op jit(solution)/shard_map/all_to_all | solution.py:379
  134.7 4.4 %unwind.1 = bf16[512,768]{1,0:T(8,128)(2,1)} custom-call(bf16[512,1440]{1,0:T(8,128)(2,1)} %constant.55.clone.inv, bf16[1440,768]{1,0:T(8,128)(2,1)} %get-tuple-element.21.y), custom_call_target="tpu_custom_call" | custom-call | flops 1000000000 | bytes 4000000 | tf_op jit(solution)/shard_map/unwind/pallas_call | solution.py:123
  139.0 35.1 %all-to-all-done.2.back = bf16[64,16,768]{2,1,0:T(8,128)(2,1)} async-done(((bf16[64,16,768]{2,1,0:T(8,128)(2,1)}), bf16[64,16,768]{2,1,0:T(8,128)(2,1)}, u32[]{:S(2)}, u32[]{:S(2)}) %all-to-all-start.2) | async-done | bytes 1572896 | tf_op jit(solution)/shard_map/all_to_all | solution.py:379
  174.2 6.4 %all-to-all-start.3 = ((bf16[64,8,768]{2,1,0:T(8,128)(2,1)}), bf16[64,8,768]{2,1,0:T(8,128)(2,1)S(1)}, u32[]{:S(2)}, u32[]{:S(2)}) async-start(bf16[64,8,768]{2,1,0:T(8,128)(2,1)} %bitcast.53), calls=%async_computation.3 | async-start | bytes 1572864 | tf_op jit(solution)/shard_map/all_to_all | solution.py:379
  180.6 4.6 %shard_map.113 = (bf16[8,12288]{1,0:T(8,128)(2,1)}, bf16[8,12288]{1,0:T(8,128)(2,1)}, bf16[8,12288]{1,0:T(8,128)(2,1)}, bf16[8,12288]{1,0:T(8,128)(2,1)}) custom-call(s32[1]{0:T(128)} %bitcast.place, bf16[64,16,768]{2,1,0:T(8,128)(2,1)} %all-to-all-done.2.back, bf16[512,512]{1,0:T(8,128)(2,1)} %constant.58.clone.table, bf16[16,12288]{1,0:T(8,128)(2,1)} %copy-done.1, ...), custom_call_target="tpu_custom_call" | custom-call | flops 536870912 | bytes 1572864 | tf_op jit(solution)/shard_map/pallas_call | solution.py:232
  185.7 1.7 collective-permute-start.13
  187.4 4.6 %shard_map.112 = (bf16[8,12288]{1,0:T(8,128)(2,1)}, bf16[8,12288]{1,0:T(8,128)(2,1)}, bf16[8,12288]{1,0:T(8,128)(2,1)}, bf16[8,12288]{1,0:T(8,128)(2,1)}) custom-call(s32[1]{0:T(128)} %bitcast.place, bf16[64,16,768]{2,1,0:T(8,128)(2,1)} %all-to-all-done.2.back, bf16[512,512]{1,0:T(8,128)(2,1)} %constant.58.clone.table, bf16[16,12288]{1,0:T(8,128)(2,1)} %copy-done.1, ...), custom_call_target="tpu_custom_call" | custom-call | flops 536870912 | bytes 1572864 | tf_op jit(solution)/shard_map/pallas_call | solution.py:232
  192.4 1.7 collective-permute-start.10
  194.0 9.4 %all-to-all-done.3.back = bf16[64,8,768]{2,1,0:T(8,128)(2,1)S(1)} async-done(((bf16[64,8,768]{2,1,0:T(8,128)(2,1)}), bf16[64,8,768]{2,1,0:T(8,128)(2,1)S(1)}, u32[]{:S(2)}, u32[]{:S(2)}) %all-to-all-start.3) | async-done | bytes 786464 | tf_op jit(solution)/shard_map/all_to_all | solution.py:379
  204.4 2.2 shard_map.111
  206.6 1.0 collective-permute-start.11
  207.7 1.3 collective-permute-start.7
  209.5 3.9 %collective-permute-done.11.refs_3_ = bf16[8,12288]{1,0:T(8,128)(2,1)S(1)} collective-permute-done((bf16[8,12288]{1,0:T(8,128)(2,1)}, bf16[8,12288]{1,0:T(8,128)(2,1)S(1)}, u32[]{:S(2)}, u32[]{:S(2)}) %collective-permute-start.11) | collective-permute-done | bytes 196640 | tf_op jit(solution)/shard_map/ppermute | solution.py:351
  213.5 0.9 copy-done.13
  215.3 2.7 %assemble.1.refs_4_ = bf16[90,12288]{1,0:T(8,128)(2,1)} custom-call(s32[1]{0:T(128)} %bitcast.place, bf16[8,12288]{1,0:T(8,128)(2,1)S(1)} %copy-done.14, bf16[8,12288]{1,0:T(8,128)(2,1)S(1)} %collective-permute-done.9.refs_1_, bf16[8,12288]{1,0:T(8,128)(2,1)S(1)} %collective-permute-done.10.refs_2_, bf16[8,12288]{1,0:T(8,128)(2,1)S(1)} %collective-permute-done.11.refs_3_, ...), custom_call_target="tpu_custom_call" | custom-call | bytes 5000000 | tf_op jit(solution)/shard_map/assemble/pallas_call | solution.py:327
  218.0 1.1 collective-permute-done.7.refs_2_
  219.0 2.8 %collective-permute-done.8.refs_3_ = bf16[8,12288]{1,0:T(8,128)(2,1)S(1)} collective-permute-done((bf16[8,12288]{1,0:T(8,128)(2,1)S(1)}, bf16[8,12288]{1,0:T(8,128)(2,1)S(1)}, u32[]{:S(2)}, u32[]{:S(2)}) %collective-permute-start.8) | collective-permute-done | bytes 196640 | tf_op jit(solution)/shard_map/ppermute | solution.py:351
  (79 shorter events, 10.7 us)
Async XLA Ops:
  1.6 7.2 %collective-permute-start.2 = (bf16[8,12288]{1,0:T(8,128)(2,1)S(1)}, bf16[8,12288]{1,0:T(8,128)(2,1)S(1)}, u32[]{:S(2)}, u32[]{:S(2)}) collective-permute-start(bf16[8,12288]{1,0:T(8,128)(2,1)S(1)} %get-tuple-element.41), channel_id=1, source_target_pairs={{0,192},{64,128},{128,64},{192,0},{1,193},{65,129},{129,65},{193,1... | collective-permute-start | bytes 589832 | tf_op jit(solution)/shard_map/ppermute | solution.py:351
  2.7 10.4 %collective-permute-start.1 = (bf16[8,12288]{1,0:T(8,128)(2,1)S(1)}, bf16[8,12288]{1,0:T(8,128)(2,1)S(1)}, u32[]{:S(2)}, u32[]{:S(2)}) collective-permute-start(bf16[8,12288]{1,0:T(8,128)(2,1)S(1)} %get-tuple-element.42), channel_id=1, source_target_pairs={{0,128},{64,192},{128,0},{192,64},{1,129},{65,193},{129,1},{193,65... | collective-permute-start | bytes 589832 | tf_op jit(solution)/shard_map/ppermute | solution.py:351
  3.4 9.7 %collective-permute-start = (bf16[8,12288]{1,0:T(8,128)(2,1)S(1)}, bf16[8,12288]{1,0:T(8,128)(2,1)S(1)}, u32[]{:S(2)}, u32[]{:S(2)}) collective-permute-start(bf16[8,12288]{1,0:T(8,128)(2,1)S(1)} %get-tuple-element.43), channel_id=1, source_target_pairs={{0,64},{64,0},{128,192},{192,128},{1,65},{65,1},{129,193},{193,129... | collective-permute-start | bytes 589832 | tf_op jit(solution)/shard_map/ppermute | solution.py:351
  8.7 20.7 %copy-start.5 = (bf16[8,12288]{1,0:T(8,128)(2,1)}, bf16[8,12288]{1,0:T(8,128)(2,1)S(1)}, u32[]{:S(2)}) copy-start(bf16[8,12288]{1,0:T(8,128)(2,1)S(1)} %collective-permute-done.2.refs_3_) | copy-start | bytes 589828
  13.1 16.4 %copy-start.7 = (bf16[8,12288]{1,0:T(8,128)(2,1)}, bf16[8,12288]{1,0:T(8,128)(2,1)S(1)}, u32[]{:S(2)}) copy-start(bf16[8,12288]{1,0:T(8,128)(2,1)S(1)} %collective-permute-done.1.refs_2_) | copy-start | bytes 589828
  13.1 16.4 %copy-start.9 = (bf16[8,12288]{1,0:T(8,128)(2,1)}, bf16[8,12288]{1,0:T(8,128)(2,1)S(1)}, u32[]{:S(2)}) copy-start(bf16[8,12288]{1,0:T(8,128)(2,1)S(1)} %collective-permute-done.refs_1_) | copy-start | bytes 589828
  14.3 14.8 %copy-start.15 = (bf16[90,1,12288]{2,0,1:T(8,128)(2,1)S(1)}, bf16[90,1,12288]{2,0,1:T(8,128)(2,1)}, u32[]{:S(2)}) copy-start(bf16[90,1,12288]{2,0,1:T(8,128)(2,1)} %param.11) | copy-start | bytes 6635524
  17.2 45.4 %all-to-all-start = ((bf16[64,8,768]{2,1,0:T(8,128)(2,1)}), bf16[64,8,768]{2,1,0:T(8,128)(2,1)}, u32[]{:S(2)}, u32[]{:S(2)}) async-start(bf16[64,8,768]{2,1,0:T(8,128)(2,1)} %shard_map.109), calls=%async_computation | async-start | bytes 1572864 | tf_op jit(solution)/shard_map/all_to_all | solution.py:379
  29.1 27.7 %copy-start.12 = (bf16[512,512]{1,0:T(8,128)(2,1)S(1)}, bf16[512,512]{1,0:T(8,128)(2,1)}, u32[]{:S(2)}) copy-start(bf16[512,512]{1,0:T(8,128)(2,1)} %constant.57.clone.refs_4_) | copy-start | bytes 1572868
  29.5 33.0 %copy-start.1 = (bf16[16,12288]{1,0:T(8,128)(2,1)}, bf16[16,12288]{1,0:T(8,128)(2,1)S(1)}, u32[]{:S(2)}) copy-start(bf16[16,12288]{1,0:T(8,128)(2,1)S(1)} %get-tuple-element.40.refs_0_) | copy-start | bytes 1179652
  29.5 16.0 %collective-permute-start.5 = (bf16[16,12288]{1,0:T(8,128)(2,1)S(1)}, bf16[16,12288]{1,0:T(8,128)(2,1)S(1)}, u32[]{:S(2)}, u32[]{:S(2)}) collective-permute-start(bf16[16,12288]{1,0:T(8,128)(2,1)S(1)} %get-tuple-element.37), channel_id=1, source_target_pairs={{0,192},{64,128},{128,64},{192,0},{1,193},{65,129},{129,65},{193,1... | collective-permute-start | bytes 1179656 | tf_op jit(solution)/shard_map/ppermute | solution.py:351
  31.0 14.5 %collective-permute-start.3 = (bf16[16,12288]{1,0:T(8,128)(2,1)S(1)}, bf16[16,12288]{1,0:T(8,128)(2,1)S(1)}, u32[]{:S(2)}, u32[]{:S(2)}) collective-permute-start(bf16[16,12288]{1,0:T(8,128)(2,1)S(1)} %get-tuple-element.38), channel_id=1, source_target_pairs={{0,64},{64,0},{128,192},{192,128},{1,65},{65,1},{129,193},{193,129... | collective-permute-start | bytes 1179656 | tf_op jit(solution)/shard_map/ppermute | solution.py:351
  31.3 25.5 %collective-permute-start.4 = (bf16[16,12288]{1,0:T(8,128)(2,1)S(1)}, bf16[16,12288]{1,0:T(8,128)(2,1)S(1)}, u32[]{:S(2)}, u32[]{:S(2)}) collective-permute-start(bf16[16,12288]{1,0:T(8,128)(2,1)S(1)} %get-tuple-element.39), channel_id=1, source_target_pairs={{0,128},{64,192},{128,0},{192,64},{1,129},{65,193},{129,1},{193,65... | collective-permute-start | bytes 1179656 | tf_op jit(solution)/shard_map/ppermute | solution.py:351
  45.5 17.0 %copy-start.2 = (bf16[16,12288]{1,0:T(8,128)(2,1)}, bf16[16,12288]{1,0:T(8,128)(2,1)S(1)}, u32[]{:S(2)}) copy-start(bf16[16,12288]{1,0:T(8,128)(2,1)S(1)} %collective-permute-done.5.refs_3_) | copy-start | bytes 1179652
  45.5 17.0 %copy-start.3 = (bf16[16,12288]{1,0:T(8,128)(2,1)}, bf16[16,12288]{1,0:T(8,128)(2,1)S(1)}, u32[]{:S(2)}) copy-start(bf16[16,12288]{1,0:T(8,128)(2,1)S(1)} %collective-permute-done.3.refs_1_) | copy-start | bytes 1179652
  62.5 11.0 %copy-start.20 = (f32[1,2,96]{2,1,0:T(2,128)S(1)}, f32[1,2,96]{2,1,0:T(2,128)}, u32[]{:S(2)}) copy-start(f32[1,2,96]{2,1,0:T(2,128)} %param.15) | copy-start | bytes 2308
  62.5 11.6 %copy-start.17 = (bf16[1,2,96,96]{3,2,1,0:T(8,128)(2,1)S(1)}, bf16[1,2,96,96]{3,2,1,0:T(8,128)(2,1)}, u32[]{:S(2)}) copy-start(bf16[1,2,96,96]{3,2,1,0:T(8,128)(2,1)} %param.12) | copy-start | bytes 110596
  62.6 49.7 %all-to-all-start.1 = ((bf16[64,16,768]{2,1,0:T(8,128)(2,1)}), bf16[64,16,768]{2,1,0:T(8,128)(2,1)S(1)}, u32[]{:S(2)}, u32[]{:S(2)}) async-start(bf16[64,16,768]{2,1,0:T(8,128)(2,1)} %shard_map.110), calls=%async_computation.1 | async-start | bytes 3145728 | tf_op jit(solution)/shard_map/all_to_all | solution.py:379
  128.0 46.1 %all-to-all-start.2 = ((bf16[64,16,768]{2,1,0:T(8,128)(2,1)}), bf16[64,16,768]{2,1,0:T(8,128)(2,1)}, u32[]{:S(2)}, u32[]{:S(2)}) async-start(bf16[64,16,768]{2,1,0:T(8,128)(2,1)} %bitcast.55), calls=%async_computation.2 | async-start | bytes 3145728 | tf_op jit(solution)/shard_map/all_to_all | solution.py:379
  174.2 29.3 %all-to-all-start.3 = ((bf16[64,8,768]{2,1,0:T(8,128)(2,1)}), bf16[64,8,768]{2,1,0:T(8,128)(2,1)S(1)}, u32[]{:S(2)}, u32[]{:S(2)}) async-start(bf16[64,8,768]{2,1,0:T(8,128)(2,1)} %bitcast.53), calls=%async_computation.3 | async-start | bytes 1572864 | tf_op jit(solution)/shard_map/all_to_all | solution.py:379
  185.2 18.3 %copy-start = (bf16[512,512]{1,0:T(8,128)(2,1)S(1)}, bf16[512,512]{1,0:T(8,128)(2,1)}, u32[]{:S(2)}) copy-start(bf16[512,512]{1,0:T(8,128)(2,1)} %constant.58.clone.table) | copy-start | bytes 1572868
  185.2 18.3 %copy-start.6 = (bf16[8,12288]{1,0:T(8,128)(2,1)S(1)}, bf16[8,12288]{1,0:T(8,128)(2,1)}, u32[]{:S(2)}) copy-start(bf16[8,12288]{1,0:T(8,128)(2,1)} %copy-done.5) | copy-start | bytes 589828
  185.2 18.3 %copy-start.8 = (bf16[8,12288]{1,0:T(8,128)(2,1)S(1)}, bf16[8,12288]{1,0:T(8,128)(2,1)}, u32[]{:S(2)}) copy-start(bf16[8,12288]{1,0:T(8,128)(2,1)} %copy-done.7) | copy-start | bytes 589828
  185.2 21.4 %collective-permute-start.12 = (bf16[8,12288]{1,0:T(8,128)(2,1)}, bf16[8,12288]{1,0:T(8,128)(2,1)}, u32[]{:S(2)}, u32[]{:S(2)}) collective-permute-start(bf16[8,12288]{1,0:T(8,128)(2,1)} %get-tuple-element.34), channel_id=1, source_target_pairs={{0,64},{64,0},{128,192},{192,128},{1,65},{65,1},{129,193},{193,129... | collective-permute-start | bytes 589832 | tf_op jit(solution)/shard_map/ppermute | solution.py:351
  185.7 22.0 %collective-permute-start.13 = (bf16[8,12288]{1,0:T(8,128)(2,1)}, bf16[8,12288]{1,0:T(8,128)(2,1)}, u32[]{:S(2)}, u32[]{:S(2)}) collective-permute-start(bf16[8,12288]{1,0:T(8,128)(2,1)} %get-tuple-element.35), channel_id=1, source_target_pairs={{0,128},{64,192},{128,0},{192,64},{1,129},{65,193},{129,1},{193,65... | collective-permute-start | bytes 589832 | tf_op jit(solution)/shard_map/ppermute | solution.py:351
  187.3 20.3 %collective-permute-start.14 = (bf16[8,12288]{1,0:T(8,128)(2,1)}, bf16[8,12288]{1,0:T(8,128)(2,1)}, u32[]{:S(2)}, u32[]{:S(2)}) collective-permute-start(bf16[8,12288]{1,0:T(8,128)(2,1)} %get-tuple-element.36), channel_id=1, source_target_pairs={{0,192},{64,128},{128,64},{192,0},{1,193},{65,129},{129,65},{193,1... | collective-permute-start | bytes 589832 | tf_op jit(solution)/shard_map/ppermute | solution.py:351
  192.0 17.0 %collective-permute-start.9 = (bf16[8,12288]{1,0:T(8,128)(2,1)}, bf16[8,12288]{1,0:T(8,128)(2,1)S(1)}, u32[]{:S(2)}, u32[]{:S(2)}) collective-permute-start(bf16[8,12288]{1,0:T(8,128)(2,1)} %get-tuple-element.30), channel_id=1, source_target_pairs={{0,64},{64,0},{128,192},{192,128},{1,65},{65,1},{129,193},{193,129... | collective-permute-start | bytes 589832 | tf_op jit(solution)/shard_map/ppermute | solution.py:351
  192.4 17.1 %collective-permute-start.10 = (bf16[8,12288]{1,0:T(8,128)(2,1)}, bf16[8,12288]{1,0:T(8,128)(2,1)S(1)}, u32[]{:S(2)}, u32[]{:S(2)}) collective-permute-start(bf16[8,12288]{1,0:T(8,128)(2,1)} %get-tuple-element.31), channel_id=1, source_target_pairs={{0,128},{64,192},{128,0},{192,64},{1,129},{65,193},{129,1},{193,65... | collective-permute-start | bytes 589832 | tf_op jit(solution)/shard_map/ppermute | solution.py:351
  206.6 6.8 %collective-permute-start.11 = (bf16[8,12288]{1,0:T(8,128)(2,1)}, bf16[8,12288]{1,0:T(8,128)(2,1)S(1)}, u32[]{:S(2)}, u32[]{:S(2)}) collective-permute-start(bf16[8,12288]{1,0:T(8,128)(2,1)} %get-tuple-element.32), channel_id=1, source_target_pairs={{0,192},{64,128},{128,64},{192,0},{1,193},{65,129},{129,65},{193,1... | collective-permute-start | bytes 589832 | tf_op jit(solution)/shard_map/ppermute | solution.py:351
  207.6 10.3 %collective-permute-start.6 = (bf16[8,12288]{1,0:T(8,128)(2,1)S(1)}, bf16[8,12288]{1,0:T(8,128)(2,1)S(1)}, u32[]{:S(2)}, u32[]{:S(2)}) collective-permute-start(bf16[8,12288]{1,0:T(8,128)(2,1)S(1)} %get-tuple-element.25), channel_id=1, source_target_pairs={{0,64},{64,0},{128,192},{192,128},{1,65},{65,1},{129,193},{193,129... | collective-permute-start | bytes 589832 | tf_op jit(solution)/shard_map/ppermute | solution.py:351
  207.7 11.4 %collective-permute-start.7 = (bf16[8,12288]{1,0:T(8,128)(2,1)S(1)}, bf16[8,12288]{1,0:T(8,128)(2,1)S(1)}, u32[]{:S(2)}, u32[]{:S(2)}) collective-permute-start(bf16[8,12288]{1,0:T(8,128)(2,1)S(1)} %get-tuple-element.26), channel_id=1, source_target_pairs={{0,128},{64,192},{128,0},{192,64},{1,129},{65,193},{129,1},{193,65... | collective-permute-start | bytes 589832 | tf_op jit(solution)/shard_map/ppermute | solution.py:351
  209.0 12.9 %collective-permute-start.8 = (bf16[8,12288]{1,0:T(8,128)(2,1)S(1)}, bf16[8,12288]{1,0:T(8,128)(2,1)S(1)}, u32[]{:S(2)}, u32[]{:S(2)}) collective-permute-start(bf16[8,12288]{1,0:T(8,128)(2,1)S(1)} %get-tuple-element.27), channel_id=1, source_target_pairs={{0,192},{64,128},{128,64},{192,0},{1,193},{65,129},{129,65},{193,1... | collective-permute-start | bytes 589832 | tf_op jit(solution)/shard_map/ppermute | solution.py:351
  (8 other events, 27.0 us)

commit v4 on v3

--- a/solution.py
+++ b/solution.py
@@ -24,21 +24,24 @@
 
 def lon_tables(lat_devices, lon_devices, local_lon, rows, chunk):
     length = local_lon * lon_devices
-    kept = length // 2
     i, j, r = np.meshgrid(
-        np.arange(lat_devices), np.arange(lon_devices), np.arange(*chunk), indexing="ij"
+        np.arange(lat_devices), np.arange(lon_devices // 2), np.arange(*chunk), indexing="ij"
     )
     offset = (i * rows + r).reshape(-1)
     place = (j.reshape(-1) * local_lon + offset).astype(np.int64)
     real = (offset < local_lon).astype(np.float32)
     place = np.where(offset < local_lon, place, 0)
-    cosine, sine = phases(np.arange(kept), place, length)
     factor = np.float32(1.0 / math.sqrt(length))
-    forward = np.concatenate([cosine, -sine], axis=0) * factor * real
-    weights = np.where(np.arange(kept) == 0, 1.0, 2.0).astype(np.float32)[:, None]
-    inverse = np.concatenate([cosine * weights, -sine * weights], axis=0).T * factor
-    inverse = inverse * real[:, None]
-    return forward.astype(jnp.bfloat16), inverse.astype(jnp.bfloat16)
+    forward, inverse = [], []
+    for parity in range(2):
+        modes = np.arange(parity, length // 2, 2)
+        cosine, sine = phases(modes, place, length)
+        extra = ((0, -len(modes) % 16), (0, 0))
+        stack = lambda c, q: np.concatenate([np.pad(c, extra), np.pad(-q, extra)], axis=0)
+        weights = np.where(modes == 0, 1.0, 2.0).astype(np.float32)[:, None]
+        forward.append(stack(cosine, sine) * factor * real)
+        inverse.append((stack(cosine * weights, sine * weights) * factor * real).T)
+    return np.stack(forward).astype(jnp.bfloat16), np.stack(inverse).astype(jnp.bfloat16)
 
 
 def lat_table(length):
@@ -74,28 +77,54 @@
     return v - jnp.minimum(jnp.maximum(v, -shrink_level), shrink_level)
 
 
-def spectral_kernel(flag, *refs, chunks):
+def fold(x, blocks):
+    half = x.shape[0] // (2 * blocks)
+    near, far = [
+        jnp.concatenate(
+            [x[pl.ds((2 * n + side) * half, half), :].astype(jnp.float32) for n in range(blocks)],
+            axis=0,
+        )
+        for side in range(2)
+    ]
+    return (near + far).astype(jnp.bfloat16), (near - far).astype(jnp.bfloat16)
+
+
+def unfold(inv, y, out, blocks):
+    count = inv.shape[2]
+    even, odd = [
+        jnp.dot(inv[p], y[pl.ds(p * count, count), :], preferred_element_type=jnp.float32)
+        for p in range(2)
+    ]
+    near, far = (even + odd).astype(out.dtype), (even - odd).astype(out.dtype)
+    half = out.shape[0] // (2 * blocks)
+    for n in range(blocks):
+        out[pl.ds(2 * n * half, half), :] = near[n * half : (n + 1) * half]
+        out[pl.ds((2 * n + 1) * half, half), :] = far[n * half : (n + 1) * half]
+
+
+def spectral_kernel(flag, *refs, chunks, blocks):
     xs, fwds = refs[:chunks], refs[chunks : 2 * chunks]
     inv, w1, b1, w2, b2, out, y, z = refs[2 * chunks :]
-    kept = fwds[0].shape[0] // 2
+    count = fwds[0].shape[1]
+    kept = count // 2
     width = w1.shape[1] // 4
     slots = y.shape[1] // (2 * width)
     lanes = w2.shape[1] // 4
-    for part in range(2):
-        rows = pl.ds(part * kept, kept)
+    folded = [fold(x, blocks) for x in xs]
+    for p in range(2):
         total = None
-        for x, fwd in zip(xs, fwds):
-            term = jnp.dot(fwd[rows, :], x[...], preferred_element_type=jnp.float32)
+        for fwd, pair in zip(fwds, folded):
+            term = jnp.dot(fwd[p], pair[p], preferred_element_type=jnp.float32)
             total = term if total is None else total + term
-        z[rows, :] = total.astype(z.dtype)
-    for s in range(slots):
+        z[pl.ds(p * count, count), :] = total.astype(z.dtype)
+    for base, s in [(p * count, s) for p in range(2) for s in range(slots)]:
         cols = pl.ds(s * 2 * width, 2 * width)
         layer = w1[min(s, 1)]
         hidden = jnp.dot(
-            z[pl.ds(0, kept), cols], layer[: 2 * width], preferred_element_type=jnp.float32
+            z[pl.ds(base, kept), cols], layer[: 2 * width], preferred_element_type=jnp.float32
         )
         hidden = hidden + jnp.dot(
-            z[pl.ds(kept, kept), cols], layer[2 * width :], preferred_element_type=jnp.float32
+            z[pl.ds(base + kept, kept), cols], layer[2 * width :], preferred_element_type=jnp.float32
         )
         hidden = jnp.maximum(hidden + b1[...], 0.0).astype(jnp.bfloat16)
         v = jnp.dot(hidden, w2[...], preferred_element_type=jnp.float32) + b2[...]
@@ -107,22 +136,22 @@
             alone = flag[0] == 1
             top = (jnp.where(alone, re, top[0]), jnp.where(alone, re2, top[1]))
             bottom = (jnp.where(alone, im, bottom[0]), jnp.where(alone, im2, bottom[1]))
-        for start, (a, b) in ((0, top), (kept, bottom)):
+        for start, (a, b) in ((base, top), (base + kept, bottom)):
             y[pl.ds(start, kept), cols] = jnp.concatenate(
                 [a[:, :width], b[:, :width]], axis=1
             ).astype(y.dtype)
-    out[...] = jnp.dot(inv[...], y[...], preferred_element_type=jnp.float32).astype(out.dtype)
-
-
-def unwind_kernel(inv, y, out):
-    out[...] = jnp.dot(inv[...], y[...], preferred_element_type=jnp.float32).astype(out.dtype)
-
-
-def unwind(inv, y):
+    unfold(inv, y, out, blocks)
+
+
+def unwind_kernel(inv, y, out, *, blocks):
+    unfold(inv, y, out, blocks)
+
+
+def unwind(inv, y, blocks):
     whole = pl.BlockSpec(memory_space=pltpu.VMEM)
     return pl.pallas_call(
-        unwind_kernel,
-        out_shape=jax.ShapeDtypeStruct((inv.shape[0], y.shape[1]), jnp.bfloat16),
+        functools.partial(unwind_kernel, blocks=blocks),
+        out_shape=jax.ShapeDtypeStruct((2 * inv.shape[1], y.shape[1]), jnp.bfloat16),
         in_specs=[whole] * 2,
         out_specs=whole,
         compiler_params=pltpu.CompilerParams(vmem_limit_bytes=62 * 2**20),
@@ -133,13 +162,13 @@
     )(inv, y)
 
 
-def spectral(flag, xs, fwds, inv, w1, b1, w2, b2):
+def spectral(flag, xs, fwds, inv, w1, b1, w2, b2, blocks):
     whole = pl.BlockSpec(memory_space=pltpu.VMEM)
-    rows, cols = fwds[0].shape[0], xs[0].shape[1]
+    rows, cols = 2 * fwds[0].shape[1], xs[0].shape[1]
     return pl.pallas_call(
-        functools.partial(spectral_kernel, chunks=len(xs)),
+        functools.partial(spectral_kernel, chunks=len(xs), blocks=blocks),
         out_shape=[
-            jax.ShapeDtypeStruct((inv.shape[0], cols), jnp.bfloat16),
+            jax.ShapeDtypeStruct((2 * inv.shape[1], cols), jnp.bfloat16),
             jax.ShapeDtypeStruct((rows, cols), jnp.bfloat16),
         ],
         in_specs=[pl.BlockSpec(memory_space=pltpu.SMEM)] + [whole] * (2 * len(xs) + 5),
@@ -390,9 +419,9 @@
         xs.append(lat_forward(place, fields[-1], lat, everyone, width))
     for n in range(2):
         xs[n] = exchange(xs[n])
-    last, y = spectral(flag, [flat(x) for x in xs], fwds, invs[1], w1, b1, w2, b2)
+    last, y = spectral(flag, [flat(x) for x in xs], fwds, invs[1], w1, b1, w2, b2, lat_n)
     outs = [None, last]
-    outs[0] = unwind(invs[0], y)
+    outs[0] = unwind(invs[0], y, lat_n)
     backs = [None, None]
     for n in (1, 0):
         if n == 0:

time: 226 us -> 222 us (0.982)
  Pallas kernels: 41.8 us -> 37.4 us
    pallas_call x2, Pallas kernels: 19 us -> 14.7 us  [the longest x1 11.1 us: spectral(): pl.pallas_call(functools.partial(spectral_kernel, chunks=len(xs), blocks=...]
where the time goes in v4:
time: 222 us; the launch traced here: 219 us
  waiting for transfers between devices  124 us (56%)
  starting transfers between devices  46.1 us (21%)
  Pallas kernels  37.4 us (17%)
  local copies, waits for them, and re-layouts  8.59 us (4%)
  other arithmetic  2.97 us (1%)
    all_to_all x4, waiting for transfers between devices, layer(): lax.all_to_all(x, group, split_axis=0, concat_axis=0, tiled=True)  81.4 us
    ppermute x15, waiting for transfers between devices, swap(): lax.ppermute(pieces[m], 'lat', [(i, i ^ m) for i in range(count)])  42.5 us
    all_to_all x4, starting transfers between devices, layer(): lax.all_to_all(x, group, split_axis=0, concat_axis=0, tiled=True)  35.1 us
    pallas_call x5, Pallas kernels, lat_call(): pl.pallas_call(kernel, grid=(rows // 8,), out_shape=out_shape, in_specs=[...  19.1 us
    pallas_call x1, Pallas kernels, spectral(): pl.pallas_call(functools.partial(spectral_kernel, chunks=len(xs), blocks=...  11.1 us
    ppermute x15, starting transfers between devices, swap(): lax.ppermute(pieces[m], 'lat', [(i, i ^ m) for i in range(count)])  11.1 us
    unnamed x42, local copies, waits for them, and re-layouts  5.94 us
  transfers between devices with their start and end apart: 19, of which 10 were waited for; matrix products, arithmetic and copies ran while one was open for 2% of the time, Pallas kernels for 10%

profile of v4, /device:TPU:38, one launch (start us, length us, event | category | flops | bytes accessed | tf_op | source)
XLA Modules:
  0.0 219.4 jit_solution(16284566052771941316)
XLA Ops:
  0.0 1.6 dynamic-slice_bitcast_fusion
  1.6 1.1 collective-permute-start.2
  3.5 5.2 %collective-permute-done.2.refs_3_ = bf16[8,12288]{1,0:T(8,128)(2,1)S(1)} collective-permute-done((bf16[8,12288]{1,0:T(8,128)(2,1)S(1)}, bf16[8,12288]{1,0:T(8,128)(2,1)S(1)}, u32[]{:S(2)}, u32[]{:S(2)}) %collective-permute-start.2) | collective-permute-done | bytes 196640 | tf_op jit(solution)/shard_map/ppermute | solution.py:380
  8.7 4.3 %collective-permute-done.1.refs_2_ = bf16[8,12288]{1,0:T(8,128)(2,1)S(1)} collective-permute-done((bf16[8,12288]{1,0:T(8,128)(2,1)S(1)}, bf16[8,12288]{1,0:T(8,128)(2,1)S(1)}, u32[]{:S(2)}, u32[]{:S(2)}) %collective-permute-start.1) | collective-permute-done | bytes 196640 | tf_op jit(solution)/shard_map/ppermute | solution.py:380
  13.1 1.2 copy-done.11
  14.3 2.9 %shard_map.109 = bf16[64,8,768]{2,1,0:T(8,128)(2,1)} custom-call(s32[1]{0:T(128)} %bitcast.place, bf16[8,12288]{1,0:T(8,128)(2,1)S(1)} %get-tuple-element.44.refs_0_, bf16[8,12288]{1,0:T(8,128)(2,1)S(1)} %collective-permute-done.refs_1_, bf16[8,12288]{1,0:T(8,128)(2,1)S(1)} %collective-permute-done.1.refs_2_, ...), custom_call_target="tpu_custom_call" | custom-call | flops 536870912 | bytes 1572864 | tf_op jit(solution)/shard_map/pallas_call | solution.py:261
  17.2 11.9 %all-to-all-start = ((bf16[64,8,768]{2,1,0:T(8,128)(2,1)}), bf16[64,8,768]{2,1,0:T(8,128)(2,1)}, u32[]{:S(2)}, u32[]{:S(2)}) async-start(bf16[64,8,768]{2,1,0:T(8,128)(2,1)} %shard_map.109), calls=%async_computation | async-start | bytes 1572864 | tf_op jit(solution)/shard_map/all_to_all | solution.py:408
  29.5 1.5 collective-permute-start.5
  31.8 13.7 %collective-permute-done.5.refs_3_ = bf16[16,12288]{1,0:T(8,128)(2,1)S(1)} collective-permute-done((bf16[16,12288]{1,0:T(8,128)(2,1)S(1)}, bf16[16,12288]{1,0:T(8,128)(2,1)S(1)}, u32[]{:S(2)}, u32[]{:S(2)}) %collective-permute-start.5) | collective-permute-done | bytes 393248 | tf_op jit(solution)/shard_map/ppermute | solution.py:380
  45.5 11.3 %collective-permute-done.4.refs_2_ = bf16[16,12288]{1,0:T(8,128)(2,1)S(1)} collective-permute-done((bf16[16,12288]{1,0:T(8,128)(2,1)S(1)}, bf16[16,12288]{1,0:T(8,128)(2,1)S(1)}, u32[]{:S(2)}, u32[]{:S(2)}) %collective-permute-start.4) | collective-permute-done | bytes 393248 | tf_op jit(solution)/shard_map/ppermute | solution.py:380
  56.8 4.9 %shard_map.110 = bf16[64,16,768]{2,1,0:T(8,128)(2,1)} custom-call(s32[1]{0:T(128)} %bitcast.place, bf16[16,12288]{1,0:T(8,128)(2,1)S(1)} %get-tuple-element.40.refs_0_, bf16[16,12288]{1,0:T(8,128)(2,1)S(1)} %collective-permute-done.3.refs_1_, bf16[16,12288]{1,0:T(8,128)(2,1)S(1)} %collective-permute-done.4.refs_2_, ...), custom_call_target="tpu_custom_call" | custom-call | flops 1073741824 | bytes 3145728 | tf_op jit(solution)/shard_map/pallas_call | solution.py:261
  62.6 10.1 %all-to-all-start.1 = ((bf16[64,16,768]{2,1,0:T(8,128)(2,1)}), bf16[64,16,768]{2,1,0:T(8,128)(2,1)S(1)}, u32[]{:S(2)}, u32[]{:S(2)}) async-start(bf16[64,16,768]{2,1,0:T(8,128)(2,1)} %shard_map.110), calls=%async_computation.1 | async-start | bytes 3145728 | tf_op jit(solution)/shard_map/all_to_all | solution.py:408
  76.5 35.7 %all-to-all-done.1 = bf16[64,16,768]{2,1,0:T(8,128)(2,1)S(1)} async-done(((bf16[64,16,768]{2,1,0:T(8,128)(2,1)}), bf16[64,16,768]{2,1,0:T(8,128)(2,1)S(1)}, u32[]{:S(2)}, u32[]{:S(2)}) %all-to-all-start.1) | async-done | bytes 1572896 | tf_op jit(solution)/shard_map/all_to_all | solution.py:408
  112.2 1.2 copy-done.16
  113.4 11.1 %spectral.1 = (bf16[1024,768]{1,0:T(8,128)(2,1)}, bf16[1472,768]{1,0:T(8,128)(2,1)}) custom-call(s32[1]{0:T(128)} %bitcast.1.flag, bf16[512,768]{1,0:T(8,128)(2,1)} %bitcast.6.refs_0_, bf16[1024,768]{1,0:T(8,128)(2,1)} %bitcast.54, bf16[2,736,256]{2,1,0:T(8,128)(2,1)} %constant.53.clone.refs_2_, bf16[2,736,512]{2,1,0:T(8,128)(2,1)} %constant.54.clone.refs_3_, ...), custom_call_target="tpu_custom_call" | custom-call | flops 8999999488 | bytes 14000000 | tf_op jit(solution)/shard_map/spectral/pallas_call | solution.py:168
  124.5 6.6 %all-to-all-start.2 = ((bf16[64,16,768]{2,1,0:T(8,128)(2,1)}), bf16[64,16,768]{2,1,0:T(8,128)(2,1)}, u32[]{:S(2)}, u32[]{:S(2)}) async-start(bf16[64,16,768]{2,1,0:T(8,128)(2,1)} %bitcast.55), calls=%async_computation.2 | async-start | bytes 3145728 | tf_op jit(solution)/shard_map/all_to_all | solution.py:408
  131.1 3.6 %unwind.1 = bf16[512,768]{1,0:T(8,128)(2,1)} custom-call(bf16[2,256,736]{2,1,0:T(8,128)(2,1)} %constant.55.clone.inv, bf16[1472,768]{1,0:T(8,128)(2,1)} %get-tuple-element.21.y), custom_call_target="tpu_custom_call" | custom-call | flops 1000000000 | bytes 4000000 | tf_op jit(solution)/shard_map/unwind/pallas_call | solution.py:152
  134.7 36.0 %all-to-all-done.2.back = bf16[64,16,768]{2,1,0:T(8,128)(2,1)} async-done(((bf16[64,16,768]{2,1,0:T(8,128)(2,1)}), bf16[64,16,768]{2,1,0:T(8,128)(2,1)}, u32[]{:S(2)}, u32[]{:S(2)}) %all-to-all-start.2) | async-done | bytes 1572896 | tf_op jit(solution)/shard_map/all_to_all | solution.py:408
  170.7 6.4 %all-to-all-start.3 = ((bf16[64,8,768]{2,1,0:T(8,128)(2,1)}), bf16[64,8,768]{2,1,0:T(8,128)(2,1)S(1)}, u32[]{:S(2)}, u32[]{:S(2)}) async-start(bf16[64,8,768]{2,1,0:T(8,128)(2,1)} %bitcast.53), calls=%async_computation.3 | async-start | bytes 1572864 | tf_op jit(solution)/shard_map/all_to_all | solution.py:408
  177.1 4.6 %shard_map.113 = (bf16[8,12288]{1,0:T(8,128)(2,1)}, bf16[8,12288]{1,0:T(8,128)(2,1)}, bf16[8,12288]{1,0:T(8,128)(2,1)}, bf16[8,12288]{1,0:T(8,128)(2,1)}) custom-call(s32[1]{0:T(128)} %bitcast.place, bf16[64,16,768]{2,1,0:T(8,128)(2,1)} %all-to-all-done.2.back, bf16[512,512]{1,0:T(8,128)(2,1)} %constant.58.clone.table, bf16[16,12288]{1,0:T(8,128)(2,1)} %copy-done.1, ...), custom_call_target="tpu_custom_call" | custom-call | flops 536870912 | bytes 1572864 | tf_op jit(solution)/shard_map/pallas_call | solution.py:261
  181.9 1.7 collective-permute-start.13
  183.7 4.6 %shard_map.112 = (bf16[8,12288]{1,0:T(8,128)(2,1)}, bf16[8,12288]{1,0:T(8,128)(2,1)}, bf16[8,12288]{1,0:T(8,128)(2,1)}, bf16[8,12288]{1,0:T(8,128)(2,1)}) custom-call(s32[1]{0:T(128)} %bitcast.place, bf16[64,16,768]{2,1,0:T(8,128)(2,1)} %all-to-all-done.2.back, bf16[512,512]{1,0:T(8,128)(2,1)} %constant.58.clone.table, bf16[16,12288]{1,0:T(8,128)(2,1)} %copy-done.1, ...), custom_call_target="tpu_custom_call" | custom-call | flops 536870912 | bytes 1572864 | tf_op jit(solution)/shard_map/pallas_call | solution.py:261
  188.6 1.7 collective-permute-start.10
  190.3 9.7 %all-to-all-done.3.back = bf16[64,8,768]{2,1,0:T(8,128)(2,1)S(1)} async-done(((bf16[64,8,768]{2,1,0:T(8,128)(2,1)}), bf16[64,8,768]{2,1,0:T(8,128)(2,1)S(1)}, u32[]{:S(2)}, u32[]{:S(2)}) %all-to-all-start.3) | async-done | bytes 786464 | tf_op jit(solution)/shard_map/all_to_all | solution.py:408
  200.9 2.2 %shard_map.111 = (bf16[8,12288]{1,0:T(8,128)(2,1)S(1)}, bf16[8,12288]{1,0:T(8,128)(2,1)S(1)}, bf16[8,12288]{1,0:T(8,128)(2,1)S(1)}, bf16[8,12288]{1,0:T(8,128)(2,1)S(1)}) custom-call(s32[1]{0:T(128)} %bitcast.place, bf16[64,8,768]{2,1,0:T(8,128)(2,1)S(1)} %all-to-all-done.3.back, bf16[512,512]{1,0:T(8,128)(2,1)S(1)} %copy-done, ...), custom_call_target="tpu_custom_call" | custom-call | flops 536870912 | bytes 1572864 | tf_op jit(solution)/shard_map/pallas_call | solution.py:261
  203.1 1.0 collective-permute-start.11
  204.1 1.3 collective-permute-start.7
  206.0 3.9 %collective-permute-done.11.refs_3_ = bf16[8,12288]{1,0:T(8,128)(2,1)S(1)} collective-permute-done((bf16[8,12288]{1,0:T(8,128)(2,1)}, bf16[8,12288]{1,0:T(8,128)(2,1)S(1)}, u32[]{:S(2)}, u32[]{:S(2)}) %collective-permute-start.11) | collective-permute-done | bytes 196640 | tf_op jit(solution)/shard_map/ppermute | solution.py:380
  209.9 0.9 copy-done.13
  211.8 2.7 %assemble.1.refs_4_ = bf16[90,12288]{1,0:T(8,128)(2,1)} custom-call(s32[1]{0:T(128)} %bitcast.place, bf16[8,12288]{1,0:T(8,128)(2,1)S(1)} %copy-done.14, bf16[8,12288]{1,0:T(8,128)(2,1)S(1)} %collective-permute-done.9.refs_1_, bf16[8,12288]{1,0:T(8,128)(2,1)S(1)} %collective-permute-done.10.refs_2_, bf16[8,12288]{1,0:T(8,128)(2,1)S(1)} %collective-permute-done.11.refs_3_, ...), custom_call_target="tpu_custom_call" | custom-call | bytes 5000000 | tf_op jit(solution)/shard_map/assemble/pallas_call | solution.py:356
  214.4 1.1 collective-permute-done.7.refs_2_
  215.5 2.8 %collective-permute-done.8.refs_3_ = bf16[8,12288]{1,0:T(8,128)(2,1)S(1)} collective-permute-done((bf16[8,12288]{1,0:T(8,128)(2,1)S(1)}, bf16[8,12288]{1,0:T(8,128)(2,1)S(1)}, u32[]{:S(2)}, u32[]{:S(2)}) %collective-permute-start.8) | collective-permute-done | bytes 196640 | tf_op jit(solution)/shard_map/ppermute | solution.py:380
  (79 shorter events, 10.5 us)
Async XLA Ops:
  1.6 7.2 %collective-permute-start.2 = (bf16[8,12288]{1,0:T(8,128)(2,1)S(1)}, bf16[8,12288]{1,0:T(8,128)(2,1)S(1)}, u32[]{:S(2)}, u32[]{:S(2)}) collective-permute-start(bf16[8,12288]{1,0:T(8,128)(2,1)S(1)} %get-tuple-element.41), channel_id=1, source_target_pairs={{0,192},{64,128},{128,64},{192,0},{1,193},{65,129},{129,65},{193,1... | collective-permute-start | bytes 589832 | tf_op jit(solution)/shard_map/ppermute | solution.py:380
  2.7 10.4 %collective-permute-start.1 = (bf16[8,12288]{1,0:T(8,128)(2,1)S(1)}, bf16[8,12288]{1,0:T(8,128)(2,1)S(1)}, u32[]{:S(2)}, u32[]{:S(2)}) collective-permute-start(bf16[8,12288]{1,0:T(8,128)(2,1)S(1)} %get-tuple-element.42), channel_id=1, source_target_pairs={{0,128},{64,192},{128,0},{192,64},{1,129},{65,193},{129,1},{193,65... | collective-permute-start | bytes 589832 | tf_op jit(solution)/shard_map/ppermute | solution.py:380
  3.4 9.7 %collective-permute-start = (bf16[8,12288]{1,0:T(8,128)(2,1)S(1)}, bf16[8,12288]{1,0:T(8,128)(2,1)S(1)}, u32[]{:S(2)}, u32[]{:S(2)}) collective-permute-start(bf16[8,12288]{1,0:T(8,128)(2,1)S(1)} %get-tuple-element.43), channel_id=1, source_target_pairs={{0,64},{64,0},{128,192},{192,128},{1,65},{65,1},{129,193},{193,129... | collective-permute-start | bytes 589832 | tf_op jit(solution)/shard_map/ppermute | solution.py:380
  8.7 20.7 %copy-start.5 = (bf16[8,12288]{1,0:T(8,128)(2,1)}, bf16[8,12288]{1,0:T(8,128)(2,1)S(1)}, u32[]{:S(2)}) copy-start(bf16[8,12288]{1,0:T(8,128)(2,1)S(1)} %collective-permute-done.2.refs_3_) | copy-start | bytes 589828
  13.1 16.4 %copy-start.7 = (bf16[8,12288]{1,0:T(8,128)(2,1)}, bf16[8,12288]{1,0:T(8,128)(2,1)S(1)}, u32[]{:S(2)}) copy-start(bf16[8,12288]{1,0:T(8,128)(2,1)S(1)} %collective-permute-done.1.refs_2_) | copy-start | bytes 589828
  13.1 16.4 %copy-start.9 = (bf16[8,12288]{1,0:T(8,128)(2,1)}, bf16[8,12288]{1,0:T(8,128)(2,1)S(1)}, u32[]{:S(2)}) copy-start(bf16[8,12288]{1,0:T(8,128)(2,1)S(1)} %collective-permute-done.refs_1_) | copy-start | bytes 589828
  14.3 14.8 %copy-start.15 = (bf16[90,1,12288]{2,0,1:T(8,128)(2,1)S(1)}, bf16[90,1,12288]{2,0,1:T(8,128)(2,1)}, u32[]{:S(2)}) copy-start(bf16[90,1,12288]{2,0,1:T(8,128)(2,1)} %param.11) | copy-start | bytes 6635524
  17.2 45.4 %all-to-all-start = ((bf16[64,8,768]{2,1,0:T(8,128)(2,1)}), bf16[64,8,768]{2,1,0:T(8,128)(2,1)}, u32[]{:S(2)}, u32[]{:S(2)}) async-start(bf16[64,8,768]{2,1,0:T(8,128)(2,1)} %shard_map.109), calls=%async_computation | async-start | bytes 1572864 | tf_op jit(solution)/shard_map/all_to_all | solution.py:408
  29.1 27.7 %copy-start.12 = (bf16[512,512]{1,0:T(8,128)(2,1)S(1)}, bf16[512,512]{1,0:T(8,128)(2,1)}, u32[]{:S(2)}) copy-start(bf16[512,512]{1,0:T(8,128)(2,1)} %constant.57.clone.refs_4_) | copy-start | bytes 1572868
  29.5 33.0 %copy-start.1 = (bf16[16,12288]{1,0:T(8,128)(2,1)}, bf16[16,12288]{1,0:T(8,128)(2,1)S(1)}, u32[]{:S(2)}) copy-start(bf16[16,12288]{1,0:T(8,128)(2,1)S(1)} %get-tuple-element.40.refs_0_) | copy-start | bytes 1179652
  29.5 16.0 %collective-permute-start.5 = (bf16[16,12288]{1,0:T(8,128)(2,1)S(1)}, bf16[16,12288]{1,0:T(8,128)(2,1)S(1)}, u32[]{:S(2)}, u32[]{:S(2)}) collective-permute-start(bf16[16,12288]{1,0:T(8,128)(2,1)S(1)} %get-tuple-element.37), channel_id=1, source_target_pairs={{0,192},{64,128},{128,64},{192,0},{1,193},{65,129},{129,65},{193,1... | collective-permute-start | bytes 1179656 | tf_op jit(solution)/shard_map/ppermute | solution.py:380
  31.0 14.5 %collective-permute-start.3 = (bf16[16,12288]{1,0:T(8,128)(2,1)S(1)}, bf16[16,12288]{1,0:T(8,128)(2,1)S(1)}, u32[]{:S(2)}, u32[]{:S(2)}) collective-permute-start(bf16[16,12288]{1,0:T(8,128)(2,1)S(1)} %get-tuple-element.38), channel_id=1, source_target_pairs={{0,64},{64,0},{128,192},{192,128},{1,65},{65,1},{129,193},{193,129... | collective-permute-start | bytes 1179656 | tf_op jit(solution)/shard_map/ppermute | solution.py:380
  31.3 25.5 %collective-permute-start.4 = (bf16[16,12288]{1,0:T(8,128)(2,1)S(1)}, bf16[16,12288]{1,0:T(8,128)(2,1)S(1)}, u32[]{:S(2)}, u32[]{:S(2)}) collective-permute-start(bf16[16,12288]{1,0:T(8,128)(2,1)S(1)} %get-tuple-element.39), channel_id=1, source_target_pairs={{0,128},{64,192},{128,0},{192,64},{1,129},{65,193},{129,1},{193,65... | collective-permute-start | bytes 1179656 | tf_op jit(solution)/shard_map/ppermute | solution.py:380
  45.5 17.0 %copy-start.2 = (bf16[16,12288]{1,0:T(8,128)(2,1)}, bf16[16,12288]{1,0:T(8,128)(2,1)S(1)}, u32[]{:S(2)}) copy-start(bf16[16,12288]{1,0:T(8,128)(2,1)S(1)} %collective-permute-done.5.refs_3_) | copy-start | bytes 1179652
  45.5 17.0 %copy-start.3 = (bf16[16,12288]{1,0:T(8,128)(2,1)}, bf16[16,12288]{1,0:T(8,128)(2,1)S(1)}, u32[]{:S(2)}) copy-start(bf16[16,12288]{1,0:T(8,128)(2,1)S(1)} %collective-permute-done.3.refs_1_) | copy-start | bytes 1179652
  62.5 11.0 %copy-start.20 = (f32[1,2,96]{2,1,0:T(2,128)S(1)}, f32[1,2,96]{2,1,0:T(2,128)}, u32[]{:S(2)}) copy-start(f32[1,2,96]{2,1,0:T(2,128)} %param.15) | copy-start | bytes 2308
  62.5 11.6 %copy-start.17 = (bf16[1,2,96,96]{3,2,1,0:T(8,128)(2,1)S(1)}, bf16[1,2,96,96]{3,2,1,0:T(8,128)(2,1)}, u32[]{:S(2)}) copy-start(bf16[1,2,96,96]{3,2,1,0:T(8,128)(2,1)} %param.12) | copy-start | bytes 110596
  62.6 49.7 %all-to-all-start.1 = ((bf16[64,16,768]{2,1,0:T(8,128)(2,1)}), bf16[64,16,768]{2,1,0:T(8,128)(2,1)S(1)}, u32[]{:S(2)}, u32[]{:S(2)}) async-start(bf16[64,16,768]{2,1,0:T(8,128)(2,1)} %shard_map.110), calls=%async_computation.1 | async-start | bytes 3145728 | tf_op jit(solution)/shard_map/all_to_all | solution.py:408
  124.5 46.1 %all-to-all-start.2 = ((bf16[64,16,768]{2,1,0:T(8,128)(2,1)}), bf16[64,16,768]{2,1,0:T(8,128)(2,1)}, u32[]{:S(2)}, u32[]{:S(2)}) async-start(bf16[64,16,768]{2,1,0:T(8,128)(2,1)} %bitcast.55), calls=%async_computation.2 | async-start | bytes 3145728 | tf_op jit(solution)/shard_map/all_to_all | solution.py:408
  170.7 29.3 %all-to-all-start.3 = ((bf16[64,8,768]{2,1,0:T(8,128)(2,1)}), bf16[64,8,768]{2,1,0:T(8,128)(2,1)S(1)}, u32[]{:S(2)}, u32[]{:S(2)}) async-start(bf16[64,8,768]{2,1,0:T(8,128)(2,1)} %bitcast.53), calls=%async_computation.3 | async-start | bytes 1572864 | tf_op jit(solution)/shard_map/all_to_all | solution.py:408
  181.7 18.3 %copy-start = (bf16[512,512]{1,0:T(8,128)(2,1)S(1)}, bf16[512,512]{1,0:T(8,128)(2,1)}, u32[]{:S(2)}) copy-start(bf16[512,512]{1,0:T(8,128)(2,1)} %constant.58.clone.table) | copy-start | bytes 1572868
  181.7 18.3 %copy-start.6 = (bf16[8,12288]{1,0:T(8,128)(2,1)S(1)}, bf16[8,12288]{1,0:T(8,128)(2,1)}, u32[]{:S(2)}) copy-start(bf16[8,12288]{1,0:T(8,128)(2,1)} %copy-done.5) | copy-start | bytes 589828
  181.7 18.3 %copy-start.8 = (bf16[8,12288]{1,0:T(8,128)(2,1)S(1)}, bf16[8,12288]{1,0:T(8,128)(2,1)}, u32[]{:S(2)}) copy-start(bf16[8,12288]{1,0:T(8,128)(2,1)} %copy-done.7) | copy-start | bytes 589828
  181.7 21.4 %collective-permute-start.12 = (bf16[8,12288]{1,0:T(8,128)(2,1)}, bf16[8,12288]{1,0:T(8,128)(2,1)}, u32[]{:S(2)}, u32[]{:S(2)}) collective-permute-start(bf16[8,12288]{1,0:T(8,128)(2,1)} %get-tuple-element.34), channel_id=1, source_target_pairs={{0,64},{64,0},{128,192},{192,128},{1,65},{65,1},{129,193},{193,129... | collective-permute-start | bytes 589832 | tf_op jit(solution)/shard_map/ppermute | solution.py:380
  181.9 22.2 %collective-permute-start.13 = (bf16[8,12288]{1,0:T(8,128)(2,1)}, bf16[8,12288]{1,0:T(8,128)(2,1)}, u32[]{:S(2)}, u32[]{:S(2)}) collective-permute-start(bf16[8,12288]{1,0:T(8,128)(2,1)} %get-tuple-element.35), channel_id=1, source_target_pairs={{0,128},{64,192},{128,0},{192,64},{1,129},{65,193},{129,1},{193,65... | collective-permute-start | bytes 589832 | tf_op jit(solution)/shard_map/ppermute | solution.py:380
  183.6 20.5 %collective-permute-start.14 = (bf16[8,12288]{1,0:T(8,128)(2,1)}, bf16[8,12288]{1,0:T(8,128)(2,1)}, u32[]{:S(2)}, u32[]{:S(2)}) collective-permute-start(bf16[8,12288]{1,0:T(8,128)(2,1)} %get-tuple-element.36), channel_id=1, source_target_pairs={{0,192},{64,128},{128,64},{192,0},{1,193},{65,129},{129,65},{193,1... | collective-permute-start | bytes 589832 | tf_op jit(solution)/shard_map/ppermute | solution.py:380
  188.2 17.2 %collective-permute-start.9 = (bf16[8,12288]{1,0:T(8,128)(2,1)}, bf16[8,12288]{1,0:T(8,128)(2,1)S(1)}, u32[]{:S(2)}, u32[]{:S(2)}) collective-permute-start(bf16[8,12288]{1,0:T(8,128)(2,1)} %get-tuple-element.30), channel_id=1, source_target_pairs={{0,64},{64,0},{128,192},{192,128},{1,65},{65,1},{129,193},{193,129... | collective-permute-start | bytes 589832 | tf_op jit(solution)/shard_map/ppermute | solution.py:380
  188.6 17.4 %collective-permute-start.10 = (bf16[8,12288]{1,0:T(8,128)(2,1)}, bf16[8,12288]{1,0:T(8,128)(2,1)S(1)}, u32[]{:S(2)}, u32[]{:S(2)}) collective-permute-start(bf16[8,12288]{1,0:T(8,128)(2,1)} %get-tuple-element.31), channel_id=1, source_target_pairs={{0,128},{64,192},{128,0},{192,64},{1,129},{65,193},{129,1},{193,65... | collective-permute-start | bytes 589832 | tf_op jit(solution)/shard_map/ppermute | solution.py:380
  203.1 6.8 %collective-permute-start.11 = (bf16[8,12288]{1,0:T(8,128)(2,1)}, bf16[8,12288]{1,0:T(8,128)(2,1)S(1)}, u32[]{:S(2)}, u32[]{:S(2)}) collective-permute-start(bf16[8,12288]{1,0:T(8,128)(2,1)} %get-tuple-element.32), channel_id=1, source_target_pairs={{0,192},{64,128},{128,64},{192,0},{1,193},{65,129},{129,65},{193,1... | collective-permute-start | bytes 589832 | tf_op jit(solution)/shard_map/ppermute | solution.py:380
  204.1 10.3 %collective-permute-start.6 = (bf16[8,12288]{1,0:T(8,128)(2,1)S(1)}, bf16[8,12288]{1,0:T(8,128)(2,1)S(1)}, u32[]{:S(2)}, u32[]{:S(2)}) collective-permute-start(bf16[8,12288]{1,0:T(8,128)(2,1)S(1)} %get-tuple-element.25), channel_id=1, source_target_pairs={{0,64},{64,0},{128,192},{192,128},{1,65},{65,1},{129,193},{193,129... | collective-permute-start | bytes 589832 | tf_op jit(solution)/shard_map/ppermute | solution.py:380
  204.1 11.4 %collective-permute-start.7 = (bf16[8,12288]{1,0:T(8,128)(2,1)S(1)}, bf16[8,12288]{1,0:T(8,128)(2,1)S(1)}, u32[]{:S(2)}, u32[]{:S(2)}) collective-permute-start(bf16[8,12288]{1,0:T(8,128)(2,1)S(1)} %get-tuple-element.26), channel_id=1, source_target_pairs={{0,128},{64,192},{128,0},{192,64},{1,129},{65,193},{129,1},{193,65... | collective-permute-start | bytes 589832 | tf_op jit(solution)/shard_map/ppermute | solution.py:380
  205.5 12.9 %collective-permute-start.8 = (bf16[8,12288]{1,0:T(8,128)(2,1)S(1)}, bf16[8,12288]{1,0:T(8,128)(2,1)S(1)}, u32[]{:S(2)}, u32[]{:S(2)}) collective-permute-start(bf16[8,12288]{1,0:T(8,128)(2,1)S(1)} %get-tuple-element.27), channel_id=1, source_target_pairs={{0,192},{64,128},{128,64},{192,0},{1,193},{65,129},{129,65},{193,1... | collective-permute-start | bytes 589832 | tf_op jit(solution)/shard_map/ppermute | solution.py:380
  (8 other events, 27.0 us)

commit v5 on v4

--- a/solution.py
+++ b/solution.py
@@ -52,25 +52,28 @@
     return (table * np.float32(1.0 / math.sqrt(length))).astype(jnp.bfloat16)
 
 
-def first_layer(weight, special):
+def first_layer(weight, special, lanes):
     u, v = weight[0], weight[1]
     z = jnp.zeros_like(u)
     rows = lambda *blocks: jnp.concatenate([jnp.concatenate(b, axis=1) for b in blocks], axis=0)
     pair = rows((u, v, u, v), (v, -u, -v, u), (-v, u, -v, u), (u, v, -u, -v))
     single = rows((u, v, z, z), (z, z, u, v), (-v, u, z, z), (z, z, -v, u))
-    return jnp.stack([jnp.where(special, single, pair), pair])
+    layers = jnp.stack([jnp.where(special, single, pair), pair])
+    width = u.shape[0]
+    layers = layers.reshape(2, 4 * width, 2, 2 * width)
+    spare = 2 * lanes - 2 * width
+    return jnp.pad(layers, ((0, 0), (0, 0), (0, 0), (0, spare))).reshape(2, 4 * width, 4 * lanes)
 
 
 def second_layer(weight, bias, lanes):
     u, v = weight[0], weight[1]
     width = u.shape[0]
-    z = jnp.zeros((width, lanes), u.dtype)
     wide = lambda m: jnp.pad(m, ((0, 0), (0, lanes - width)))
     u, v, m = wide(u), wide(v), wide(-v)
-    rows = [(u, v, z, z), (m, u, z, z), (z, z, u, v), (z, z, m, u)]
-    matrix = jnp.concatenate([jnp.concatenate(r, axis=1) for r in rows], axis=0)
+    rows = [jnp.concatenate(r, axis=1) for r in ((u, v), (m, u))]
+    matrix = jnp.pad(jnp.concatenate(rows, axis=0), ((0, 2 * (lanes - width)), (0, 0)))
     padded = jnp.pad(bias, ((0, 0), (0, lanes - width))).reshape(-1)
-    return matrix, jnp.concatenate([padded, padded])[None]
+    return matrix, padded[None]
 
 
 def soft_threshold(v):
@@ -109,7 +112,7 @@
     kept = count // 2
     width = w1.shape[1] // 4
     slots = y.shape[1] // (2 * width)
-    lanes = w2.shape[1] // 4
+    lanes = w2.shape[1] // 2
     folded = [fold(x, blocks) for x in xs]
     for p in range(2):
         total = None
@@ -127,9 +130,13 @@
             z[pl.ds(base + kept, kept), cols], layer[2 * width :], preferred_element_type=jnp.float32
         )
         hidden = jnp.maximum(hidden + b1[...], 0.0).astype(jnp.bfloat16)
-        v = jnp.dot(hidden, w2[...], preferred_element_type=jnp.float32) + b2[...]
-        v = soft_threshold(v)
-        re, im, re2, im2 = [v[:, n * lanes : (n + 1) * lanes] for n in range(4)]
+        parts = []
+        for m in range(2):
+            v = hidden[:, 2 * m * lanes : 2 * (m + 1) * lanes]
+            v = jnp.dot(v, w2[...], preferred_element_type=jnp.float32) + b2[...]
+            v = soft_threshold(v)
+            parts += [v[:, :lanes], v[:, lanes:]]
+        re, im, re2, im2 = parts
         top = (re + re2, im2 - im)
         bottom = (im + im2, re - re2)
         if s == 0:
@@ -396,8 +403,9 @@
     lat = lat_table(lat_size)
     lat, lat_back = jnp.asarray(lat), jnp.asarray(np.ascontiguousarray(lat.T))
     special = (lax.axis_index("lat") == 0) & (lax.axis_index("lon") == 0)
-    w1 = first_layer(first_weight[0], special)
-    b1 = jnp.concatenate([first_bias[0].reshape(-1)] * 2)[None]
+    w1 = first_layer(first_weight[0], special, 128)
+    b1 = jnp.pad(first_bias[0].reshape(-1), (0, 256 - 2 * width))
+    b1 = jnp.concatenate([b1, b1])[None]
     w2, b2 = second_layer(second_weight[0], second_bias[0], 128)
     flag = special.astype(jnp.int32).reshape(1)
     me = lax.axis_index("lat")

time: 222 us -> 220 us (level)
    unnamed x42 -> x44, local copies, waits for them, and re-layouts: 5.94 us -> 3.1 us
  transfers between devices with their start and end apart: 19 -> 19, of which waited for: 10 -> 10; matrix products, arithmetic and copies ran while one was open for 2% -> 3% of each run, Pallas kernels for 10% -> 10%
where the time goes in v5:
time: 220 us; the launch traced here: 217 us
  waiting for transfers between devices  124 us (56%)
  starting transfers between devices  45.5 us (21%)
  Pallas kernels  36.7 us (17%)
  local copies, waits for them, and re-layouts  8.99 us (4%)
    all_to_all x4, waiting for transfers between devices, layer(): lax.all_to_all(x, group, split_axis=0, concat_axis=0, tiled=True)  81 us
    ppermute x15, waiting for transfers between devices, swap(): lax.ppermute(pieces[m], 'lat', [(i, i ^ m) for i in range(count)])  43.3 us
    all_to_all x4, starting transfers between devices, layer(): lax.all_to_all(x, group, split_axis=0, concat_axis=0, tiled=True)  34.5 us
    pallas_call x5, Pallas kernels, lat_call(): pl.pallas_call(kernel, grid=(rows // 8,), out_shape=out_shape, in_specs=[...  19.2 us
    ppermute x15, starting transfers between devices, swap(): lax.ppermute(pieces[m], 'lat', [(i, i ^ m) for i in range(count)])  10.9 us
    pallas_call x1, Pallas kernels, spectral(): pl.pallas_call(functools.partial(spectral_kernel, chunks=len(xs), blocks=...  10.3 us
  transfers between devices with their start and end apart: 19, of which 10 were waited for; matrix products, arithmetic and copies ran while one was open for 3% of the time, Pallas kernels for 10%

profile of v5, /device:TPU:38, one launch (start us, length us, event | category | flops | bytes accessed | tf_op | source)
XLA Modules:
  0.0 217.2 jit_solution(17263619144012211886)
XLA Ops:
  0.0 1.6 dynamic-slice_bitcast_fusion
  1.6 1.1 collective-permute-start.2
  3.6 5.2 %collective-permute-done.2.refs_3_ = bf16[8,12288]{1,0:T(8,128)(2,1)S(1)} collective-permute-done((bf16[8,12288]{1,0:T(8,128)(2,1)S(1)}, bf16[8,12288]{1,0:T(8,128)(2,1)S(1)}, u32[]{:S(2)}, u32[]{:S(2)}) %collective-permute-start.2) | collective-permute-done | bytes 196640 | tf_op jit(solution)/shard_map/ppermute | solution.py:387
  8.8 4.3 %collective-permute-done.1.refs_2_ = bf16[8,12288]{1,0:T(8,128)(2,1)S(1)} collective-permute-done((bf16[8,12288]{1,0:T(8,128)(2,1)S(1)}, bf16[8,12288]{1,0:T(8,128)(2,1)S(1)}, u32[]{:S(2)}, u32[]{:S(2)}) %collective-permute-start.1) | collective-permute-done | bytes 196640 | tf_op jit(solution)/shard_map/ppermute | solution.py:387
  13.2 2.9 %shard_map.109 = bf16[64,8,768]{2,1,0:T(8,128)(2,1)} custom-call(s32[1]{0:T(128)} %bitcast.place, bf16[8,12288]{1,0:T(8,128)(2,1)S(1)} %get-tuple-element.44.refs_0_, bf16[8,12288]{1,0:T(8,128)(2,1)S(1)} %collective-permute-done.refs_1_, bf16[8,12288]{1,0:T(8,128)(2,1)S(1)} %collective-permute-done.1.refs_2_, ...), custom_call_target="tpu_custom_call" | custom-call | flops 536870912 | bytes 1572864 | tf_op jit(solution)/shard_map/pallas_call | solution.py:268
  16.1 11.8 %all-to-all-start = ((bf16[64,8,768]{2,1,0:T(8,128)(2,1)}), bf16[64,8,768]{2,1,0:T(8,128)(2,1)S(1)}, u32[]{:S(2)}, u32[]{:S(2)}) async-start(bf16[64,8,768]{2,1,0:T(8,128)(2,1)} %shard_map.109), calls=%async_computation | async-start | bytes 1572864 | tf_op jit(solution)/shard_map/all_to_all | solution.py:416
  27.8 1.7 pad_dynamic-slice_fusion
  29.5 1.5 collective-permute-start.5
  31.8 14.2 %collective-permute-done.5.refs_3_ = bf16[16,12288]{1,0:T(8,128)(2,1)S(1)} collective-permute-done((bf16[16,12288]{1,0:T(8,128)(2,1)S(1)}, bf16[16,12288]{1,0:T(8,128)(2,1)S(1)}, u32[]{:S(2)}, u32[]{:S(2)}) %collective-permute-start.5) | collective-permute-done | bytes 393248 | tf_op jit(solution)/shard_map/ppermute | solution.py:387
  46.0 10.1 %collective-permute-done.4.refs_2_ = bf16[16,12288]{1,0:T(8,128)(2,1)S(1)} collective-permute-done((bf16[16,12288]{1,0:T(8,128)(2,1)S(1)}, bf16[16,12288]{1,0:T(8,128)(2,1)S(1)}, u32[]{:S(2)}, u32[]{:S(2)}) %collective-permute-start.4) | collective-permute-done | bytes 393248 | tf_op jit(solution)/shard_map/ppermute | solution.py:387
  56.0 4.9 %shard_map.110 = bf16[64,16,768]{2,1,0:T(8,128)(2,1)} custom-call(s32[1]{0:T(128)} %bitcast.place, bf16[16,12288]{1,0:T(8,128)(2,1)S(1)} %get-tuple-element.40.refs_0_, bf16[16,12288]{1,0:T(8,128)(2,1)S(1)} %collective-permute-done.3.refs_1_, bf16[16,12288]{1,0:T(8,128)(2,1)S(1)} %collective-permute-done.4.refs_2_, ...), custom_call_target="tpu_custom_call" | custom-call | flops 1073741824 | bytes 3145728 | tf_op jit(solution)/shard_map/pallas_call | solution.py:268
  61.7 9.7 %all-to-all-start.1 = ((bf16[64,16,768]{2,1,0:T(8,128)(2,1)}), bf16[64,16,768]{2,1,0:T(8,128)(2,1)S(1)}, u32[]{:S(2)}, u32[]{:S(2)}) async-start(bf16[64,16,768]{2,1,0:T(8,128)(2,1)} %shard_map.110), calls=%async_computation.1 | async-start | bytes 3145728 | tf_op jit(solution)/shard_map/all_to_all | solution.py:416
  74.0 1.2 copy.16.refs_5_
  75.8 35.3 %all-to-all-done.1 = bf16[64,16,768]{2,1,0:T(8,128)(2,1)S(1)} async-done(((bf16[64,16,768]{2,1,0:T(8,128)(2,1)}), bf16[64,16,768]{2,1,0:T(8,128)(2,1)S(1)}, u32[]{:S(2)}, u32[]{:S(2)}) %all-to-all-start.1) | async-done | bytes 1572896 | tf_op jit(solution)/shard_map/all_to_all | solution.py:416
  111.0 1.2 copy-done.14
  112.2 10.3 %spectral.1 = (bf16[1024,768]{1,0:T(8,128)(2,1)}, bf16[1472,768]{1,0:T(8,128)(2,1)}) custom-call(s32[1]{0:T(128)} %bitcast.1.flag, bf16[512,768]{1,0:T(8,128)(2,1)} %bitcast.45, bf16[1024,768]{1,0:T(8,128)(2,1)} %bitcast.42, bf16[2,736,256]{2,1,0:T(8,128)(2,1)} %constant.52.clone.refs_2_, bf16[2,736,512]{2,1,0:T(8,128)(2,1)} %constant.53.clone.refs_3_, ...), custom_call_target="tpu_custom_call" | custom-call | flops 8999999488 | bytes 14000000 | tf_op jit(solution)/shard_map/spectral/pallas_call | solution.py:175
  122.5 6.6 %all-to-all-start.2 = ((bf16[64,16,768]{2,1,0:T(8,128)(2,1)}), bf16[64,16,768]{2,1,0:T(8,128)(2,1)}, u32[]{:S(2)}, u32[]{:S(2)}) async-start(bf16[64,16,768]{2,1,0:T(8,128)(2,1)} %bitcast.43), calls=%async_computation.2 | async-start | bytes 3145728 | tf_op jit(solution)/shard_map/all_to_all | solution.py:416
  129.1 3.6 %unwind.1 = bf16[512,768]{1,0:T(8,128)(2,1)} custom-call(bf16[2,256,736]{2,1,0:T(8,128)(2,1)} %constant.54.clone.inv, bf16[1472,768]{1,0:T(8,128)(2,1)} %get-tuple-element.21.y), custom_call_target="tpu_custom_call" | custom-call | flops 1000000000 | bytes 4000000 | tf_op jit(solution)/shard_map/unwind/pallas_call | solution.py:159
  132.7 36.0 %all-to-all-done.2.back = bf16[64,16,768]{2,1,0:T(8,128)(2,1)} async-done(((bf16[64,16,768]{2,1,0:T(8,128)(2,1)}), bf16[64,16,768]{2,1,0:T(8,128)(2,1)}, u32[]{:S(2)}, u32[]{:S(2)}) %all-to-all-start.2) | async-done | bytes 1572896 | tf_op jit(solution)/shard_map/all_to_all | solution.py:416
  168.7 6.4 %all-to-all-start.3 = ((bf16[64,8,768]{2,1,0:T(8,128)(2,1)}), bf16[64,8,768]{2,1,0:T(8,128)(2,1)S(1)}, u32[]{:S(2)}, u32[]{:S(2)}) async-start(bf16[64,8,768]{2,1,0:T(8,128)(2,1)} %bitcast.41), calls=%async_computation.3 | async-start | bytes 1572864 | tf_op jit(solution)/shard_map/all_to_all | solution.py:416
  175.1 4.6 %shard_map.113 = (bf16[8,12288]{1,0:T(8,128)(2,1)}, bf16[8,12288]{1,0:T(8,128)(2,1)}, bf16[8,12288]{1,0:T(8,128)(2,1)}, bf16[8,12288]{1,0:T(8,128)(2,1)}) custom-call(s32[1]{0:T(128)} %bitcast.place, bf16[64,16,768]{2,1,0:T(8,128)(2,1)} %all-to-all-done.2.back, bf16[512,512]{1,0:T(8,128)(2,1)} %constant.57.clone.table, bf16[16,12288]{1,0:T(8,128)(2,1)} %copy-done.1, ...), custom_call_target="tpu_custom_call" | custom-call | flops 536870912 | bytes 1572864 | tf_op jit(solution)/shard_map/pallas_call | solution.py:268
  179.8 1.7 collective-permute-start.13
  181.7 4.6 %shard_map.112 = (bf16[8,12288]{1,0:T(8,128)(2,1)}, bf16[8,12288]{1,0:T(8,128)(2,1)}, bf16[8,12288]{1,0:T(8,128)(2,1)}, bf16[8,12288]{1,0:T(8,128)(2,1)}) custom-call(s32[1]{0:T(128)} %bitcast.place, bf16[64,16,768]{2,1,0:T(8,128)(2,1)} %all-to-all-done.2.back, bf16[512,512]{1,0:T(8,128)(2,1)} %constant.57.clone.table, bf16[16,12288]{1,0:T(8,128)(2,1)} %copy-done.1, ...), custom_call_target="tpu_custom_call" | custom-call | flops 536870912 | bytes 1572864 | tf_op jit(solution)/shard_map/pallas_call | solution.py:268
  186.6 1.6 collective-permute-start.10
  188.2 9.8 %all-to-all-done.3.back = bf16[64,8,768]{2,1,0:T(8,128)(2,1)S(1)} async-done(((bf16[64,8,768]{2,1,0:T(8,128)(2,1)}), bf16[64,8,768]{2,1,0:T(8,128)(2,1)S(1)}, u32[]{:S(2)}, u32[]{:S(2)}) %all-to-all-start.3) | async-done | bytes 786464 | tf_op jit(solution)/shard_map/all_to_all | solution.py:416
  198.9 2.2 %shard_map.111 = (bf16[8,12288]{1,0:T(8,128)(2,1)S(1)}, bf16[8,12288]{1,0:T(8,128)(2,1)S(1)}, bf16[8,12288]{1,0:T(8,128)(2,1)S(1)}, bf16[8,12288]{1,0:T(8,128)(2,1)S(1)}) custom-call(s32[1]{0:T(128)} %bitcast.place, bf16[64,8,768]{2,1,0:T(8,128)(2,1)S(1)} %all-to-all-done.3.back, bf16[512,512]{1,0:T(8,128)(2,1)S(1)} %copy-done, ...), custom_call_target="tpu_custom_call" | custom-call | flops 536870912 | bytes 1572864 | tf_op jit(solution)/shard_map/pallas_call | solution.py:268
  201.1 1.0 collective-permute-start.11
  202.2 1.3 collective-permute-start.7
  204.0 3.7 %collective-permute-done.11.refs_3_ = bf16[8,12288]{1,0:T(8,128)(2,1)S(1)} collective-permute-done((bf16[8,12288]{1,0:T(8,128)(2,1)S(1)}, bf16[8,12288]{1,0:T(8,128)(2,1)S(1)}, u32[]{:S(2)}, u32[]{:S(2)}) %collective-permute-start.11) | collective-permute-done | bytes 196640 | tf_op jit(solution)/shard_map/ppermute | solution.py:387
  207.7 2.7 %assemble.1.refs_4_ = bf16[90,12288]{1,0:T(8,128)(2,1)} custom-call(s32[1]{0:T(128)} %bitcast.place, bf16[8,12288]{1,0:T(8,128)(2,1)S(1)} %copy-done.13, bf16[8,12288]{1,0:T(8,128)(2,1)S(1)} %collective-permute-done.9.refs_1_, bf16[8,12288]{1,0:T(8,128)(2,1)S(1)} %collective-permute-done.10.refs_2_, bf16[8,12288]{1,0:T(8,128)(2,1)S(1)} %collective-permute-done.11.refs_3_, ...), custom_call_target="tpu_custom_call" | custom-call | bytes 5000000 | tf_op jit(solution)/shard_map/assemble/pallas_call | solution.py:363
  210.4 2.9 %collective-permute-done.7.refs_2_ = bf16[8,12288]{1,0:T(8,128)(2,1)S(1)} collective-permute-done((bf16[8,12288]{1,0:T(8,128)(2,1)S(1)}, bf16[8,12288]{1,0:T(8,128)(2,1)S(1)}, u32[]{:S(2)}, u32[]{:S(2)}) %collective-permute-start.7) | collective-permute-done | bytes 196640 | tf_op jit(solution)/shard_map/ppermute | solution.py:387
  213.3 2.8 %collective-permute-done.8.refs_3_ = bf16[8,12288]{1,0:T(8,128)(2,1)S(1)} collective-permute-done((bf16[8,12288]{1,0:T(8,128)(2,1)S(1)}, bf16[8,12288]{1,0:T(8,128)(2,1)S(1)}, u32[]{:S(2)}, u32[]{:S(2)}) %collective-permute-start.8) | collective-permute-done | bytes 196640 | tf_op jit(solution)/shard_map/ppermute | solution.py:387
  (79 shorter events, 8.3 us)
Async XLA Ops:
  0.0 13.2 %copy-start.11 = (bf16[512,512]{1,0:T(8,128)(2,1)S(1)}, bf16[512,512]{1,0:T(8,128)(2,1)}, u32[]{:S(2)}) copy-start(bf16[512,512]{1,0:T(8,128)(2,1)} %constant.56.clone.refs_4_) | copy-start | bytes 1572868
  1.6 7.2 %collective-permute-start.2 = (bf16[8,12288]{1,0:T(8,128)(2,1)S(1)}, bf16[8,12288]{1,0:T(8,128)(2,1)S(1)}, u32[]{:S(2)}, u32[]{:S(2)}) collective-permute-start(bf16[8,12288]{1,0:T(8,128)(2,1)S(1)} %get-tuple-element.41), channel_id=1, source_target_pairs={{0,192},{64,128},{128,64},{192,0},{1,193},{65,129},{129,65},{193,1... | collective-permute-start | bytes 589832 | tf_op jit(solution)/shard_map/ppermute | solution.py:387
  2.8 10.4 %collective-permute-start.1 = (bf16[8,12288]{1,0:T(8,128)(2,1)S(1)}, bf16[8,12288]{1,0:T(8,128)(2,1)S(1)}, u32[]{:S(2)}, u32[]{:S(2)}) collective-permute-start(bf16[8,12288]{1,0:T(8,128)(2,1)S(1)} %get-tuple-element.42), channel_id=1, source_target_pairs={{0,128},{64,192},{128,0},{192,64},{1,129},{65,193},{129,1},{193,65... | collective-permute-start | bytes 589832 | tf_op jit(solution)/shard_map/ppermute | solution.py:387
  3.4 9.7 %collective-permute-start = (bf16[8,12288]{1,0:T(8,128)(2,1)S(1)}, bf16[8,12288]{1,0:T(8,128)(2,1)S(1)}, u32[]{:S(2)}, u32[]{:S(2)}) collective-permute-start(bf16[8,12288]{1,0:T(8,128)(2,1)S(1)} %get-tuple-element.43), channel_id=1, source_target_pairs={{0,64},{64,0},{128,192},{192,128},{1,65},{65,1},{129,193},{193,129... | collective-permute-start | bytes 589832 | tf_op jit(solution)/shard_map/ppermute | solution.py:387
  16.1 45.7 %all-to-all-start = ((bf16[64,8,768]{2,1,0:T(8,128)(2,1)}), bf16[64,8,768]{2,1,0:T(8,128)(2,1)S(1)}, u32[]{:S(2)}, u32[]{:S(2)}) async-start(bf16[64,8,768]{2,1,0:T(8,128)(2,1)} %shard_map.109), calls=%async_computation | async-start | bytes 1572864 | tf_op jit(solution)/shard_map/all_to_all | solution.py:416
  29.5 31.4 %copy-start.1 = (bf16[16,12288]{1,0:T(8,128)(2,1)}, bf16[16,12288]{1,0:T(8,128)(2,1)S(1)}, u32[]{:S(2)}) copy-start(bf16[16,12288]{1,0:T(8,128)(2,1)S(1)} %get-tuple-element.40.refs_0_) | copy-start | bytes 1179652
  29.5 16.4 %collective-permute-start.5 = (bf16[16,12288]{1,0:T(8,128)(2,1)S(1)}, bf16[16,12288]{1,0:T(8,128)(2,1)S(1)}, u32[]{:S(2)}, u32[]{:S(2)}) collective-permute-start(bf16[16,12288]{1,0:T(8,128)(2,1)S(1)} %get-tuple-element.37), channel_id=1, source_target_pairs={{0,192},{64,128},{128,64},{192,0},{1,193},{65,129},{129,65},{193,1... | collective-permute-start | bytes 1179656 | tf_op jit(solution)/shard_map/ppermute | solution.py:387
  31.0 14.9 %collective-permute-start.3 = (bf16[16,12288]{1,0:T(8,128)(2,1)S(1)}, bf16[16,12288]{1,0:T(8,128)(2,1)S(1)}, u32[]{:S(2)}, u32[]{:S(2)}) collective-permute-start(bf16[16,12288]{1,0:T(8,128)(2,1)S(1)} %get-tuple-element.38), channel_id=1, source_target_pairs={{0,64},{64,0},{128,192},{192,128},{1,65},{65,1},{129,193},{193,129... | collective-permute-start | bytes 1179656 | tf_op jit(solution)/shard_map/ppermute | solution.py:387
  31.3 24.7 %collective-permute-start.4 = (bf16[16,12288]{1,0:T(8,128)(2,1)S(1)}, bf16[16,12288]{1,0:T(8,128)(2,1)S(1)}, u32[]{:S(2)}, u32[]{:S(2)}) collective-permute-start(bf16[16,12288]{1,0:T(8,128)(2,1)S(1)} %get-tuple-element.39), channel_id=1, source_target_pairs={{0,128},{64,192},{128,0},{192,64},{1,129},{65,193},{129,1},{193,65... | collective-permute-start | bytes 1179656 | tf_op jit(solution)/shard_map/ppermute | solution.py:387
  46.0 15.0 %copy-start.2 = (bf16[16,12288]{1,0:T(8,128)(2,1)}, bf16[16,12288]{1,0:T(8,128)(2,1)S(1)}, u32[]{:S(2)}) copy-start(bf16[16,12288]{1,0:T(8,128)(2,1)S(1)} %collective-permute-done.5.refs_3_) | copy-start | bytes 1179652
  46.0 15.0 %copy-start.3 = (bf16[16,12288]{1,0:T(8,128)(2,1)}, bf16[16,12288]{1,0:T(8,128)(2,1)S(1)}, u32[]{:S(2)}) copy-start(bf16[16,12288]{1,0:T(8,128)(2,1)S(1)} %collective-permute-done.3.refs_1_) | copy-start | bytes 1179652
  61.7 9.8 %copy-start.18 = (f32[1,2,96]{2,1,0:T(2,128)S(1)}, f32[1,2,96]{2,1,0:T(2,128)}, u32[]{:S(2)}) copy-start(f32[1,2,96]{2,1,0:T(2,128)} %param.13) | copy-start | bytes 2308
  61.7 9.9 %copy-start.19 = (f32[1,2,96]{2,1,0:T(2,128)S(1)}, f32[1,2,96]{2,1,0:T(2,128)}, u32[]{:S(2)}) copy-start(f32[1,2,96]{2,1,0:T(2,128)} %param.15) | copy-start | bytes 2308
  61.7 10.5 %copy-start.17 = (bf16[1,2,96,96]{3,2,1,0:T(8,128)(2,1)S(1)}, bf16[1,2,96,96]{3,2,1,0:T(8,128)(2,1)}, u32[]{:S(2)}) copy-start(bf16[1,2,96,96]{3,2,1,0:T(8,128)(2,1)} %param.12) | copy-start | bytes 110596
  61.7 10.7 %copy-start.16 = (bf16[1,2,96,96]{3,2,1,0:T(8,128)(2,1)S(1)}, bf16[1,2,96,96]{3,2,1,0:T(8,128)(2,1)}, u32[]{:S(2)}) copy-start(bf16[1,2,96,96]{3,2,1,0:T(8,128)(2,1)} %param.14) | copy-start | bytes 110596
  61.7 9.7 %copy-start.15 = (bf16[64,8,768]{2,1,0:T(8,128)(2,1)}, bf16[64,8,768]{2,1,0:T(8,128)(2,1)S(1)}, u32[]{:S(2)}) copy-start(bf16[64,8,768]{2,1,0:T(8,128)(2,1)S(1)} %all-to-all-done) | copy-start | bytes 2359300
  61.7 49.3 %all-to-all-start.1 = ((bf16[64,16,768]{2,1,0:T(8,128)(2,1)}), bf16[64,16,768]{2,1,0:T(8,128)(2,1)S(1)}, u32[]{:S(2)}, u32[]{:S(2)}) async-start(bf16[64,16,768]{2,1,0:T(8,128)(2,1)} %shard_map.110), calls=%async_computation.1 | async-start | bytes 3145728 | tf_op jit(solution)/shard_map/all_to_all | solution.py:416
  122.5 46.1 %all-to-all-start.2 = ((bf16[64,16,768]{2,1,0:T(8,128)(2,1)}), bf16[64,16,768]{2,1,0:T(8,128)(2,1)}, u32[]{:S(2)}, u32[]{:S(2)}) async-start(bf16[64,16,768]{2,1,0:T(8,128)(2,1)} %bitcast.43), calls=%async_computation.2 | async-start | bytes 3145728 | tf_op jit(solution)/shard_map/all_to_all | solution.py:416
  168.7 29.3 %all-to-all-start.3 = ((bf16[64,8,768]{2,1,0:T(8,128)(2,1)}), bf16[64,8,768]{2,1,0:T(8,128)(2,1)S(1)}, u32[]{:S(2)}, u32[]{:S(2)}) async-start(bf16[64,8,768]{2,1,0:T(8,128)(2,1)} %bitcast.41), calls=%async_computation.3 | async-start | bytes 1572864 | tf_op jit(solution)/shard_map/all_to_all | solution.py:416
  179.7 21.4 %collective-permute-start.12 = (bf16[8,12288]{1,0:T(8,128)(2,1)}, bf16[8,12288]{1,0:T(8,128)(2,1)}, u32[]{:S(2)}, u32[]{:S(2)}) collective-permute-start(bf16[8,12288]{1,0:T(8,128)(2,1)} %get-tuple-element.34), channel_id=1, source_target_pairs={{0,64},{64,0},{128,192},{192,128},{1,65},{65,1},{129,193},{193,129... | collective-permute-start | bytes 589832 | tf_op jit(solution)/shard_map/ppermute | solution.py:387
  179.8 22.3 %collective-permute-start.13 = (bf16[8,12288]{1,0:T(8,128)(2,1)}, bf16[8,12288]{1,0:T(8,128)(2,1)}, u32[]{:S(2)}, u32[]{:S(2)}) collective-permute-start(bf16[8,12288]{1,0:T(8,128)(2,1)} %get-tuple-element.35), channel_id=1, source_target_pairs={{0,128},{64,192},{128,0},{192,64},{1,129},{65,193},{129,1},{193,65... | collective-permute-start | bytes 589832 | tf_op jit(solution)/shard_map/ppermute | solution.py:387
  181.5 16.5 %copy-start = (bf16[512,512]{1,0:T(8,128)(2,1)S(1)}, bf16[512,512]{1,0:T(8,128)(2,1)}, u32[]{:S(2)}) copy-start(bf16[512,512]{1,0:T(8,128)(2,1)} %constant.57.clone.table) | copy-start | bytes 1572868
  181.5 16.5 %copy-start.6 = (bf16[8,12288]{1,0:T(8,128)(2,1)S(1)}, bf16[8,12288]{1,0:T(8,128)(2,1)}, u32[]{:S(2)}) copy-start(bf16[8,12288]{1,0:T(8,128)(2,1)} %copy-done.5) | copy-start | bytes 589828
  181.5 16.5 %copy-start.8 = (bf16[8,12288]{1,0:T(8,128)(2,1)S(1)}, bf16[8,12288]{1,0:T(8,128)(2,1)}, u32[]{:S(2)}) copy-start(bf16[8,12288]{1,0:T(8,128)(2,1)} %copy-done.7) | copy-start | bytes 589828
  181.5 20.7 %collective-permute-start.14 = (bf16[8,12288]{1,0:T(8,128)(2,1)}, bf16[8,12288]{1,0:T(8,128)(2,1)}, u32[]{:S(2)}, u32[]{:S(2)}) collective-permute-start(bf16[8,12288]{1,0:T(8,128)(2,1)} %get-tuple-element.36), channel_id=1, source_target_pairs={{0,192},{64,128},{128,64},{192,0},{1,193},{65,129},{129,65},{193,1... | collective-permute-start | bytes 589832 | tf_op jit(solution)/shard_map/ppermute | solution.py:387
  186.3 17.1 %collective-permute-start.9 = (bf16[8,12288]{1,0:T(8,128)(2,1)}, bf16[8,12288]{1,0:T(8,128)(2,1)S(1)}, u32[]{:S(2)}, u32[]{:S(2)}) collective-permute-start(bf16[8,12288]{1,0:T(8,128)(2,1)} %get-tuple-element.30), channel_id=1, source_target_pairs={{0,64},{64,0},{128,192},{192,128},{1,65},{65,1},{129,193},{193,129... | collective-permute-start | bytes 589832 | tf_op jit(solution)/shard_map/ppermute | solution.py:387
  186.6 17.5 %collective-permute-start.10 = (bf16[8,12288]{1,0:T(8,128)(2,1)}, bf16[8,12288]{1,0:T(8,128)(2,1)S(1)}, u32[]{:S(2)}, u32[]{:S(2)}) collective-permute-start(bf16[8,12288]{1,0:T(8,128)(2,1)} %get-tuple-element.31), channel_id=1, source_target_pairs={{0,128},{64,192},{128,0},{192,64},{1,129},{65,193},{129,1},{193,65... | collective-permute-start | bytes 589832 | tf_op jit(solution)/shard_map/ppermute | solution.py:387
  198.9 8.8 %copy-start.13 = (bf16[8,12288]{1,0:T(8,128)(2,1)S(1)}, bf16[8,12288]{1,0:T(8,128)(2,1)}, u32[]{:S(2)}) copy-start(bf16[8,12288]{1,0:T(8,128)(2,1)} %get-tuple-element.29.refs_0_) | copy-start | bytes 589828
  201.1 6.6 %collective-permute-start.11 = (bf16[8,12288]{1,0:T(8,128)(2,1)S(1)}, bf16[8,12288]{1,0:T(8,128)(2,1)S(1)}, u32[]{:S(2)}, u32[]{:S(2)}) collective-permute-start(bf16[8,12288]{1,0:T(8,128)(2,1)S(1)} %copy-done.20), channel_id=1, source_target_pairs={{0,192},{64,128},{128,64},{192,0},{1,193},{65,129},{129,65},{193,1... | collective-permute-start | bytes 589832 | tf_op jit(solution)/shard_map/ppermute | solution.py:387
  202.1 8.3 %collective-permute-start.6 = (bf16[8,12288]{1,0:T(8,128)(2,1)S(1)}, bf16[8,12288]{1,0:T(8,128)(2,1)S(1)}, u32[]{:S(2)}, u32[]{:S(2)}) collective-permute-start(bf16[8,12288]{1,0:T(8,128)(2,1)S(1)} %get-tuple-element.25), channel_id=1, source_target_pairs={{0,64},{64,0},{128,192},{192,128},{1,65},{65,1},{129,193},{193,129... | collective-permute-start | bytes 589832 | tf_op jit(solution)/shard_map/ppermute | solution.py:387
  202.2 11.2 %collective-permute-start.7 = (bf16[8,12288]{1,0:T(8,128)(2,1)S(1)}, bf16[8,12288]{1,0:T(8,128)(2,1)S(1)}, u32[]{:S(2)}, u32[]{:S(2)}) collective-permute-start(bf16[8,12288]{1,0:T(8,128)(2,1)S(1)} %get-tuple-element.26), channel_id=1, source_target_pairs={{0,128},{64,192},{128,0},{192,64},{1,129},{65,193},{129,1},{193,65... | collective-permute-start | bytes 589832 | tf_op jit(solution)/shard_map/ppermute | solution.py:387
  203.5 12.7 %collective-permute-start.8 = (bf16[8,12288]{1,0:T(8,128)(2,1)S(1)}, bf16[8,12288]{1,0:T(8,128)(2,1)S(1)}, u32[]{:S(2)}, u32[]{:S(2)}) collective-permute-start(bf16[8,12288]{1,0:T(8,128)(2,1)S(1)} %get-tuple-element.27), channel_id=1, source_target_pairs={{0,192},{64,128},{128,64},{192,0},{1,193},{65,129},{129,65},{193,1... | collective-permute-start | bytes 589832 | tf_op jit(solution)/shard_map/ppermute | solution.py:387
  (8 other events, 27.0 us)
